TPU v7x, 128 devices: a whole 4x4x4 slice. The times are simulated.
128 devices in a mesh: vrow: 8 (over z, y_hi), img: 16 (over x, y_lo, core).
Axes of the slice: x: 4, y: 4 (y_hi: 2, y_lo: 2; y = y_hi * 2 + y_lo), z: 4, core: 2. Of those that a mesh axis runs over, the one named last changes fastest.
Arguments:
- features: bfloat16 [8, 16, 128, 1024], P('vrow', None, 'img'), may hold values from -6 to 6
- weight_h: bfloat16 [64, 64, 3, 3], replicated, may hold values from -0.25 to 0.25
- weight_v: bfloat16 [64, 64, 3, 3], replicated, may hold values from -0.25 to 0.25
- beta_h: float32 [5, 64], replicated, may hold values from 0.2 to 1
- beta_v: float32 [5, 64], replicated, may hold values from 0.2 to 1
- shear_set: int32 [5], replicated, may hold values from -2 to 2
- cotangent: bfloat16 [16, 128, 8192], P('vrow', 'img'), may hold values from -6 to 6
Outputs:
- output: bfloat16 [16, 128, 8192], P('vrow', 'img')
- grad_features: bfloat16 [8, 16, 128, 1024], P('vrow', None, 'img')
- grad_weight_h: float32 [64, 64, 3, 3], replicated
- grad_weight_v: float32 [64, 64, 3, 3], replicated
- grad_beta_h: float32 [5, 64], replicated
- grad_beta_v: float32 [5, 64], replicated
All inputs are finite; a program needn't handle non-finite values.
Results may differ from a plain program's by a relative error of at most 0.0057.
Values may be sent and summed in bfloat16 or wider, within the bound.
No kernel may reach another device: no remote copies, remote signals or barrier semaphores. Data moves between devices by JAX's collectives and lax.ppermute only.
A program may use at most 128 MiB of HBM per device.

v0:
```python
import jax
import jax.numpy as jnp
from jax import lax
from jax.sharding import PartitionSpec as P

SHIFT_MAX = 2


def conv_taps(source, kernel_row):
    return lax.conv_general_dilated(
        source,
        kernel_row,
        (1, 1),
        ((0, 0), (0, 0)),
        dimension_numbers=("NCHW", "OIHW", "NCHW"),
        preferred_element_type=jnp.float32,
    )


def conv_back(grads, kernel_row):
    return lax.conv_general_dilated(
        grads,
        kernel_row,
        (1, 1),
        ((0, 0), (0, 0)),
        dimension_numbers=("NCHW", "IOHW", "NCHW"),
        preferred_element_type=jnp.float32,
    )


def conv_weight(grads, source):
    result = lax.conv_general_dilated(
        source,
        grads,
        (1, 1),
        ((0, 0), (0, 0)),
        dimension_numbers=("CNHW", "IOHW", "NCHW"),
        preferred_element_type=jnp.float32,
    )
    return jnp.transpose(result, (1, 0, 2, 3))


def view_offsets(count):
    return jnp.arange(count, dtype=jnp.int32) - count // 2


def pad_views(field):
    return jnp.pad(field, ((0, 0), (0, 0), (1, 1), (0, 0)))


def window(padded, row_start, col_start, width):
    starts = (jnp.int32(0), jnp.int32(0), jnp.int32(row_start), jnp.asarray(col_start))
    sizes = (padded.shape[0], padded.shape[1], padded.shape[2] - 2, width + 2)
    return lax.dynamic_slice(padded, starts, sizes)


def masked_source(extended, amounts, start, total):
    columns = start + jnp.arange(extended.shape[3], dtype=jnp.int32)
    shifted = columns[None, :] - amounts[:, None]
    inside = (shifted >= 0) & (shifted < total)
    return (extended * inside[None, None].astype(extended.dtype), inside)


def forward_pass(extended, kernel, blend, shear_set, start, total, reach):
    width = extended.shape[3] - 2 * reach
    offsets = view_offsets(extended.shape[2])
    source_local = extended[:, :, :, reach : reach + width]
    branch = jnp.zeros(source_local.shape, jnp.float32)
    saved = []
    for shear_idx in range(shear_set.shape[0]):
        disparity = shear_set[shear_idx]
        amounts = disparity * offsets
        masked, inside = masked_source(extended, amounts, start, total)
        masked_pad = pad_views(masked)
        preact = jnp.zeros(source_local.shape, jnp.float32)
        for tap_row in range(3):
            piece = window(masked_pad, tap_row, reach - 1 + (tap_row - 1) * disparity, width)
            preact = preact + conv_taps(piece, kernel[:, :, tap_row : tap_row + 1, :])
        keep = inside[:, reach : reach + width].astype(jnp.float32)[None, None]
        branch = branch + blend[shear_idx][None, :, None, None] * (keep * jax.nn.silu(preact))
        saved.append((masked_pad, preact, keep, disparity))
    return ((source_local.astype(jnp.float32) + branch).astype(jnp.bfloat16), saved)


def backward_pass(kernel, blend, grads, saved, extend, reach):
    width = grads.shape[3]
    channels = kernel.shape[0]
    kernel_grad = jnp.zeros((channels, channels, 3, 3), jnp.float32)
    blend_rows = []
    dpre_list = []
    for shear_idx in range(len(saved)):
        masked_pad, preact, keep, disparity = saved[shear_idx]
        blend_rows.append(jnp.sum(grads * (keep * jax.nn.silu(preact)), axis=(0, 2, 3)))
        sigma = jax.nn.sigmoid(preact)
        slope = sigma * (1.0 + preact * (1.0 - sigma))
        dpre = (blend[shear_idx][None, :, None, None] * grads * slope * keep).astype(jnp.bfloat16)
        dpre_list.append(dpre)
        pieces = []
        for tap_row in range(3):
            piece = window(masked_pad, tap_row, reach - 1 + (tap_row - 1) * disparity, width)
            pieces.append(conv_weight(dpre, piece))
        kernel_grad = kernel_grad + jnp.concatenate(pieces, axis=2)
    stacked = extend(jnp.stack(dpre_list))
    total = grads
    for shear_idx in range(len(saved)):
        masked_pad, preact, keep, disparity = saved[shear_idx]
        dpre_pad = pad_views(stacked[shear_idx])
        inputs_grad = jnp.zeros(grads.shape, jnp.float32)
        for tap_row in range(3):
            piece = window(dpre_pad, 2 - tap_row, reach - 1 - (tap_row - 1) * disparity, width)
            inputs_grad = inputs_grad + conv_back(piece, kernel[:, :, tap_row : tap_row + 1, ::-1])
        total = total + keep * inputs_grad
    return (total.astype(jnp.bfloat16), kernel_grad, jnp.stack(blend_rows))


def per_device(features, weight_h, weight_v, beta_h, beta_v, shear_set, cotangent):
    reach = SHIFT_MAX + 1
    vrow_count = lax.axis_size("vrow")
    img_count = lax.axis_size("img")
    channels = weight_h.shape[0]
    u_local, y_all, x_local, merged = features.shape
    v_all = merged // channels
    v_local = v_all // vrow_count
    u_all = u_local * vrow_count
    x_all = x_local * img_count
    y_local = y_all // img_count

    def zero_rims(field):
        widths = [(0, 0)] * (field.ndim - 1) + [(reach, reach)]
        return jnp.pad(field, widths)

    lines = lax.all_to_all(features, "img", split_axis=1, concat_axis=2, tiled=True)
    layout = jnp.transpose(
        lines.reshape(u_local, y_local, x_all, v_all, channels), (0, 1, 4, 3, 2)
    ).reshape(u_local * y_local, channels, v_all, x_all)
    extended_h = zero_rims(layout)
    start_h = -reach
    hfeat, saved_h = forward_pass(extended_h, weight_h, beta_h, shear_set, start_h, x_all, reach)
    block = hfeat.reshape(u_local, y_local, channels, v_all, x_all)
    moved = lax.all_to_all(
        lax.all_to_all(block, "vrow", split_axis=3, concat_axis=0, tiled=True),
        "img",
        split_axis=4,
        concat_axis=1,
        tiled=True,
    )
    vert_in = jnp.transpose(moved, (3, 4, 2, 0, 1)).reshape(
        v_local * x_local, channels, u_all, y_all
    )
    vout, saved_v = forward_pass(
        zero_rims(vert_in), weight_v, beta_v, shear_set, -reach, y_all, reach
    )
    output = jnp.transpose(
        vout.reshape(v_local, x_local, channels, u_all, y_all), (0, 1, 3, 4, 2)
    ).reshape(v_local, x_local, u_all * y_all * channels)
    grad_v = (
        jnp.transpose(cotangent.reshape(v_local, x_local, u_all, y_all, channels), (0, 1, 4, 2, 3))
        .reshape(v_local * x_local, channels, u_all, y_all)
        .astype(jnp.float32)
    )
    dvert, raw_weight_v, raw_beta_v = backward_pass(
        weight_v, beta_v, grad_v, saved_v, zero_rims, reach
    )
    back_block = jnp.transpose(
        dvert.reshape(v_local, x_local, channels, u_all, y_all), (3, 4, 2, 0, 1)
    )
    returned = lax.all_to_all(
        lax.all_to_all(back_block, "vrow", split_axis=0, concat_axis=3, tiled=True),
        "img",
        split_axis=1,
        concat_axis=4,
        tiled=True,
    )
    grad_h = returned.reshape(u_local * y_local, channels, v_all, x_all)
    dhor, raw_weight_h, raw_beta_h = backward_pass(
        weight_h, beta_h, grad_h.astype(jnp.float32), saved_h, zero_rims, reach
    )
    dhor_stored = jnp.transpose(
        dhor.reshape(u_local, y_local, channels, v_all, x_all), (0, 1, 4, 3, 2)
    ).reshape(u_local, y_local, x_all, v_all * channels)
    grad_features = lax.all_to_all(dhor_stored, "img", split_axis=2, concat_axis=1, tiled=True)
    raw_weight_h, raw_weight_v, raw_beta_h, raw_beta_v = lax.psum(
        (raw_weight_h, raw_weight_v, raw_beta_h, raw_beta_v), ("vrow", "img")
    )
    factor = float(u_all * v_all * y_all * x_all) ** (-0.5)
    return (
        output,
        grad_features,
        raw_weight_h * factor,
        raw_weight_v * factor,
        raw_beta_h * factor,
        raw_beta_v * factor,
    )


def solution(mesh):
    placed = (P("vrow", None, "img", None), P(), P(), P(), P(), P(), P("vrow", "img", None))
    return jax.shard_map(
        per_device,
        mesh=mesh,
        in_specs=placed,
        out_specs=(P("vrow", "img", None), P("vrow", None, "img", None), P(), P(), P(), P()),
        check_vma=False,
    )
```

profile of v0, /device:TPU:1, one launch (start us, length us, event | category | flops | bytes accessed | tf_op | source)
XLA Modules:
  0.0 720.8 jit_solution(4382883863679388415)
XLA Ops:
  7.2 6.8 all-to-all-start
  38.2 15.4 %broadcast_multiply_fusion.4 = (bf16[1,64,16,134]{1,0,3,2:T(2,128)(2,1)S(1)}, bf16[1,64,16,134]{1,0,3,2:T(2,128)(2,1)S(1)}, bf16[1,64,16,134]{1,0,3,2:T(2,128)(2...) fusion(bf16[16,134]{1,0:T(8,128)(2,1)S(1)} %copy-done.121, bf16[1,64,16,128]{1,0,3,2:T(2,128)(2,1)S(1)} %copy.364, ...), kind=kLoop, calls=%fused_computation.390 | loop fusion | flops 686080 | bytes 1655744 | tf_op jit(solution)/shard_map/mul | solution.py:61
  58.2 2.8 copy.370
  67.7 2.8 copy.384
  79.1 2.7 copy.398
  85.6 3.6 copy.411
  91.2 2.7 copy.412
  97.6 3.7 copy.425
  103.5 2.7 copy.426
  109.8 3.6 pad_dynamic-slice_fusion.39
  113.5 2.8 copy.365
  132.4 6.5 pad_dynamic-slice_fusion.35
  138.8 3.0 copy.393
  154.8 3.1 add_multiply_fusion.3
  159.0 3.7 add_multiply_fusion.2
  164.0 2.6 copy.543
  166.7 6.9 pad_dynamic-slice_fusion.31
  173.5 2.8 copy.421
  200.7 2.7 add_multiply_fusion.1
  206.5 3.8 add_multiply_fusion
  211.6 2.6 copy.545
  216.6 7.4 %all-to-all-start.1 = ((bf16[1,1,64,16,128]{4,2,1,0,3:T(8,128)(2,1)}), bf16[1,1,64,16,128]{4,2,1,0,3:T(8,128)(2,1)S(1)}, u32[]{:S(2)}, u32[]{:S(2)}) async-start(bf16[1,1,64,16,128]{4,2,1,0,3:T(8,128)(2,1)} %copy.435), calls=%async_computation.1 | async-start | bytes 524288 | tf_op jit(solution)/shard_map/all_to_all | solution.py:141
  224.7 7.8 %all-to-all-done.1 = bf16[1,1,64,16,128]{4,2,1,0,3:T(8,128)(2,1)S(1)} async-done(((bf16[1,1,64,16,128]{4,2,1,0,3:T(8,128)(2,1)}), bf16[1,1,64,16,128]{4,2,1,0,3:T(8,128)(2,1)S(1)}, u32[]{:S(2)}, u32[]{:S(2)}) %all-to-all-start.1) | async-done | bytes 262176 | tf_op jit(solution)/shard_map/all_to_all | solution.py:141
  234.4 6.1 all-to-all-start.2
  317.1 4.1 all-to-all-start.3
  321.2 5.7 fusion.86
  332.5 6.3 all-to-all-start.4
  353.9 4.3 fusion.665
  358.2 4.5 fusion.666
  362.7 4.5 fusion.664
  368.5 4.3 fusion.662
  372.8 4.5 fusion.663
  377.4 4.5 fusion.661
  383.1 4.3 fusion.659
  387.5 4.5 fusion.660
  392.0 4.5 fusion.658
  397.8 4.3 fusion.656
  402.1 3.9 fusion.657
  406.0 4.5 fusion.655
  411.8 4.3 fusion.653
  416.1 4.5 fusion.654
  420.7 4.5 fusion.652
  425.2 3.0 fusion.363
  478.9 2.6 copy.551
  481.6 3.1 fusion.301
  485.4 63.5 %all-reduce.24 = (f32[5,64]{1,0:T(8,128)S(1)}, f32[5,64]{1,0:T(8,128)S(1)}) all-reduce(f32[5,64]{1,0:T(8,128)S(1)} %stack.89, f32[5,64]{1,0:T(8,128)S(1)} %copy-done.126), channel_id=1, replica_groups=mesh['vrow'=8,'img'=16] {'vrow','img'}, use_global_device_ids=true, to_apply=%region_7.8 | all-reduce | flops 640 | bytes 5120 | tf_op jit(solution)/shard_map/psum | solution.py:182
  553.8 4.0 all-to-all-start.5
  559.4 150.4 %all-reduce.28.cloned.1.call-done = (f32[64,64,3,3]{0,1,3,2:T(8,128)}, f32[64,64,3,3]{0,1,3,2:T(8,128)}) async-done(((f32[64,64,3,3]{0,1,3,2:T(8,128)}, f32[64,64,3,3]{0,1,3,2:T(8,128)}), (f32[64,64,3,3]{0,1,3,2:T(8,128)}, f32[64,64,3,3]{0,1,3,2:T(8,128)})) %all-reduce.28.cloned.1.call-update) | async-done | bytes 294928 | tf_op jit(solution)/shard_map/psum | solution.py:182
  (645 shorter events, 263.7 us)
Async XLA Ops:
  7.2 29.0 %all-to-all-start = ((bf16[1,16,8,1024]{3,2,0,1:T(8,128)(2,1)}), bf16[1,16,8,1024]{3,2,0,1:T(8,128)(2,1)S(1)}, u32[]{:S(2)}, u32[]{:S(2)}) async-start(bf16[1,16,8,1024]{3,2,0,1:T(8,128)(2,1)} %bitcast.649), calls=%async_computation | async-start | bytes 524288 | tf_op jit(solution)/shard_map/all_to_all | solution.py:132
  53.6 56.2 %copy-start.3 = (bf16[1,64,16,134]{1,0,3,2:T(2,128)(2,1)}, bf16[1,64,16,134]{1,0,3,2:T(2,128)(2,1)S(1)}, u32[]{:S(2)}) copy-start(bf16[1,64,16,134]{1,0,3,2:T(2,128)(2,1)S(1)} %get-tuple-element.100) | copy-start | bytes 823300
  53.6 78.7 %copy-start.5 = (bf16[1,64,16,134]{1,0,3,2:T(2,128)(2,1)}, bf16[1,64,16,134]{1,0,3,2:T(2,128)(2,1)S(1)}, u32[]{:S(2)}) copy-start(bf16[1,64,16,134]{1,0,3,2:T(2,128)(2,1)S(1)} %get-tuple-element.101) | copy-start | bytes 823300
  53.6 78.7 %copy-start.7 = (bf16[1,64,16,134]{1,0,3,2:T(2,128)(2,1)}, bf16[1,64,16,134]{1,0,3,2:T(2,128)(2,1)S(1)}, u32[]{:S(2)}) copy-start(bf16[1,64,16,134]{1,0,3,2:T(2,128)(2,1)S(1)} %get-tuple-element.102) | copy-start | bytes 823300
  132.3 81.9 %copy-start.12 = (f32[16,1,128,64]{2,0,3,1:T(8,128)}, f32[16,1,128,64]{2,0,3,1:T(8,128)S(1)}, u32[]{:S(2)}) copy-start(f32[16,1,128,64]{2,0,3,1:T(8,128)S(1)} %copy.541) | copy-start | bytes 1572868
  159.0 55.2 %copy-start.14 = (f32[16,1,128,64]{2,0,3,1:T(8,128)}, f32[16,1,128,64]{2,0,3,1:T(8,128)S(1)}, u32[]{:S(2)}) copy-start(f32[16,1,128,64]{2,0,3,1:T(8,128)S(1)} %copy.542) | copy-start | bytes 1572868
  206.4 7.8 %copy-start.18 = (f32[16,1,128,64]{2,0,3,1:T(8,128)}, f32[16,1,128,64]{2,0,3,1:T(8,128)S(1)}, u32[]{:S(2)}) copy-start(f32[16,1,128,64]{2,0,3,1:T(8,128)S(1)} %copy.544) | copy-start | bytes 1572868
  214.3 9.6 %copy-start.153 = (f32[5,64]{1,0:T(8,128)S(1)}, f32[5,64]{1,0:T(8,128)}, u32[]{:S(2)}) copy-start(f32[5,64]{1,0:T(8,128)} %param.11) | copy-start | bytes 3844
  214.3 10.2 %copy-start.140 = (pred[8,22]{1,0:T(8,128)(4,1)S(1)}, pred[8,22]{1,0:T(8,128)(4,1)}, u32[]{:S(2)}) copy-start(pred[8,22]{1,0:T(8,128)(4,1)} %get-tuple-element.141) | copy-start | bytes 532
  214.4 10.2 %copy-start.141 = (pred[8,22]{1,0:T(8,128)(4,1)S(1)}, pred[8,22]{1,0:T(8,128)(4,1)}, u32[]{:S(2)}) copy-start(pred[8,22]{1,0:T(8,128)(4,1)} %get-tuple-element.164) | copy-start | bytes 532
  216.6 15.9 %all-to-all-start.1 = ((bf16[1,1,64,16,128]{4,2,1,0,3:T(8,128)(2,1)}), bf16[1,1,64,16,128]{4,2,1,0,3:T(8,128)(2,1)S(1)}, u32[]{:S(2)}, u32[]{:S(2)}) async-start(bf16[1,1,64,16,128]{4,2,1,0,3:T(8,128)(2,1)} %copy.435), calls=%async_computation.1 | async-start | bytes 524288 | tf_op jit(solution)/shard_map/all_to_all | solution.py:141
  224.6 47.6 %copy-start.142 = (f32[64]{0:T(128)}, f32[64]{0:T(128)S(1)}, u32[]{:S(2)}) copy-start(f32[64]{0:T(128)S(1)} %get-tuple-element.126) | copy-start | bytes 772
  233.0 7.6 %copy-start.139 = (pred[8,22]{1,0:T(8,128)(4,1)S(1)}, pred[8,22]{1,0:T(8,128)(4,1)}, u32[]{:S(2)}) copy-start(pred[8,22]{1,0:T(8,128)(4,1)} %get-tuple-element.166) | copy-start | bytes 532
  234.4 20.1 %copy-start.137 = (pred[8,22]{1,0:T(8,128)(4,1)S(1)}, pred[8,22]{1,0:T(8,128)(4,1)}, u32[]{:S(2)}) copy-start(pred[8,22]{1,0:T(8,128)(4,1)} %get-tuple-element.160) | copy-start | bytes 532
  234.4 20.1 %copy-start.138 = (pred[8,22]{1,0:T(8,128)(4,1)S(1)}, pred[8,22]{1,0:T(8,128)(4,1)}, u32[]{:S(2)}) copy-start(pred[8,22]{1,0:T(8,128)(4,1)} %get-tuple-element.162) | copy-start | bytes 532
  234.4 20.2 %copy-start.50 = (f32[16,8,17,64]{3,1,2,0:T(8,128)S(1)}, f32[16,8,17,64]{3,1,2,0:T(8,128)}, u32[]{:S(2)}) copy-start(f32[16,8,17,64]{3,1,2,0:T(8,128)} %get-tuple-element.88) | copy-start | bytes 1671172
  234.4 33.3 %all-to-all-start.2 = ((bf16[16,2,4096]{2,1,0:T(2,128)(2,1)}), bf16[16,2,4096]{2,1,0:T(2,128)(2,1)}, u32[]{:S(2)}, u32[]{:S(2)}) async-start(bf16[16,2,4096]{2,1,0:T(2,128)(2,1)} %reshape.837), calls=%async_computation.2 | async-start | bytes 524288 | tf_op jit(solution)/shard_map/all_to_all | solution.py:140
  315.0 6.2 copy-start.143
  317.1 12.8 %all-to-all-start.3 = ((bf16[8,2,8192]{2,1,0:T(2,128)(2,1)}), bf16[8,2,8192]{2,1,0:T(2,128)(2,1)}, u32[]{:S(2)}, u32[]{:S(2)}) async-start(bf16[8,2,8192]{2,1,0:T(2,128)(2,1)} %reshape.839), calls=%async_computation.3 | async-start | bytes 524288 | tf_op jit(solution)/shard_map/all_to_all | solution.py:168
  321.2 5.8 copy-start.159
  331.3 7.5 %copy-start.160 = (bf16[16,64,8,16]{1,0,3,2:T(8,128)(2,1)S(1)}, bf16[16,64,8,16]{1,0,3,2:T(8,128)(2,1)}, u32[]{:S(2)}) copy-start(bf16[16,64,8,16]{1,0,3,2:T(8,128)(2,1)} %copy-done.158) | copy-start | bytes 786436
  332.5 13.7 %all-to-all-start.4 = ((bf16[16,2,4096]{2,1,0:T(2,128)(2,1)}), bf16[16,2,4096]{2,1,0:T(2,128)(2,1)S(1)}, u32[]{:S(2)}, u32[]{:S(2)}) async-start(bf16[16,2,4096]{2,1,0:T(2,128)(2,1)} %reshape.841), calls=%async_computation.4 | async-start | bytes 524288 | tf_op jit(solution)/shard_map/all_to_all | solution.py:167
  358.2 4.5 copy-start.35
  372.8 4.5 copy-start.32
  377.4 4.5 copy-start.58
  387.5 4.5 copy-start.28
  392.0 4.5 copy-start.57
  406.0 4.5 copy-start.56
  416.1 4.5 copy-start.21
  420.7 4.5 copy-start.49
  477.1 4.5 copy-start.72
  477.1 4.5 copy-start.74
  550.1 7.7 %copy-start.79 = (f32[64,64,1,3]{0,1,3,2:T(8,128)S(1)}, f32[64,64,1,3]{0,1,3,2:T(8,128)}, u32[]{:S(2)}) copy-start(f32[64,64,1,3]{0,1,3,2:T(8,128)} %fusion.665) | copy-start | bytes 147460
  550.2 7.7 %copy-start.80 = (f32[64,64,1,3]{0,1,3,2:T(8,128)S(1)}, f32[64,64,1,3]{0,1,3,2:T(8,128)}, u32[]{:S(2)}) copy-start(f32[64,64,1,3]{0,1,3,2:T(8,128)} %fusion.666) | copy-start | bytes 147460
  550.2 7.7 %copy-start.81 = (f32[64,64,1,3]{0,1,3,2:T(8,128)S(1)}, f32[64,64,1,3]{0,1,3,2:T(8,128)}, u32[]{:S(2)}) copy-start(f32[64,64,1,3]{0,1,3,2:T(8,128)} %fusion.664) | copy-start | bytes 147460
  550.2 7.7 %copy-start.82 = (f32[64,64,1,3]{0,1,3,2:T(8,128)S(1)}, f32[64,64,1,3]{0,1,3,2:T(8,128)}, u32[]{:S(2)}) copy-start(f32[64,64,1,3]{0,1,3,2:T(8,128)} %fusion.662) | copy-start | bytes 147460
  550.2 7.7 %copy-start.83 = (f32[64,64,1,3]{0,1,3,2:T(8,128)S(1)}, f32[64,64,1,3]{0,1,3,2:T(8,128)}, u32[]{:S(2)}) copy-start(f32[64,64,1,3]{0,1,3,2:T(8,128)} %fusion.663) | copy-start | bytes 147460
  550.2 7.7 %copy-start.84 = (f32[64,64,1,3]{0,1,3,2:T(8,128)S(1)}, f32[64,64,1,3]{0,1,3,2:T(8,128)}, u32[]{:S(2)}) copy-start(f32[64,64,1,3]{0,1,3,2:T(8,128)} %fusion.661) | copy-start | bytes 147460
  550.2 7.7 %copy-start.85 = (f32[64,64,1,3]{0,1,3,2:T(8,128)S(1)}, f32[64,64,1,3]{0,1,3,2:T(8,128)}, u32[]{:S(2)}) copy-start(f32[64,64,1,3]{0,1,3,2:T(8,128)} %fusion.659) | copy-start | bytes 147460
  550.2 7.7 %copy-start.86 = (f32[64,64,1,3]{0,1,3,2:T(8,128)S(1)}, f32[64,64,1,3]{0,1,3,2:T(8,128)}, u32[]{:S(2)}) copy-start(f32[64,64,1,3]{0,1,3,2:T(8,128)} %fusion.660) | copy-start | bytes 147460
  550.2 7.7 %copy-start.87 = (f32[64,64,1,3]{0,1,3,2:T(8,128)S(1)}, f32[64,64,1,3]{0,1,3,2:T(8,128)}, u32[]{:S(2)}) copy-start(f32[64,64,1,3]{0,1,3,2:T(8,128)} %fusion.658) | copy-start | bytes 147460
  550.2 7.7 %copy-start.88 = (f32[64,64,1,3]{0,1,3,2:T(8,128)S(1)}, f32[64,64,1,3]{0,1,3,2:T(8,128)}, u32[]{:S(2)}) copy-start(f32[64,64,1,3]{0,1,3,2:T(8,128)} %fusion.656) | copy-start | bytes 147460
  550.2 7.7 %copy-start.89 = (f32[64,64,1,3]{0,1,3,2:T(8,128)S(1)}, f32[64,64,1,3]{0,1,3,2:T(8,128)}, u32[]{:S(2)}) copy-start(f32[64,64,1,3]{0,1,3,2:T(8,128)} %fusion.655) | copy-start | bytes 147460
  550.3 7.7 %copy-start.90 = (f32[64,64,1,3]{0,1,3,2:T(8,128)S(1)}, f32[64,64,1,3]{0,1,3,2:T(8,128)}, u32[]{:S(2)}) copy-start(f32[64,64,1,3]{0,1,3,2:T(8,128)} %fusion.653) | copy-start | bytes 147460
  550.3 7.7 %copy-start.91 = (f32[64,64,1,3]{0,1,3,2:T(8,128)S(1)}, f32[64,64,1,3]{0,1,3,2:T(8,128)}, u32[]{:S(2)}) copy-start(f32[64,64,1,3]{0,1,3,2:T(8,128)} %fusion.654) | copy-start | bytes 147460
  550.3 7.7 %copy-start.92 = (f32[64,64,1,3]{0,1,3,2:T(8,128)S(1)}, f32[64,64,1,3]{0,1,3,2:T(8,128)}, u32[]{:S(2)}) copy-start(f32[64,64,1,3]{0,1,3,2:T(8,128)} %fusion.652) | copy-start | bytes 147460
  553.8 158.8 %all-to-all-start.5 = ((bf16[16,2,4096]{2,1,0:T(2,128)(2,1)}), bf16[16,2,4096]{2,1,0:T(2,128)(2,1)S(1)}, u32[]{:S(2)}, u32[]{:S(2)}) async-start(bf16[16,2,4096]{2,1,0:T(2,128)(2,1)} %reshape.843), calls=%async_computation.5 | async-start | bytes 524288 | tf_op jit(solution)/shard_map/all_to_all | solution.py:181
  557.8 152.1 %all-reduce.28.cloned.1.call-start = ((), (), s32[]{:S(2)}) async-start(), calls=%async_computation.6 | async-start | bytes 1179648 | tf_op jit(solution)/shard_map/psum | solution.py:182
  (120 other events, 230.6 us)
Sparse Core Ops, SparseCore 0:
  564.0 145.8 all-reduce.27
where the time goes:
time: 733 us; the launch traced here: 721 us
  local copies, waits for them, and re-layouts  215 us (29%)
  waiting for transfers between devices  162 us (22%)
  matrix products  159 us (22%)
  blocking collectives  63.5 us (9%)
  other arithmetic  47.4 us (6%)
  between operations  39.2 us (5%)
  starting transfers between devices  34.7 us (5%)
    psum x1, waiting for transfers between devices, per_device(): lax.psum((raw_weight_h, raw_weight_v, raw_beta_h, raw_beta_v), ('vrow', '...  150 us
    transpose x30, matrix products, conv_weight(): return jnp.transpose(result, (1, 0, 2, 3))  84.4 us
    unnamed x371, local copies, waits for them, and re-layouts  75.8 us
    psum x1, blocking collectives, per_device(): lax.psum((raw_weight_h, raw_weight_v, raw_beta_h, raw_beta_v), ('vrow', '...  63.5 us
    conv_general_dilated x30, matrix products, conv_taps(): lax.conv_general_dilated(source, kernel_row, (1, 1), ((0, 0), (0, 0)), di...  52.2 us
    dynamic_slice x38, local copies, waits for them, and re-layouts, window(): return lax.dynamic_slice(padded, starts, sizes)  44.9 us
    mul x15, local copies, waits for them, and re-layouts, masked_source(): return (extended * inside[None, None].astype(extended.dtype), inside)  38 us
    conv_general_dilated x30, matrix products, conv_back(): lax.conv_general_dilated(grads, kernel_row, (1, 1), ((0, 0), (0, 0)), dim...  22 us
  transfers between devices with their start and end apart: 7, of which 4 were waited for; matrix products, arithmetic and copies ran while one was open for 6% of the time, Pallas kernels for 0%

commit v1 on v0

v1 whole, which is shorter than its diff:
```python
import jax
import jax.numpy as jnp
from jax import lax
from jax.experimental import pallas as pl
from jax.experimental.pallas import tpu as pltpu
from jax.sharding import PartitionSpec as P

BF = jnp.bfloat16
F32 = jnp.float32
LANES = 128
HALF = 64
TAPS = 9
REACH = 3
VMEM_BYTES = 60 * 1024 * 1024
NT = (((1,), (1,)), ((), ()))
NN = (((1,), (0,)), ((), ()))
TN = (((0,), (0,)), ((), ()))


def mm(lhs, rhs, dims):
    return lax.dot_general(lhs, rhs, dims, preferred_element_type=F32)


def lanes_of(shape):
    return lax.broadcasted_iota(jnp.int32, shape, len(shape) - 1)


def swap(value):
    return pltpu.roll(value, HALF, axis=value.ndim - 1)


def low(shape):
    return lanes_of(shape) < HALF


def sigmoid(value):
    return 0.5 * jnp.tanh(0.5 * value) + 0.5


def fill_weights(w_ref, wt_ref):
    zero = jnp.zeros((HALF, HALF), BF)
    for tap in range(TAPS):
        w = w_ref[tap]
        wt_ref[pl.ds(tap * LANES, HALF), :] = jnp.concatenate([w, zero], axis=1)
        wt_ref[pl.ds(tap * LANES + HALF, HALF), :] = jnp.concatenate([zero, w], axis=1)


def pack_grads(blocks, blend_ref, pay_ref):
    first = low((HALF, LANES))
    rows = lax.broadcasted_iota(jnp.int32, (HALF, LANES), 0)
    blend = jnp.zeros((HALF, LANES), F32)
    for k in range(blend_ref.shape[0]):
        line = jnp.sum(blend_ref[k], axis=0, keepdims=True)
        line = line + swap(line)
        blend = blend + jnp.where(rows == k, line, 0.0)
    for pair in range(5):
        even = blocks[2 * pair]
        left = even[:HALF] + swap(even[HALF:])
        if pair < 4:
            odd = blocks[2 * pair + 1]
            right = swap(odd[:HALF]) + odd[HALF:]
        else:
            right = blend
        pay_ref[pl.ds(pair * HALF, HALF), :] = jnp.where(first, left, right)


def h_forward(shear, base, beta, w_ref, fl, fm, fr, hfeat, pre_ref, f0_out, fm_out, fp_out, stage, f0, fmi, fpl, taps, wt):
    shears = shear.shape[0]
    fill_weights(w_ref, wt)
    first16 = low((16, LANES))

    @pl.loop(0, 16)
    def _(y):
        for part, ref in enumerate((fl, fm, fr)):
            for q in range(8):
                stage[q, pl.ds(y * 24 + 8 * part, 8), :] = ref[y, :, pl.ds(q * LANES, LANES)].astype(F32)

    @pl.loop(0, 20)
    def _(x):
        own = [stage[q, pl.ds(x + 2, 16, stride=24), :] for q in range(8)]
        turned = [swap(a) for a in own]
        zero = jnp.zeros((16, LANES), F32)
        moved = [
            jnp.where(first16, turned[q - 1] if q > 0 else zero, turned[q] if q < 8 else zero).astype(BF)
            for q in range(9)
        ]
        for q in range(8):
            at = pl.ds(x * LANES + q * 16, 16)
            f0[at, :] = own[q].astype(BF)
            fmi[at, :] = moved[q]
            fpl[at, :] = moved[q + 1]
        at = pl.ds(pl.multiple_of(x * LANES, LANES), LANES)
        for side, ref in enumerate((fmi, f0, fpl)):
            product = mm(ref[at, :], wt[pl.ds(side * 384, 384), :], NT)
            for j in range(3):
                taps[3 * side + j, x] = product[:, j * LANES : (j + 1) * LANES]

    f0_out[...] = f0[pl.ds(6 * LANES, 1024), :]
    fm_out[...] = fmi[pl.ds(6 * LANES, 1024), :]
    fp_out[...] = fpl[pl.ds(6 * LANES, 1024), :]

    half = (lanes_of((16, LANES)) >= HALF).astype(jnp.int32)

    def body(xe, q, local):
        rows = pl.ds(pl.multiple_of(q * 16, 16), 16)
        center = xe + 3
        vrel = half + (2 * q - 8)
        xg = base[0] + xe - REACH
        mid = taps[4, center, rows, :]
        left = taps[3, center - 1, rows, :]
        right = taps[5, center + 1, rows, :]
        branch = jnp.zeros((16, LANES), F32)
        for k in range(shears):
            d = shear[k]
            xs = xg - d * vrel
            a, b = center - d, center + d
            main = mid + taps[1, a, rows, :] + taps[7, b, rows, :]
            minus = left + taps[0, a - 1, rows, :] + taps[6, b - 1, rows, :]
            plus = right + taps[2, a + 1, rows, :] + taps[8, b + 1, rows, :]
            pre = main + jnp.where(xs >= 1, minus, 0.0) + jnp.where(xs <= LANES - 2, plus, 0.0)
            pre_ref[k, xe, q] = pre
            if local:
                keep = (xs >= 0) & (xs < LANES)
                branch = branch + beta[pl.ds(k, 1), :] * jnp.where(keep, pre * sigmoid(pre), 0.0)
        if local:
            own = f0[pl.ds(pl.multiple_of(center * LANES + q * 16, 16), 16), :].astype(F32)
            hfeat[q, xe - REACH] = (own + branch).astype(BF)

    @pl.loop(0, 64)
    def _(n):
        body(n // 8 + REACH, n % 8, True)

    @pl.loop(0, 48)
    def _(n):
        xe = n // 8
        body(jnp.where(xe < REACH, xe, xe + 8), n % 8, False)


def h_backward(shear, base, beta, w_ref, pre_ref, f0, fmi, fpl, gm, gl, gr, out, pay, dps, sums, edges, dfs, stage, blend, wt):
    shears = shear.shape[0]
    fill_weights(w_ref, wt)
    half = (lanes_of((16, LANES)) >= HALF).astype(jnp.int32)
    blend[...] = jnp.zeros(blend.shape, F32)

    def body(xe, q, g, local):
        vrel = half + (2 * q - 8)
        xg = base[0] + xe - REACH
        total = [jnp.zeros((16, LANES), F32) for _ in range(3)]
        for k in range(shears):
            xs = xg - shear[k] * vrel
            pre = pre_ref[k, xe, q]
            s = sigmoid(pre)
            slope = s * (1.0 + pre * (1.0 - s))
            gk = jnp.where((xs >= 0) & (xs < LANES), g, 0.0)
            dp = (beta[pl.ds(k, 1), :] * gk * slope).astype(BF).astype(F32)
            parts = (jnp.where(xs >= 1, dp, 0.0), dp, jnp.where(xs <= LANES - 2, dp, 0.0))
            for j in range(3):
                dps[j, k, xe, q] = parts[j]
                total[j] = total[j] + parts[j]
            if local:
                blend[k] += gk * (pre * s)
        for j in range(3):
            sums[j, xe, q] = total[j]

    @pl.loop(0, 64)
    def _(n):
        x, q = n // 8, n % 8
        body(x + REACH, q, gm[q, x].astype(F32), True)

    @pl.loop(0, 24)
    def _(n):
        x, q = n // 8, n % 8
        body(x, q, gl[q, x].astype(F32), False)
        body(x + 8 + REACH, q, gr[q, x].astype(F32), False)

    @pl.loop(0, 64)
    def _(n):
        x, q = n // 8, n % 8
        xe = x + REACH
        at = pl.ds(pl.multiple_of(n * 16, 16), 16)
        for j in range(3):
            below = jnp.zeros((16, LANES), F32)
            above = jnp.zeros((16, LANES), F32)
            for k in range(shears):
                d = shear[k]
                below = below + dps[j, k, xe + d - (j - 1), q]
                above = above + dps[j, k, xe - d - (j - 1), q]
            lanes = pl.ds(j * LANES, LANES)
            edges[0, at, lanes] = below.astype(BF)
            edges[1, at, lanes] = sums[j, xe - (j - 1), q].astype(BF)
            edges[2, at, lanes] = above.astype(BF)

    blocks = []
    for side, ref in enumerate((fmi, f0, fpl)):
        grad = mm(edges[side], ref[...], TN)
        blocks += [grad[j * LANES : (j + 1) * LANES] for j in range(3)]
    pack_grads(blocks, blend, pay)

    @pl.loop(0, 8)
    def _(x):
        at = pl.ds(pl.multiple_of(x * LANES, LANES), LANES)
        for side in range(3):
            dfs[side, at, :] = mm(edges[side, at, :], wt[pl.ds(side * 384, 384), :], NN)

    first16 = low((16, LANES))

    @pl.loop(0, 8)
    def _(x):
        def piece(side, q):
            if q < 0 or q > 7:
                return jnp.zeros((16, LANES), F32)
            return dfs[side, pl.ds(x * LANES + q * 16, 16), :]

        for q in range(8):
            upper = piece(0, q) + piece(2, q - 1)
            lower = piece(0, q + 1) + piece(2, q)
            turned = swap(jnp.where(first16, lower, upper))
            total = gm[q, x].astype(F32) + piece(1, q) + turned
            stage[q, pl.ds(x * 16, 16), :] = total

    @pl.loop(0, 16)
    def _(y):
        for q in range(8):
            out[y, :, pl.ds(q * LANES, LANES)] = stage[q, pl.ds(y, 8, stride=16), :].astype(BF)


def v_both(shear, beta, w_ref, h_ref, cot, out, dvert, pay, own, fv, taps, dps, sums, grads, outs, edges, blend, wt):
    shears = shear.shape[0]
    fill_weights(w_ref, wt)
    blend[...] = jnp.zeros(blend.shape, F32)
    first8 = low((8, LANES))

    for tap in range(TAPS):
        for u in (0, 9):
            taps[tap, u] = jnp.zeros((22, 8, LANES), F32)

    @pl.loop(0, 10)
    def _(u):
        rim = jnp.zeros((REACH, 8, LANES), F32)
        for tap in range(TAPS):
            taps[tap, u, pl.ds(0, REACH)] = rim
            taps[tap, u, pl.ds(16 + REACH, REACH)] = rim
        for j in range(3):
            sums[j, u, pl.ds(0, REACH)] = rim
            sums[j, u, pl.ds(16 + REACH, REACH)] = rim
            for k in range(shears):
                dps[j, k, u, pl.ds(0, REACH)] = rim
                dps[j, k, u, pl.ds(16 + REACH, REACH)] = rim

    for j in range(3):
        for k in range(shears):
            for u in (0, 9):
                dps[j, k, u] = jnp.zeros((22, 8, LANES), F32)

    @pl.loop(0, 8)
    def _(u):
        for x in range(8):
            own[u, pl.ds(x * 16, 16), :] = h_ref[u, x].astype(F32)
        for y in range(0, 16, 2):
            pair = [own[u, pl.ds(y + e, 8, stride=16), :] for e in range(2)]
            fv[pl.ds(pl.multiple_of(u * LANES + y * 8, 16), 16), :] = jnp.concatenate(pair, axis=0).astype(BF)
        rows = pl.ds(pl.multiple_of(u * LANES, LANES), LANES)
        for side in range(3):
            product = mm(fv[rows, :], wt[pl.ds(side * 384, 384), :], NT)
            for j in range(3):
                taps[3 * side + j, u + 1, pl.ds(REACH, 16)] = product[:, j * LANES : (j + 1) * LANES].reshape(16, 8, LANES)
        for q in range(8):
            lanes = pl.ds(pl.multiple_of((u * 8 + q) * LANES, LANES), LANES)
            a, b = cot[0, :, lanes].astype(F32), cot[1, :, lanes].astype(F32)
            grads[u, 2 * q] = jnp.where(first8, a, swap(b))
            grads[u, 2 * q + 1] = jnp.where(first8, swap(a), b)

    def body(u, y):
        up, yp = u + 1, y + REACH
        g = grads[u, y]
        mid = taps[4, up, yp]
        left = taps[3, up, yp - 1]
        right = taps[5, up, yp + 1]
        branch = jnp.zeros((8, LANES), F32)
        total = [jnp.zeros((8, LANES), F32) for _ in range(3)]
        for k in range(shears):
            d = shear[k]
            ys = y - d * (u - 4)
            keep = ((ys >= 0) & (ys < 16)).astype(F32)
            has_minus = (ys >= 1).astype(F32)
            has_plus = (ys <= 14).astype(F32)
            a, b = yp - d, yp + d
            main = mid + taps[1, u, a] + taps[7, up + 1, b]
            minus = left + taps[0, u, a - 1] + taps[6, up + 1, b - 1]
            plus = right + taps[2, u, a + 1] + taps[8, up + 1, b + 1]
            pre = main + has_minus * minus + has_plus * plus
            s = sigmoid(pre)
            act = keep * (pre * s)
            slope = s * (1.0 + pre * (1.0 - s))
            bk = beta[pl.ds(k, 1), :]
            branch = branch + bk * act
            blend[k] += g * act
            dp = (bk * (keep * g) * slope).astype(BF).astype(F32)
            parts = (has_minus * dp, dp, has_plus * dp)
            for j in range(3):
                dps[j, k, up, yp] = parts[j]
                total[j] = total[j] + parts[j]
        for j in range(3):
            sums[j, up, yp] = total[j]
        outs[u, y] = own[u, pl.ds(y, 8, stride=16), :] + branch

    @pl.loop(0, 128)
    def _(n):
        body(n // 16, n % 16)

    @pl.loop(0, 64)
    def _(n):
        u, y = n // 8, (n % 8) * 2
        at = pl.ds(pl.multiple_of(n * 16, 16), 16)
        for j in range(3):
            cells = []
            for e in range(2):
                yp = y + e + REACH
                below = jnp.zeros((8, LANES), F32)
                above = jnp.zeros((8, LANES), F32)
                for k in range(shears):
                    d = shear[k]
                    below = below + dps[j, k, u + 2, yp + d - (j - 1)]
                    above = above + dps[j, k, u, yp - d - (j - 1)]
                cells.append((below, sums[j, u + 1, yp - (j - 1)], above))
            for side in range(3):
                value = jnp.concatenate([cells[0][side], cells[1][side]], axis=0)
                edges[at, pl.ds((3 * side + j) * LANES, LANES)] = value.astype(BF)

    blocks = []
    for side in range(3):
        grad = mm(edges[:, pl.ds(side * 384, 384)], fv[...], TN)
        blocks += [grad[j * LANES : (j + 1) * LANES] for j in range(3)]
    pack_grads(blocks, blend, pay)

    @pl.loop(0, 8)
    def _(u):
        rows = pl.ds(pl.multiple_of(u * LANES, LANES), LANES)
        back = mm(edges[rows, :], wt[...], NN)
        own[u] = grads[u].reshape(LANES, LANES) + back
        for x in range(8):
            dvert[u, x] = own[u, pl.ds(x, 16, stride=8), :].astype(BF)
        for q in range(8):
            lanes = pl.ds(pl.multiple_of((u * 8 + q) * LANES, LANES), LANES)
            a, b = outs[u, 2 * q], outs[u, 2 * q + 1]
            out[0, :, lanes] = jnp.where(first8, a, swap(b)).astype(BF)
            out[1, :, lanes] = jnp.where(first8, swap(a), b).astype(BF)


def call(body, operands, out_shapes, scratch, smem, cost):
    vmem = pl.BlockSpec(memory_space=pltpu.VMEM)
    specs = [pl.BlockSpec(memory_space=pltpu.SMEM)] * smem + [vmem] * (len(operands) - smem)
    return pl.pallas_call(
        body,
        out_shape=out_shapes,
        in_specs=specs,
        out_specs=[vmem] * len(out_shapes),
        scratch_shapes=scratch,
        compiler_params=pltpu.CompilerParams(vmem_limit_bytes=VMEM_BYTES),
        cost_estimate=pl.CostEstimate(flops=cost, bytes_accessed=4_000_000, transcendentals=1_000_000),
    )(*operands)


def reduce_all(pay):
    part = lax.all_to_all(pay.reshape(16, 40, LANES), "img", 0, 0, tiled=True).sum(0)
    part = lax.all_to_all(part.reshape(8, 5, LANES), "vrow", 0, 0, tiled=True).sum(0)
    part = lax.all_to_all(jnp.broadcast_to(part[None], (8, 5, LANES)), "vrow", 0, 0, tiled=True).reshape(40, LANES)
    return lax.all_to_all(jnp.broadcast_to(part[None], (16, 40, LANES)), "img", 0, 0, tiled=True).reshape(640, LANES)


def per_device(features, weight_h, weight_v, beta_h, beta_v, shear_set, cotangent):
    shears = shear_set.shape[0]
    img = lax.axis_size("img")
    sds = jax.ShapeDtypeStruct
    own = features.reshape(16, 8, 1024)
    to_right = [(i, i + 1) for i in range(img - 1)]
    to_left = [(i + 1, i) for i in range(img - 1)]
    from_left = lax.ppermute(own, "img", to_right)
    from_right = lax.ppermute(own, "img", to_left)
    base = (lax.axis_index("img") * 8).astype(jnp.int32).reshape(1)
    wide_h = jnp.concatenate([beta_h, beta_h], axis=1)
    wide_v = jnp.concatenate([beta_v, beta_v], axis=1)
    w_h = jnp.transpose(weight_h, (2, 3, 0, 1)).reshape(TAPS, HALF, HALF)
    w_v = jnp.transpose(weight_v, (2, 3, 0, 1)).reshape(TAPS, HALF, HALF)

    hfeat, pre, f0, fmi, fpl = call(
        h_forward,
        (shear_set, base, wide_h, w_h, from_left, own, from_right),
        [sds((8, 8, 16, LANES), BF), sds((shears, 14, 8, 16, LANES), F32)] + [sds((1024, LANES), BF)] * 3,
        [pltpu.VMEM((8, 384, LANES), F32)]
        + [pltpu.VMEM((20 * LANES, LANES), BF)] * 3
        + [pltpu.VMEM((TAPS, 20, LANES, LANES), F32), pltpu.VMEM((TAPS * LANES, LANES), BF)],
        2,
        2 * 2560 * LANES * TAPS * LANES,
    )
    moved = lax.all_to_all(hfeat, "vrow", 0, 0, tiled=True)
    output, dvert, pay_v = call(
        v_both,
        (shear_set, wide_v, w_v, moved, cotangent),
        [sds((2, 8, 8192), BF), sds((8, 8, 16, LANES), BF), sds((320, LANES), F32)],
        [
            pltpu.VMEM((8, LANES, LANES), F32),
            pltpu.VMEM((1024, LANES), BF),
            pltpu.VMEM((TAPS, 10, 22, 8, LANES), F32),
            pltpu.VMEM((3, shears, 10, 22, 8, LANES), F32),
            pltpu.VMEM((3, 10, 22, 8, LANES), F32),
            pltpu.VMEM((8, 16, 8, LANES), F32),
            pltpu.VMEM((8, 16, 8, LANES), F32),
            pltpu.VMEM((1024, TAPS * LANES), BF),
            pltpu.VMEM((shears, 8, LANES), F32),
            pltpu.VMEM((TAPS * LANES, LANES), BF),
        ],
        1,
        6 * 1024 * LANES * TAPS * LANES,
    )
    grad = lax.all_to_all(dvert, "vrow", 0, 0, tiled=True)
    grad_right = lax.ppermute(grad[:, :REACH], "img", to_left)
    grad_left = lax.ppermute(grad[:, 8 - REACH :], "img", to_right)
    grad_features, pay_h = call(
        h_backward,
        (shear_set, base, wide_h, w_h, pre, f0, fmi, fpl, grad, grad_left, grad_right),
        [sds((16, 8, 1024), BF), sds((320, LANES), F32)],
        [
            pltpu.VMEM((3, shears, 14, 8, 16, LANES), F32),
            pltpu.VMEM((3, 14, 8, 16, LANES), F32),
            pltpu.VMEM((3, 1024, 384), BF),
            pltpu.VMEM((3, 1024, LANES), F32),
            pltpu.VMEM((8, LANES, LANES), F32),
            pltpu.VMEM((shears, 16, LANES), F32),
            pltpu.VMEM((TAPS * LANES, LANES), BF),
        ],
        2,
        4 * 1024 * LANES * TAPS * LANES,
    )
    total = reduce_all(jnp.concatenate([pay_h, pay_v], axis=0)) * (262144.0**-0.5)

    def unpack(block):
        pairs = jnp.stack([block[:, :HALF].reshape(5, HALF, HALF), block[:, HALF:].reshape(5, HALF, HALF)], axis=1)
        weight = jnp.transpose(pairs.reshape(10, HALF, HALF)[:TAPS].reshape(3, 3, HALF, HALF), (2, 3, 0, 1))
        return weight, block[4 * HALF : 4 * HALF + shears, HALF:]

    weight_grad_h, beta_grad_h = unpack(total[:320])
    weight_grad_v, beta_grad_v = unpack(total[320:])
    return (
        output,
        grad_features.reshape(features.shape),
        weight_grad_h,
        weight_grad_v,
        beta_grad_h,
        beta_grad_v,
    )


def solution(mesh):
    placed = (P("vrow", None, "img", None), P(), P(), P(), P(), P(), P("vrow", "img", None))
    return jax.shard_map(
        per_device,
        mesh=mesh,
        in_specs=placed,
        out_specs=(P("vrow", "img", None), P("vrow", None, "img", None), P(), P(), P(), P()),
        check_vma=False,
    )
```

time: 733 us -> 154 us (0.21); the launches traced: 721 us -> 153 us
  local copies, waits for them, and re-layouts: 215 us -> 4.4 us
  matrix products: 159 us -> 0 us
  waiting for transfers between devices: 162 us -> 11.8 us
  Pallas kernels: 0 us -> 52.7 us
  other arithmetic: 47.4 us -> 3.91 us
  between operations: 39.2 us -> 0.73 us
  starting transfers between devices: 34.7 us -> 22.1 us
    psum x1 -> x0, waiting for transfers between devices: 150 us -> none  [per_device(): lax.psum((raw_weight_h, raw_weight_v, raw_beta_h, raw_beta_v), ('vrow', '...]
    transpose x30 -> x0, matrix products: 84.4 us -> none  [conv_weight(): return jnp.transpose(result, (1, 0, 2, 3))]
    conv_general_dilated x60 -> x0, matrix products: 74.2 us -> none  [the longest x30 52.2 us: conv_taps(): lax.conv_general_dilated(source, kernel_row, (1, 1), ((0, 0), (0, 0)), di...]
    unnamed x371 -> x14, local copies, waits for them, and re-layouts: 75.8 us -> 2.05 us
    psum x1 -> x0, blocking collectives: 63.5 us -> none  [per_device(): lax.psum((raw_weight_h, raw_weight_v, raw_beta_h, raw_beta_v), ('vrow', '...]
    all_to_all x0 -> x5, blocking collectives: none -> 57.3 us  [the longest x1 14.9 us: reduce_all(): lax.all_to_all(pay.reshape(16, 40, LANES), 'img', 0, 0, tiled=True).sum(0)]
    pallas_call x0 -> x3, Pallas kernels: none -> 52.7 us  [call(): pl.pallas_call(body, out_shape=out_shapes, in_specs=specs, out_specs=[vme...]
    mul x37 -> x0, local copies, waits for them, and re-layouts: 51.9 us -> none  [the longest x15 38 us: masked_source(): return (extended * inside[None, None].astype(extended.dtype), inside)]
  transfers between devices with their start and end apart: 7 -> 5, of which waited for: 4 -> 5; matrix products, arithmetic and copies ran while one was open for 6% -> 2% of each run, Pallas kernels for 0% -> 0%
where the time goes in v1:
time: 154 us; the launch traced here: 153 us
  blocking collectives  57.3 us (37%)
  Pallas kernels  52.7 us (34%)
  starting transfers between devices  22.1 us (14%)
  waiting for transfers between devices  11.8 us (8%)
  local copies, waits for them, and re-layouts  4.4 us (3%)
  other arithmetic  3.91 us (3%)
    pallas_call x3, Pallas kernels, call(): pl.pallas_call(body, out_shape=out_shapes, in_specs=specs, out_specs=[vme...  52.7 us
    all_to_all x1, blocking collectives, reduce_all(): lax.all_to_all(pay.reshape(16, 40, LANES), 'img', 0, 0, tiled=True).sum(0)  14.9 us
    all_to_all x1, blocking collectives, reduce_all(): lax.all_to_all(jnp.broadcast_to(part[None], (16, 40, LANES)), 'img', 0, 0...  13.3 us
    all_to_all x1, blocking collectives, per_device(): grad = lax.all_to_all(dvert, 'vrow', 0, 0, tiled=True)  11.1 us
    all_to_all x1, blocking collectives, reduce_all(): lax.all_to_all(jnp.broadcast_to(part[None], (8, 5, LANES)), 'vrow', 0, 0,...  8.98 us
    all_to_all x1, blocking collectives, reduce_all(): lax.all_to_all(part.reshape(8, 5, LANES), 'vrow', 0, 0, tiled=True).sum(0)  8.98 us
    all_to_all x1, starting transfers between devices, per_device(): moved = lax.all_to_all(hfeat, 'vrow', 0, 0, tiled=True)  7.38 us
    ppermute x1, starting transfers between devices, per_device(): grad_left = lax.ppermute(grad[:, 8 - REACH:], 'img', to_right)  6.25 us
  transfers between devices with their start and end apart: 5, of which 5 were waited for; matrix products, arithmetic and copies ran while one was open for 2% of the time, Pallas kernels for 0%

profile of v1, /device:TPU:1, one launch (start us, length us, event | category | flops | bytes accessed | tf_op | source)
XLA Modules:
  0.0 152.9 jit_solution(13447552453739858931)
XLA Ops:
  0.6 3.3 %collective-permute-start.1 = (bf16[16,8,1024]{2,1,0:T(8,128)(2,1)}, bf16[16,8,1024]{2,1,0:T(8,128)(2,1)S(1)}, u32[]{:S(2)}, u32[]{:S(2)}) collective-permute-start(bf16[16,8,1024]{2,1,0:T(8,128)(2,1)} %bitcast.36), channel_id=1, source_target_pairs={{1,0},{2,1},{3,2},{4,3},{5,4},{6,5},{7,6},{8,7},{9,8},{10,9},{11,1... | collective-permute-start | bytes 786440 | tf_op jit(solution)/shard_map/ppermute | solution.py:379
  3.9 3.2 %collective-permute-start = (bf16[16,8,1024]{2,1,0:T(8,128)(2,1)}, bf16[16,8,1024]{2,1,0:T(8,128)(2,1)S(1)}, u32[]{:S(2)}, u32[]{:S(2)}) collective-permute-start(bf16[16,8,1024]{2,1,0:T(8,128)(2,1)} %bitcast.37), channel_id=1, source_target_pairs={{0,1},{1,2},{2,3},{3,4},{4,5},{5,6},{6,7},{7,8},{8,9},{9,10},{10,1... | collective-permute-start | bytes 786440 | tf_op jit(solution)/shard_map/ppermute | solution.py:378
  7.2 1.4 pad_maximum_fusion.4.beta
  8.6 0.9 collective-permute-done.1.fr
  9.5 0.0 copy-start.5
  9.5 3.1 %collective-permute-done.fl = bf16[16,8,1024]{2,1,0:T(8,128)(2,1)S(1)} collective-permute-done((bf16[16,8,1024]{2,1,0:T(8,128)(2,1)}, bf16[16,8,1024]{2,1,0:T(8,128)(2,1)S(1)}, u32[]{:S(2)}, u32[]{:S(2)}) %collective-permute-start) | collective-permute-done | bytes 262176 | tf_op jit(solution)/shard_map/ppermute | solution.py:378
  12.6 0.0 copy-start.6
  12.6 0.0 copy-done.5
  12.6 0.7 copy-done.6
  13.3 15.9 %shard_map.118 = (bf16[8,8,16,128]{3,2,1,0:T(8,128)(2,1)}, f32[5,14,8,16,128]{4,3,2,1,0:T(8,128)}, bf16[1024,128]{1,0:T(8,128)(2,1)}, bf16[1024,128]{1,0:T(8,128)(2,1)}, bf16[1024,128]{1,0:T(8,128)(2,1)}) custom-call(s32[5]{0:T(128)} %shear.5, s32[1]{0:T(128)} %bitcast.2.base, f32[5,128]{1,0:T(8,128)} %pad_maximum_fusion.4.beta, ...), custom_call_target="tpu_custom_call" | custom-call | flops 754974720 | bytes 4000000 | tf_op jit(solution)/shard_map/pallas_call | solution.py:353
  29.2 7.4 %all-to-all-start = ((bf16[8,8,16,128]{3,2,1,0:T(8,128)(2,1)}), bf16[8,8,16,128]{3,2,1,0:T(8,128)(2,1)S(1)}, u32[]{:S(2)}, u32[]{:S(2)}) async-start(bf16[8,8,16,128]{3,2,1,0:T(8,128)(2,1)} %get-tuple-element.16), calls=%async_computation | async-start | bytes 524288 | tf_op jit(solution)/shard_map/all_to_all | solution.py:396
  36.6 1.4 pad_maximum_fusion.3.beta
  38.0 6.2 %all-to-all-done.h_ref = bf16[8,8,16,128]{3,2,1,0:T(8,128)(2,1)S(1)} async-done(((bf16[8,8,16,128]{3,2,1,0:T(8,128)(2,1)}), bf16[8,8,16,128]{3,2,1,0:T(8,128)(2,1)S(1)}, u32[]{:S(2)}, u32[]{:S(2)}) %all-to-all-start) | async-done | bytes 262176 | tf_op jit(solution)/shard_map/all_to_all | solution.py:396
  44.2 0.0 copy-start.1
  44.2 0.7 copy-done.1
  44.9 21.9 %shard_map.119 = (bf16[2,8,8192]{2,1,0:T(8,128)(2,1)}, bf16[8,8,16,128]{3,2,1,0:T(8,128)(2,1)}, f32[320,128]{1,0:T(8,128)}) custom-call(s32[5]{0:T(128)} %shear.5, f32[5,128]{1,0:T(8,128)} %pad_maximum_fusion.3.beta, bf16[9,64,64]{2,1,0:T(8,128)(2,1)} %bitcast.40, bf16[8,8,16,128]{3,2,1,0:T(8,128)(2,1)} %copy-done.1, bf16[2,8,8192]{2,1,0:T(8,128)(2,1)} %cot.1), custom_call_target="tpu_custom_call" | custom-call | flops 905969664 | bytes 4000000 | tf_op jit(solution)/shard_map/pallas_call | solution.py:353
  66.9 0.0 copy-start.2
  66.9 11.1 %all_to_all.30.gm = bf16[8,8,16,128]{3,2,1,0:T(8,128)(2,1)S(1)} all-to-all(bf16[8,8,16,128]{3,2,1,0:T(8,128)(2,1)} %get-tuple-element.22), channel_id=1, replica_groups=mesh['vrow'=8,'img'=16] {'vrow'}, dimensions={0} | all-to-all | bytes 524288 | tf_op jit(solution)/shard_map/all_to_all | solution.py:416
  77.9 0.0 copy-start
  78.0 1.9 %collective-permute-start.3 = (bf16[8,3,16,128]{3,2,1,0:T(8,128)(2,1)S(1)}, bf16[8,3,16,128]{3,2,1,0:T(8,128)(2,1)S(1)}, u32[]{:S(2)}, u32[]{:S(2)}) collective-permute-start(bf16[8,3,16,128]{3,2,1,0:T(8,128)(2,1)S(1)} %get-tuple-element.32), channel_id=1, source_target_pairs={{1,0},{2,1},{3,2},{4,3},{5,4},{6,5},{7,6},{8,7},{9,8},{10,9},{11,1... | collective-permute-start | bytes 294920 | tf_op jit(solution)/shard_map/ppermute | solution.py:417
  79.9 6.3 %collective-permute-start.2 = (bf16[8,3,16,128]{3,2,1,0:T(8,128)(2,1)S(1)}, bf16[8,3,16,128]{3,2,1,0:T(8,128)(2,1)S(1)}, u32[]{:S(2)}, u32[]{:S(2)}) collective-permute-start(bf16[8,3,16,128]{3,2,1,0:T(8,128)(2,1)S(1)} %get-tuple-element.33), channel_id=1, source_target_pairs={{0,1},{1,2},{2,3},{3,4},{4,5},{5,6},{6,7},{7,8},{8,9},{9,10},{10,1... | collective-permute-start | bytes 294920 | tf_op jit(solution)/shard_map/ppermute | solution.py:418
  86.1 0.4 collective-permute-done.3.gr
  86.5 0.0 copy-start.3
  86.5 1.3 collective-permute-done.2.gl
  87.8 0.0 copy-start.4
  87.8 0.0 copy-done
  87.8 0.0 copy-done.3
  87.8 0.6 copy-done.4
  88.4 14.9 %shard_map.120 = (bf16[16,8,1024]{2,1,0:T(8,128)(2,1)}, f32[320,128]{1,0:T(8,128)}) custom-call(s32[5]{0:T(128)} %shear.5, s32[1]{0:T(128)} %bitcast.2.base, f32[5,128]{1,0:T(8,128)} %pad_maximum_fusion.4.beta, bf16[9,64,64]{2,1,0:T(8,128)(2,1)} %bitcast.35, f32[5,14,8,16,128]{4,3,2,1,0:T(8,128)} %get-tuple-element.18.pre_ref, ...), custom_call_target="tpu_custom_call" | custom-call | flops 603979776 | bytes 4000000 | tf_op jit(solution)/shard_map/pallas_call | solution.py:353
  103.3 0.0 copy-done.2
  103.3 0.9 pad_maximum_fusion
  104.2 14.9 %all_to_all.31 = f32[16,40,128]{2,1,0:T(8,128)S(1)} all-to-all(f32[16,40,128]{2,1,0:T(8,128)S(1)} %bitcast.25), channel_id=1, replica_groups=mesh['vrow'=8,'img'=16] {'img'}, dimensions={0} | all-to-all | bytes 655360 | tf_op jit(solution)/shard_map/all_to_all | solution.py:365
  119.2 9.0 %all_to_all.32 = f32[8,5,128]{2,1,0:T(8,128)S(1)} all-to-all(f32[8,5,128]{2,1,0:T(8,128)S(1)} %reshape.56), channel_id=1, replica_groups=mesh['vrow'=8,'img'=16] {'vrow'}, dimensions={0} | all-to-all | bytes 40960 | tf_op jit(solution)/shard_map/all_to_all | solution.py:366
  128.2 9.0 %all_to_all.33 = f32[8,5,128]{2,1,0:T(8,128)S(1)} all-to-all(f32[8,5,128]{2,1,0:T(8,128)S(1)} %broadcast_in_dim.6), channel_id=1, replica_groups=mesh['vrow'=8,'img'=16] {'vrow'}, dimensions={0} | all-to-all | bytes 40960 | tf_op jit(solution)/shard_map/all_to_all | solution.py:367
  137.2 13.3 %all_to_all.34 = f32[16,40,128]{2,1,0:T(8,128)S(1)} all-to-all(f32[16,40,128]{2,1,0:T(8,128)S(1)} %broadcast_in_dim.15), channel_id=1, replica_groups=mesh['vrow'=8,'img'=16] {'img'}, dimensions={0} | all-to-all | bytes 655360 | tf_op jit(solution)/shard_map/all_to_all | solution.py:368
  150.6 0.7 fusion
  151.2 0.2 fusion.1
  151.4 0.7 slice.55
  152.2 0.7 slice.52
  (10 shorter events, 0.2 us)
Async XLA Ops:
  0.6 8.8 %collective-permute-start.1 = (bf16[16,8,1024]{2,1,0:T(8,128)(2,1)}, bf16[16,8,1024]{2,1,0:T(8,128)(2,1)S(1)}, u32[]{:S(2)}, u32[]{:S(2)}) collective-permute-start(bf16[16,8,1024]{2,1,0:T(8,128)(2,1)} %bitcast.36), channel_id=1, source_target_pairs={{1,0},{2,1},{3,2},{4,3},{5,4},{6,5},{7,6},{8,7},{9,8},{10,9},{11,1... | collective-permute-start | bytes 786440 | tf_op jit(solution)/shard_map/ppermute | solution.py:379
  3.9 8.6 %collective-permute-start = (bf16[16,8,1024]{2,1,0:T(8,128)(2,1)}, bf16[16,8,1024]{2,1,0:T(8,128)(2,1)S(1)}, u32[]{:S(2)}, u32[]{:S(2)}) collective-permute-start(bf16[16,8,1024]{2,1,0:T(8,128)(2,1)} %bitcast.37), channel_id=1, source_target_pairs={{0,1},{1,2},{2,3},{3,4},{4,5},{5,6},{6,7},{7,8},{8,9},{9,10},{10,1... | collective-permute-start | bytes 786440 | tf_op jit(solution)/shard_map/ppermute | solution.py:378
  9.5 3.1 %copy-start.5 = (bf16[16,8,1024]{2,1,0:T(8,128)(2,1)}, bf16[16,8,1024]{2,1,0:T(8,128)(2,1)S(1)}, u32[]{:S(2)}) copy-start(bf16[16,8,1024]{2,1,0:T(8,128)(2,1)S(1)} %collective-permute-done.1.fr) | copy-start | bytes 786436
  12.6 0.7 copy-start.6
  29.2 15.0 %all-to-all-start = ((bf16[8,8,16,128]{3,2,1,0:T(8,128)(2,1)}), bf16[8,8,16,128]{3,2,1,0:T(8,128)(2,1)S(1)}, u32[]{:S(2)}, u32[]{:S(2)}) async-start(bf16[8,8,16,128]{3,2,1,0:T(8,128)(2,1)} %get-tuple-element.16), calls=%async_computation | async-start | bytes 524288 | tf_op jit(solution)/shard_map/all_to_all | solution.py:396
  44.2 0.7 copy-start.1
  66.9 36.4 %copy-start.2 = (f32[320,128]{1,0:T(8,128)S(1)}, f32[320,128]{1,0:T(8,128)}, u32[]{:S(2)}) copy-start(f32[320,128]{1,0:T(8,128)} %get-tuple-element.25) | copy-start | bytes 491524
  77.9 9.8 %copy-start = (bf16[8,8,16,128]{3,2,1,0:T(8,128)(2,1)}, bf16[8,8,16,128]{3,2,1,0:T(8,128)(2,1)S(1)}, u32[]{:S(2)}) copy-start(bf16[8,8,16,128]{3,2,1,0:T(8,128)(2,1)S(1)} %all_to_all.30.gm) | copy-start | bytes 786436
  78.0 8.5 %collective-permute-start.3 = (bf16[8,3,16,128]{3,2,1,0:T(8,128)(2,1)S(1)}, bf16[8,3,16,128]{3,2,1,0:T(8,128)(2,1)S(1)}, u32[]{:S(2)}, u32[]{:S(2)}) collective-permute-start(bf16[8,3,16,128]{3,2,1,0:T(8,128)(2,1)S(1)} %get-tuple-element.32), channel_id=1, source_target_pairs={{1,0},{2,1},{3,2},{4,3},{5,4},{6,5},{7,6},{8,7},{9,8},{10,9},{11,1... | collective-permute-start | bytes 294920 | tf_op jit(solution)/shard_map/ppermute | solution.py:417
  79.9 7.9 %collective-permute-start.2 = (bf16[8,3,16,128]{3,2,1,0:T(8,128)(2,1)S(1)}, bf16[8,3,16,128]{3,2,1,0:T(8,128)(2,1)S(1)}, u32[]{:S(2)}, u32[]{:S(2)}) collective-permute-start(bf16[8,3,16,128]{3,2,1,0:T(8,128)(2,1)S(1)} %get-tuple-element.33), channel_id=1, source_target_pairs={{0,1},{1,2},{2,3},{3,4},{4,5},{5,6},{6,7},{7,8},{8,9},{9,10},{10,1... | collective-permute-start | bytes 294920 | tf_op jit(solution)/shard_map/ppermute | solution.py:418
  86.5 1.3 copy-start.3
  87.8 0.6 copy-start.4

commit v2 on v1

v2 whole, which is shorter than its diff:
```python
import jax
import jax.numpy as jnp
from jax import lax
from jax.experimental import pallas as pl
from jax.experimental.pallas import tpu as pltpu
from jax.sharding import PartitionSpec as P

BF = jnp.bfloat16
F32 = jnp.float32
LANES = 128
HALF = 64
TAPS = 9
REACH = 3
VMEM_BYTES = 36 * 1024 * 1024
NT = (((1,), (1,)), ((), ()))
NN = (((1,), (0,)), ((), ()))
TN = (((0,), (0,)), ((), ()))


def mm(lhs, rhs, dims):
    return lax.dot_general(lhs, rhs, dims, preferred_element_type=F32)


def lanes_of(shape):
    return lax.broadcasted_iota(jnp.int32, shape, len(shape) - 1)


def swap(value):
    return pltpu.roll(value, HALF, axis=value.ndim - 1)


def low(shape):
    return lanes_of(shape) < HALF


def fill_weights(w_ref, wt_ref):
    zero = jnp.zeros((HALF, HALF), BF)
    for tap in range(TAPS):
        w = w_ref[tap]
        wt_ref[pl.ds(tap * LANES, HALF), :] = jnp.concatenate([w, zero], axis=1)
        wt_ref[pl.ds(tap * LANES + HALF, HALF), :] = jnp.concatenate([zero, w], axis=1)


def spread(beta_ref, beta):
    for k in range(beta.shape[0]):
        line = beta_ref[pl.ds(k, 1), :]
        beta[k] = jnp.broadcast_to(jnp.concatenate([line, line], axis=1), (8, LANES))


def pack_grads(grads, blend_ref, pay_ref):
    first = low((HALF, LANES))
    rows = lax.broadcasted_iota(jnp.int32, (HALF, LANES), 0)
    blend = jnp.zeros((HALF, LANES), F32)
    for k in range(blend_ref.shape[0]):
        line = jnp.sum(blend_ref[k], axis=0, keepdims=True)
        blend = blend + jnp.where(rows == k, line + swap(line), 0.0)

    def tap_of(tap):
        block = grads[tap // 3][:, (tap % 3) * LANES : (tap % 3 + 1) * LANES]
        return block[:HALF] + swap(block[HALF:])

    for pair in range(5):
        even = tap_of(2 * pair)
        odd = tap_of(2 * pair + 1) if pair < 4 else even
        both = jnp.transpose(jnp.where(first, even, swap(odd)))
        value = jnp.concatenate([both[:HALF], both[HALF:]], axis=1)
        if pair == 4:
            value = jnp.where(first, value, blend)
        pay_ref[pl.ds(pair * HALF, HALF), :] = value


def gate(pre):
    s = 0.5 * jnp.tanh(0.5 * pre) + 0.5
    act = pre * s
    return act, s + act * (1.0 - s)


def halves():
    return (lanes_of((1, 8, LANES)) >= HALF).astype(jnp.int32)


def h_forward(shear, base, beta_ref, w_ref, fl, fm, fr, hfeat, pre_ref, f0_out, fm_out, fp_out, beta, stage, f0, fmi, fpl, taps, wt):
    shears = shear.shape[0]
    spread(beta_ref, beta)
    fill_weights(w_ref, wt)
    first16 = low((16, LANES))

    @pl.loop(0, 16)
    def _(y):
        for part, ref in enumerate((fl, fm, fr)):
            for q in range(8):
                stage[q, pl.ds(y * 24 + 8 * part, 8), :] = ref[y, :, pl.ds(q * LANES, LANES)].astype(F32)

    @pl.loop(0, 20)
    def _(x):
        own = [stage[q, pl.ds(x + 2, 16, stride=24), :] for q in range(8)]
        turned = [swap(a) for a in own]
        zero = jnp.zeros((16, LANES), F32)
        moved = [
            jnp.where(first16, turned[q - 1] if q > 0 else zero, turned[q] if q < 8 else zero).astype(BF)
            for q in range(9)
        ]
        for q in range(8):
            at = pl.ds(pl.multiple_of(x * LANES + q * 16, 16), 16)
            f0[at, :] = own[q].astype(BF)
            fmi[at, :] = moved[q]
            fpl[at, :] = moved[q + 1]

    @pl.loop(0, 5)
    def _(n):
        at = pl.ds(pl.multiple_of(n * 512, 512), 512)
        for side, ref in enumerate((fmi, f0, fpl)):
            product = mm(ref[at, :], wt[pl.ds(side * 384, 384), :], NT)
            for j in range(3):
                part = product[:, j * LANES : (j + 1) * LANES].reshape(32, 2, 8, LANES)
                taps[pl.ds((3 * side + j) * 160 + n * 32, 32)] = part

    f0_out[...] = f0[pl.ds(6 * LANES, 1024), :]
    fm_out[...] = fmi[pl.ds(6 * LANES, 1024), :]
    fp_out[...] = fpl[pl.ds(6 * LANES, 1024), :]

    half = halves()

    def body(xe, q, local):
        here = (xe + 3) * 8 + q
        vrel = half + (2 * q - 8)
        xg = base[0] + xe - REACH
        mid = taps[4 * 160 + here]
        left = taps[3 * 160 - 8 + here]
        right = taps[5 * 160 + 8 + here]
        branch = jnp.zeros((2, 8, LANES), F32)
        for k in range(shears):
            d = shear[k]
            xs = xg - d * vrel
            a, b = here - d * 8, here + d * 8
            main = mid + (taps[160 + a] + taps[7 * 160 + b])
            minus = left + (taps[a - 8] + taps[6 * 160 - 8 + b])
            plus = right + (taps[2 * 160 + 8 + a] + taps[8 * 160 + 8 + b])
            pre = main + jnp.where(xs >= 1, minus, 0.0) + jnp.where(xs <= LANES - 2, plus, 0.0)
            pre_ref[k * 112 + xe * 8 + q] = pre
            if local:
                keep = (xs >= 0) & (xs < LANES)
                branch = branch + jnp.where(keep, beta[k] * gate(pre)[0], 0.0)
        if local:
            own = f0[pl.ds(pl.multiple_of(here * 16, 16), 16), :].astype(F32)
            hfeat[q, xe - REACH] = (own + branch.reshape(16, LANES)).astype(BF)

    @pl.loop(0, 64)
    def _(n):
        body(n // 8 + REACH, n % 8, True)

    @pl.loop(0, 24)
    def _(n):
        body(n // 8, n % 8, False)
        body(n // 8 + 8 + REACH, n % 8, False)


def h_backward(shear, base, beta_ref, w_ref, pre_ref, f0, fmi, fpl, gm, gl, gr, pay_v, out, pay, beta, dps, sums, edges, dfs, stage, blend, wt):
    shears = shear.shape[0]
    step = shears * 112
    spread(beta_ref, beta)
    fill_weights(w_ref, wt)
    half = halves()
    blend[...] = jnp.zeros(blend.shape, F32)

    def body(xe, q, g, local):
        here = xe * 8 + q
        g = g.astype(F32).reshape(2, 8, LANES)
        vrel = half + (2 * q - 8)
        xg = base[0] + xe - REACH
        total = [jnp.zeros((2, 8, LANES), F32) for _ in range(3)]
        for k in range(shears):
            xs = xg - shear[k] * vrel
            act, slope = gate(pre_ref[k * 112 + here])
            gk = jnp.where((xs >= 0) & (xs < LANES), g, 0.0)
            dp = (beta[k] * gk * slope).astype(BF).astype(F32)
            parts = (jnp.where(xs >= 1, dp, 0.0), dp, jnp.where(xs <= LANES - 2, dp, 0.0))
            for j in range(3):
                dps[j * step + k * 112 + here] = parts[j]
                total[j] = total[j] + parts[j]
            if local:
                blend[k] += jnp.sum(gk * act, axis=0)
        for j in range(3):
            sums[j * 112 + here] = total[j]

    @pl.loop(0, 64)
    def _(n):
        x, q = n // 8, n % 8
        body(x + REACH, q, gm[q, x], True)

    @pl.loop(0, 24)
    def _(n):
        x, q = n // 8, n % 8
        body(x, q, gl[q, x], False)
        body(x + 8 + REACH, q, gr[q, x], False)

    @pl.loop(0, 64)
    def _(n):
        here = n + REACH * 8
        at = pl.ds(pl.multiple_of(n * 16, 16), 16)
        below = [jnp.zeros((2, 8, LANES), F32) for _ in range(3)]
        above = [jnp.zeros((2, 8, LANES), F32) for _ in range(3)]
        for k in range(shears):
            d = shear[k]
            up, down = here + d * 8, here - d * 8
            for j in range(3):
                below[j] = below[j] + dps[j * step + k * 112 - (j - 1) * 8 + up]
                above[j] = above[j] + dps[j * step + k * 112 - (j - 1) * 8 + down]
        for j in range(3):
            lanes = pl.ds(j * LANES, LANES)
            edges[0, at, lanes] = below[j].reshape(16, LANES).astype(BF)
            edges[1, at, lanes] = sums[j * 112 - (j - 1) * 8 + here].reshape(16, LANES).astype(BF)
            edges[2, at, lanes] = above[j].reshape(16, LANES).astype(BF)

    pack_grads([mm(ref[...], edges[side], TN) for side, ref in enumerate((fmi, f0, fpl))], blend, pay)
    pay[pl.ds(5 * HALF, 5 * HALF), :] = pay_v[...]

    @pl.loop(0, 4)
    def _(x):
        at = pl.ds(pl.multiple_of(x * 256, 256), 256)
        for side in range(3):
            dfs[side, at, :] = mm(edges[side, at, :], wt[pl.ds(side * 384, 384), :], NN)

    first16 = low((16, LANES))

    @pl.loop(0, 8)
    def _(x):
        def piece(side, q):
            if q < 0 or q > 7:
                return jnp.zeros((16, LANES), F32)
            return dfs[side, pl.ds(pl.multiple_of(x * LANES + q * 16, 16), 16), :]

        for q in range(8):
            upper = piece(0, q) + piece(2, q - 1)
            lower = piece(0, q + 1) + piece(2, q)
            turned = swap(jnp.where(first16, lower, upper))
            total = gm[q, x].astype(F32) + piece(1, q) + turned
            stage[q, pl.ds(x * 16, 16), :] = total

    @pl.loop(0, 16)
    def _(y):
        for q in range(8):
            out[y, :, pl.ds(q * LANES, LANES)] = stage[q, pl.ds(y, 8, stride=16), :].astype(BF)


def v_both(shear, beta_ref, w_ref, h_ref, cot, out, dvert, pay, beta, own, fv, taps, dps, sums, grads, outs, edges, blend, wt):
    shears = shear.shape[0]
    wide = 22
    plane = 10 * wide
    spread(beta_ref, beta)
    fill_weights(w_ref, wt)
    blend[...] = jnp.zeros(blend.shape, F32)
    first8 = low((8, LANES))

    for u in (0, 9):
        sheet = jnp.zeros((wide, 8, LANES), F32)
        for tap in (0, 1, 2) if u == 0 else (6, 7, 8):
            taps[pl.ds(tap * plane + u * wide, wide)] = sheet
        for jk in range(3 * shears):
            dps[pl.ds(jk * plane + u * wide, wide)] = sheet

    @pl.loop(1, 9)
    def _(u):
        rim = jnp.zeros((REACH, 8, LANES), F32)
        for side in (0, 16 + REACH):
            for tap in range(TAPS):
                taps[pl.ds(tap * plane + side + u * wide, REACH)] = rim
            for j in range(3):
                sums[pl.ds(j * plane + side + u * wide, REACH)] = rim
            for jk in range(3 * shears):
                dps[pl.ds(jk * plane + side + u * wide, REACH)] = rim

    @pl.loop(0, 8)
    def _(u):
        for x in range(8):
            own[u, pl.ds(x * 16, 16), :] = h_ref[u, x].astype(F32)
        for y in range(0, 16, 2):
            pair = [own[u, pl.ds(y + e, 8, stride=16), :] for e in range(2)]
            fv[pl.ds(pl.multiple_of(u * LANES + y * 8, 16), 16), :] = jnp.concatenate(pair, axis=0).astype(BF)
        for q in range(8):
            lanes = pl.ds(pl.multiple_of((u * 8 + q) * LANES, LANES), LANES)
            a, b = cot[0, :, lanes].astype(F32), cot[1, :, lanes].astype(F32)
            grads[u, 2 * q] = jnp.where(first8, a, swap(b))
            grads[u, 2 * q + 1] = jnp.where(first8, swap(a), b)

    @pl.loop(0, 2)
    def _(n):
        rows = pl.ds(pl.multiple_of(n * 512, 512), 512)
        for side in range(3):
            product = mm(fv[rows, :], wt[pl.ds(side * 384, 384), :], NT)
            for j in range(3):
                part = product[:, j * LANES : (j + 1) * LANES].reshape(4, 16, 8, LANES)
                for e in range(4):
                    taps[pl.ds((3 * side + j) * plane + (e + 1) * wide + REACH + n * 4 * wide, 16)] = part[e]

    def body(u, y):
        here = (u + 1) * wide + REACH + y
        g = grads[u, y]
        mid = taps[4 * plane + here]
        left = taps[3 * plane - 1 + here]
        right = taps[5 * plane + 1 + here]
        branch = jnp.zeros((8, LANES), F32)
        total = [jnp.zeros((8, LANES), F32) for _ in range(3)]
        shared = []
        for k in range(shears):
            d = shear[k]
            ys = y - d * (u - 4)
            keep = ((ys >= 0) & (ys < 16)).astype(F32)
            has_minus = (ys >= 1).astype(F32)
            has_plus = (ys <= 14).astype(F32)
            a, b = here - d, here + d
            main = mid + (taps[plane - wide + a] + taps[7 * plane + wide + b])
            minus = left + (taps[-wide - 1 + a] + taps[6 * plane + wide - 1 + b])
            plus = right + (taps[2 * plane - wide + 1 + a] + taps[8 * plane + wide + 1 + b])
            act, slope = gate(main + has_minus * minus + has_plus * plus)
            act = keep * act
            bk = beta[k]
            branch = branch + bk * act
            shared.append(g * act)
            dp = (bk * (keep * g) * slope).astype(BF).astype(F32)
            parts = (has_minus * dp, dp, has_plus * dp)
            for j in range(3):
                dps[(j * shears + k) * plane + here] = parts[j]
                total[j] = total[j] + parts[j]
        for j in range(3):
            sums[j * plane + here] = total[j]
        outs[u, y] = own[u, pl.ds(y, 8, stride=16), :] + branch
        return shared

    @pl.loop(0, 64)
    def _(n):
        u, y = n // 8, (n % 8) * 2
        first, second = body(u, y), body(u, y + 1)
        for k in range(shears):
            blend[k] += first[k] + second[k]

    @pl.loop(0, 64)
    def _(n):
        here = (n // 8 + 1) * wide + REACH + (n % 8) * 2
        at = pl.ds(pl.multiple_of(n * 16, 16), 16)
        below = [jnp.zeros((2, 8, LANES), F32) for _ in range(3)]
        above = [jnp.zeros((2, 8, LANES), F32) for _ in range(3)]
        for k in range(shears):
            d = shear[k]
            up, down = here + d, here - d
            for j in range(3):
                offset = (j * shears + k) * plane - (j - 1)
                below[j] = below[j] + dps[pl.ds(offset + wide + up, 2)]
                above[j] = above[j] + dps[pl.ds(offset - wide + down, 2)]
        for j in range(3):
            middle = sums[pl.ds(j * plane - (j - 1) + here, 2)]
            for side, value in enumerate((below[j], middle, above[j])):
                edges[at, pl.ds((3 * side + j) * LANES, LANES)] = value.reshape(16, LANES).astype(BF)

    pack_grads([mm(fv[...], edges[:, pl.ds(side * 384, 384)], TN) for side in range(3)], blend, pay)

    @pl.loop(0, 4)
    def _(n):
        rows = pl.ds(pl.multiple_of(n * 256, 256), 256)
        back = mm(edges[rows, :], wt[...], NN).reshape(2, LANES, LANES)
        for e in range(2):
            u = 2 * n + e
            own[u] = grads[u].reshape(LANES, LANES) + back[e]
            for x in range(8):
                dvert[u, x] = own[u, pl.ds(x, 16, stride=8), :].astype(BF)
            for q in range(8):
                lanes = pl.ds(pl.multiple_of((u * 8 + q) * LANES, LANES), LANES)
                a, b = outs[u, 2 * q], outs[u, 2 * q + 1]
                out[0, :, lanes] = jnp.where(first8, a, swap(b)).astype(BF)
                out[1, :, lanes] = jnp.where(first8, swap(a), b).astype(BF)


def call(body, operands, out_shapes, scratch, smem, cost):
    vmem = pl.BlockSpec(memory_space=pltpu.VMEM)
    specs = [pl.BlockSpec(memory_space=pltpu.SMEM)] * smem + [vmem] * (len(operands) - smem)
    return pl.pallas_call(
        body,
        out_shape=out_shapes,
        in_specs=specs,
        out_specs=[vmem] * len(out_shapes),
        scratch_shapes=scratch,
        compiler_params=pltpu.CompilerParams(vmem_limit_bytes=VMEM_BYTES),
        cost_estimate=pl.CostEstimate(flops=cost, bytes_accessed=4_000_000, transcendentals=1_000_000),
    )(*operands)


def reduce_all(pay):
    part = lax.all_to_all(pay.reshape(16, 40, LANES), "img", 0, 0, tiled=True).sum(0)
    part = lax.all_to_all(jnp.broadcast_to(part[None], (8, 40, LANES)), "vrow", 0, 0, tiled=True).sum(0)
    return lax.all_to_all(jnp.broadcast_to(part[None], (16, 40, LANES)), "img", 0, 0, tiled=True).reshape(640, LANES)


def per_device(features, weight_h, weight_v, beta_h, beta_v, shear_set, cotangent):
    shears = shear_set.shape[0]
    img = lax.axis_size("img")
    sds = jax.ShapeDtypeStruct
    own = features.reshape(16, 8, 1024)
    to_right = [(i, i + 1) for i in range(img - 1)]
    to_left = [(i + 1, i) for i in range(img - 1)]
    from_left = lax.ppermute(own, "img", to_right)
    from_right = lax.ppermute(own, "img", to_left)
    base = (lax.axis_index("img") * 8).astype(jnp.int32).reshape(1)
    w_h = jnp.transpose(weight_h, (2, 3, 0, 1)).reshape(TAPS, HALF, HALF)
    w_v = jnp.transpose(weight_v, (2, 3, 0, 1)).reshape(TAPS, HALF, HALF)

    hfeat, pre, f0, fmi, fpl = call(
        h_forward,
        (shear_set, base, beta_h, w_h, from_left, own, from_right),
        [sds((8, 8, 16, LANES), BF), sds((shears * 112, 2, 8, LANES), F32)] + [sds((1024, LANES), BF)] * 3,
        [pltpu.VMEM((shears, 8, LANES), F32), pltpu.VMEM((8, 384, LANES), F32)]
        + [pltpu.VMEM((20 * LANES, LANES), BF)] * 3
        + [pltpu.VMEM((TAPS * 160, 2, 8, LANES), F32), pltpu.VMEM((TAPS * LANES, LANES), BF)],
        2,
        2 * 2560 * LANES * TAPS * LANES,
    )
    moved = lax.all_to_all(hfeat, "vrow", 0, 0, tiled=True)
    output, dvert, pay_v = call(
        v_both,
        (shear_set, beta_v, w_v, moved, cotangent),
        [sds((2, 8, 8192), BF), sds((8, 8, 16, LANES), BF), sds((320, LANES), F32)],
        [
            pltpu.VMEM((shears, 8, LANES), F32),
            pltpu.VMEM((8, LANES, LANES), F32),
            pltpu.VMEM((1024, LANES), BF),
            pltpu.VMEM((TAPS * 220, 8, LANES), F32),
            pltpu.VMEM((3 * shears * 220, 8, LANES), F32),
            pltpu.VMEM((3 * 220, 8, LANES), F32),
            pltpu.VMEM((8, 16, 8, LANES), F32),
            pltpu.VMEM((8, 16, 8, LANES), F32),
            pltpu.VMEM((1024, TAPS * LANES), BF),
            pltpu.VMEM((shears, 8, LANES), F32),
            pltpu.VMEM((TAPS * LANES, LANES), BF),
        ],
        1,
        6 * 1024 * LANES * TAPS * LANES,
    )
    grad = lax.all_to_all(dvert, "vrow", 0, 0, tiled=True)
    grad_right = lax.ppermute(grad[:, :REACH], "img", to_left)
    grad_left = lax.ppermute(grad[:, 8 - REACH :], "img", to_right)
    grad_features, pay = call(
        h_backward,
        (shear_set, base, beta_h, w_h, pre, f0, fmi, fpl, grad, grad_left, grad_right, pay_v),
        [sds((16, 8, 1024), BF), sds((640, LANES), F32)],
        [
            pltpu.VMEM((shears, 8, LANES), F32),
            pltpu.VMEM((3 * shears * 112, 2, 8, LANES), F32),
            pltpu.VMEM((3 * 112, 2, 8, LANES), F32),
            pltpu.VMEM((3, 1024, 384), BF),
            pltpu.VMEM((3, 1024, LANES), F32),
            pltpu.VMEM((8, LANES, LANES), F32),
            pltpu.VMEM((shears, 8, LANES), F32),
            pltpu.VMEM((TAPS * LANES, LANES), BF),
        ],
        2,
        4 * 1024 * LANES * TAPS * LANES,
    )
    total = reduce_all(pay) * (262144.0**-0.5)

    def unpack(block):
        pairs = jnp.stack([block[:, :HALF].reshape(5, HALF, HALF), block[:, HALF:].reshape(5, HALF, HALF)], axis=1)
        weight = jnp.transpose(pairs.reshape(10, HALF, HALF)[:TAPS].reshape(3, 3, HALF, HALF), (2, 3, 0, 1))
        return weight, block[4 * HALF : 4 * HALF + shears, HALF:]

    weight_grad_h, beta_grad_h = unpack(total[:320])
    weight_grad_v, beta_grad_v = unpack(total[320:])
    return (
        output,
        grad_features.reshape(features.shape),
        weight_grad_h,
        weight_grad_v,
        beta_grad_h,
        beta_grad_v,
    )


def solution(mesh):
    placed = (P("vrow", None, "img", None), P(), P(), P(), P(), P(), P("vrow", "img", None))
    return jax.shard_map(
        per_device,
        mesh=mesh,
        in_specs=placed,
        out_specs=(P("vrow", "img", None), P("vrow", None, "img", None), P(), P(), P(), P()),
        check_vma=False,
    )
```

time: 154 us -> 127 us (0.82)
  Pallas kernels: 52.7 us -> 33.9 us
  starting transfers between devices: 22.1 us -> 14.8 us
  waiting for transfers between devices: 11.8 us -> 7.02 us
  blocking collectives: 57.3 us -> 61.6 us
  other arithmetic: 3.91 us -> 0.11 us
  local copies, waits for them, and re-layouts: 4.4 us -> 8.1 us
    pallas_call x3, Pallas kernels: 52.7 us -> 33.9 us  [call(): pl.pallas_call(body, out_shape=out_shapes, in_specs=specs, out_specs=[vme...]
    all_to_all x1 -> x0, starting transfers between devices: 7.38 us -> none  [per_device(): moved = lax.all_to_all(hfeat, 'vrow', 0, 0, tiled=True)]
    all_to_all x2, blocking collectives: 18 us -> 24.4 us  [the longest x1 14.8 us: per_device(): moved = lax.all_to_all(hfeat, 'vrow', 0, 0, tiled=True)]
    all_to_all x1 -> x0, waiting for transfers between devices: 6.21 us -> none  [per_device(): moved = lax.all_to_all(hfeat, 'vrow', 0, 0, tiled=True)]
    concatenate x3 -> x0, other arithmetic: 3.79 us -> none  [the longest x1 1.43 us: per_device(): wide_h = jnp.concatenate([beta_h, beta_h], axis=1)]
    unnamed x14 -> x18, local copies, waits for them, and re-layouts: 2.05 us -> 5.75 us
  transfers between devices with their start and end apart: 5 -> 4, of which waited for: 5 -> 4; matrix products, arithmetic and copies ran while one was open for 2% -> 0% of each run, Pallas kernels for 0% -> 0%
where the time goes in v2:
time: 127 us; the launch traced here: 126 us
  blocking collectives  61.6 us (49%)
  Pallas kernels  33.9 us (27%)
  starting transfers between devices  14.8 us (12%)
  local copies, waits for them, and re-layouts  8.1 us (6%)
  waiting for transfers between devices  7.02 us (6%)
    pallas_call x3, Pallas kernels, call(): pl.pallas_call(body, out_shape=out_shapes, in_specs=specs, out_specs=[vme...  33.9 us
    all_to_all x1, blocking collectives, reduce_all(): lax.all_to_all(pay.reshape(16, 40, LANES), 'img', 0, 0, tiled=True).sum(0)  14.9 us
    all_to_all x1, blocking collectives, per_device(): moved = lax.all_to_all(hfeat, 'vrow', 0, 0, tiled=True)  14.8 us
    all_to_all x1, blocking collectives, reduce_all(): lax.all_to_all(jnp.broadcast_to(part[None], (16, 40, LANES)), 'img', 0, 0...  12.2 us
    all_to_all x1, blocking collectives, per_device(): grad = lax.all_to_all(dvert, 'vrow', 0, 0, tiled=True)  10 us
    all_to_all x1, blocking collectives, reduce_all(): lax.all_to_all(jnp.broadcast_to(part[None], (8, 40, LANES)), 'vrow', 0, 0...  9.58 us
    ppermute x1, starting transfers between devices, per_device(): grad_left = lax.ppermute(grad[:, 8 - REACH:], 'img', to_right)  6.37 us
    unnamed x18, local copies, waits for them, and re-layouts  5.75 us
  transfers between devices with their start and end apart: 4, of which 4 were waited for; matrix products, arithmetic and copies ran while one was open for 0% of the time, Pallas kernels for 0%

profile of v2, /device:TPU:1, one launch (start us, length us, event | category | flops | bytes accessed | tf_op | source)
XLA Modules:
  0.0 126.3 jit_solution(15829524586480281613)
XLA Ops:
  0.6 0.0 copy-start.3
  0.6 3.3 %collective-permute-start.1 = (bf16[16,8,1024]{2,1,0:T(8,128)(2,1)}, bf16[16,8,1024]{2,1,0:T(8,128)(2,1)S(1)}, u32[]{:S(2)}, u32[]{:S(2)}) collective-permute-start(bf16[16,8,1024]{2,1,0:T(8,128)(2,1)} %bitcast.26), channel_id=1, source_target_pairs={{1,0},{2,1},{3,2},{4,3},{5,4},{6,5},{7,6},{8,7},{9,8},{10,9},{11,1... | collective-permute-start | bytes 786440 | tf_op jit(solution)/shard_map/ppermute | solution.py:401
  3.9 3.2 %collective-permute-start = (bf16[16,8,1024]{2,1,0:T(8,128)(2,1)}, bf16[16,8,1024]{2,1,0:T(8,128)(2,1)S(1)}, u32[]{:S(2)}, u32[]{:S(2)}) collective-permute-start(bf16[16,8,1024]{2,1,0:T(8,128)(2,1)} %bitcast.27), channel_id=1, source_target_pairs={{0,1},{1,2},{2,3},{3,4},{4,5},{5,6},{6,7},{7,8},{8,9},{9,10},{10,1... | collective-permute-start | bytes 786440 | tf_op jit(solution)/shard_map/ppermute | solution.py:400
  7.2 2.3 %collective-permute-done.1.fr = bf16[16,8,1024]{2,1,0:T(8,128)(2,1)S(1)} collective-permute-done((bf16[16,8,1024]{2,1,0:T(8,128)(2,1)}, bf16[16,8,1024]{2,1,0:T(8,128)(2,1)S(1)}, u32[]{:S(2)}, u32[]{:S(2)}) %collective-permute-start.1) | collective-permute-done | bytes 262176 | tf_op jit(solution)/shard_map/ppermute | solution.py:401
  9.5 3.1 %collective-permute-done.fl = bf16[16,8,1024]{2,1,0:T(8,128)(2,1)S(1)} collective-permute-done((bf16[16,8,1024]{2,1,0:T(8,128)(2,1)}, bf16[16,8,1024]{2,1,0:T(8,128)(2,1)S(1)}, u32[]{:S(2)}, u32[]{:S(2)}) %collective-permute-start) | collective-permute-done | bytes 262176 | tf_op jit(solution)/shard_map/ppermute | solution.py:400
  12.6 0.0 copy-start
  12.6 0.9 copy-done
  13.5 0.0 copy-start.2
  13.5 0.7 copy-done.2
  14.2 0.0 copy-start.4
  14.2 0.7 copy-done.4
  14.8 0.0 copy-start.5
  14.8 0.9 copy-done.5
  15.8 0.0 copy-start.1
  15.8 9.4 %shard_map.118 = (bf16[8,8,16,128]{3,2,1,0:T(8,128)(2,1)S(1)}, f32[560,2,8,128]{3,2,1,0:T(8,128)S(1)}, bf16[1024,128]{1,0:T(8,128)(2,1)S(1)}, bf16[1024,128]{1,0:T(8,128)(2,1)S(1)}, bf16[1024,128]{1,0:T(8,128)(2,1)S(1)}) custom-call(s32[5]{0:T(128)S(1)} %copy-done.4, s32[1]{0:T(128)} %bitcast.2.base, f32[5,64]{1,0:T(8,128)S(1)} %copy-done.2, ...), custom_call_target="tpu_custom_call" | custom-call | flops 754974720 | bytes 4000000 | tf_op jit(solution)/shard_map/pallas_call | solution.py:376
  25.2 14.8 %all_to_all.25.h_ref = bf16[8,8,16,128]{3,2,1,0:T(8,128)(2,1)S(1)} all-to-all(bf16[8,8,16,128]{3,2,1,0:T(8,128)(2,1)S(1)} %get-tuple-element.16), channel_id=1, replica_groups=mesh['vrow'=8,'img'=16] {'vrow'}, dimensions={0} | all-to-all | bytes 524288 | tf_op jit(solution)/shard_map/all_to_all | solution.py:416
  40.0 0.0 copy-start.6
  40.0 0.9 copy-done.6
  41.0 0.0 copy-start.7
  41.0 0.9 copy-done.7
  41.9 0.0 copy-start.8
  41.9 0.7 copy-done.8
  42.6 13.3 %shard_map.119 = (bf16[2,8,8192]{2,1,0:T(8,128)(2,1)}, bf16[8,8,16,128]{3,2,1,0:T(8,128)(2,1)S(1)}, f32[320,128]{1,0:T(8,128)S(1)}) custom-call(s32[5]{0:T(128)S(1)} %copy-done.4, f32[5,64]{1,0:T(8,128)S(1)} %copy-done.8, bf16[9,64,64]{2,1,0:T(8,128)(2,1)S(1)} %bitcast.29, bf16[8,8,16,128]{3,2,1,0:T(8,128)(2,1)S(1)} %all_to_all.25.h_ref, ...), custom_call_target="tpu_custom_call" | custom-call | flops 905969664 | bytes 4000000 | tf_op jit(solution)/shard_map/pallas_call | solution.py:376
  55.8 10.0 %all_to_all.26.gm = bf16[8,8,16,128]{3,2,1,0:T(8,128)(2,1)S(1)} all-to-all(bf16[8,8,16,128]{3,2,1,0:T(8,128)(2,1)S(1)} %get-tuple-element.22), channel_id=1, replica_groups=mesh['vrow'=8,'img'=16] {'vrow'}, dimensions={0} | all-to-all | bytes 524288 | tf_op jit(solution)/shard_map/all_to_all | solution.py:437
  65.9 1.9 %collective-permute-start.3 = (bf16[8,3,16,128]{3,2,1,0:T(8,128)(2,1)S(1)}, bf16[8,3,16,128]{3,2,1,0:T(8,128)(2,1)S(1)}, u32[]{:S(2)}, u32[]{:S(2)}) collective-permute-start(bf16[8,3,16,128]{3,2,1,0:T(8,128)(2,1)S(1)} %get-tuple-element.32), channel_id=1, source_target_pairs={{1,0},{2,1},{3,2},{4,3},{5,4},{6,5},{7,6},{8,7},{9,8},{10,9},{11,1... | collective-permute-start | bytes 294920 | tf_op jit(solution)/shard_map/ppermute | solution.py:438
  67.8 6.4 %collective-permute-start.2 = (bf16[8,3,16,128]{3,2,1,0:T(8,128)(2,1)S(1)}, bf16[8,3,16,128]{3,2,1,0:T(8,128)(2,1)S(1)}, u32[]{:S(2)}, u32[]{:S(2)}) collective-permute-start(bf16[8,3,16,128]{3,2,1,0:T(8,128)(2,1)S(1)} %get-tuple-element.33), channel_id=1, source_target_pairs={{0,1},{1,2},{2,3},{3,4},{4,5},{5,6},{6,7},{7,8},{8,9},{9,10},{10,1... | collective-permute-start | bytes 294920 | tf_op jit(solution)/shard_map/ppermute | solution.py:439
  74.2 0.4 collective-permute-done.3.gr
  74.6 1.3 collective-permute-done.2.gl
  75.8 0.0 copy-done.3
  75.8 0.0 copy-done.1
  75.8 11.2 %shard_map.120 = (bf16[16,8,1024]{2,1,0:T(8,128)(2,1)}, f32[640,128]{1,0:T(8,128)S(1)}) custom-call(s32[5]{0:T(128)S(1)} %copy-done.4, s32[1]{0:T(128)} %bitcast.2.base, f32[5,64]{1,0:T(8,128)S(1)} %copy-done.3, bf16[9,64,64]{2,1,0:T(8,128)(2,1)S(1)} %bitcast.25, f32[560,2,8,128]{3,2,1,0:T(8,128)S(1)} %get-tuple-element.18.pre_ref, ...), custom_call_target="tpu_custom_call" | custom-call | flops 603979776 | bytes 4000000 | tf_op jit(solution)/shard_map/pallas_call | solution.py:376
  87.1 14.9 %all_to_all.27 = f32[16,40,128]{2,1,0:T(8,128)S(1)} all-to-all(f32[16,40,128]{2,1,0:T(8,128)S(1)} %bitcast.23), channel_id=1, replica_groups=mesh['vrow'=8,'img'=16] {'img'}, dimensions={0} | all-to-all | bytes 655360 | tf_op jit(solution)/shard_map/all_to_all | solution.py:388
  102.0 9.6 %all_to_all.28 = f32[8,40,128]{2,1,0:T(8,128)S(1)} all-to-all(f32[8,40,128]{2,1,0:T(8,128)S(1)} %broadcast_in_dim.4), channel_id=1, replica_groups=mesh['vrow'=8,'img'=16] {'vrow'}, dimensions={0} | all-to-all | bytes 327680 | tf_op jit(solution)/shard_map/all_to_all | solution.py:389
  111.6 12.2 %all_to_all.29 = f32[16,40,128]{2,1,0:T(8,128)S(1)} all-to-all(f32[16,40,128]{2,1,0:T(8,128)S(1)} %broadcast_in_dim.5), channel_id=1, replica_groups=mesh['vrow'=8,'img'=16] {'img'}, dimensions={0} | all-to-all | bytes 655360 | tf_op jit(solution)/shard_map/all_to_all | solution.py:390
  123.9 0.7 fusion
  124.6 0.2 fusion.1
  124.8 0.7 slice.55
  125.5 0.7 slice.52
  (8 shorter events, 0.2 us)
Async XLA Ops:
  0.6 75.2 %copy-start.3 = (f32[5,64]{1,0:T(8,128)S(1)}, f32[5,64]{1,0:T(8,128)}, u32[]{:S(2)}) copy-start(f32[5,64]{1,0:T(8,128)} %beta_ref.5) | copy-start | bytes 3844
  0.6 8.8 %collective-permute-start.1 = (bf16[16,8,1024]{2,1,0:T(8,128)(2,1)}, bf16[16,8,1024]{2,1,0:T(8,128)(2,1)S(1)}, u32[]{:S(2)}, u32[]{:S(2)}) collective-permute-start(bf16[16,8,1024]{2,1,0:T(8,128)(2,1)} %bitcast.26), channel_id=1, source_target_pairs={{1,0},{2,1},{3,2},{4,3},{5,4},{6,5},{7,6},{8,7},{9,8},{10,9},{11,1... | collective-permute-start | bytes 786440 | tf_op jit(solution)/shard_map/ppermute | solution.py:401
  3.9 8.6 %collective-permute-start = (bf16[16,8,1024]{2,1,0:T(8,128)(2,1)}, bf16[16,8,1024]{2,1,0:T(8,128)(2,1)S(1)}, u32[]{:S(2)}, u32[]{:S(2)}) collective-permute-start(bf16[16,8,1024]{2,1,0:T(8,128)(2,1)} %bitcast.27), channel_id=1, source_target_pairs={{0,1},{1,2},{2,3},{3,4},{4,5},{5,6},{6,7},{7,8},{8,9},{9,10},{10,1... | collective-permute-start | bytes 786440 | tf_op jit(solution)/shard_map/ppermute | solution.py:400
  12.6 0.9 copy-start
  13.5 0.7 copy-start.2
  14.2 0.7 copy-start.4
  14.8 0.9 copy-start.5
  15.8 60.0 %copy-start.1 = (bf16[64,64,3,3]{1,0,3,2:T(8,128)(2,1)S(1)}, bf16[64,64,3,3]{1,0,3,2:T(8,128)(2,1)}, u32[]{:S(2)}) copy-start(bf16[64,64,3,3]{1,0,3,2:T(8,128)(2,1)} %param.8) | copy-start | bytes 221188
  40.0 1.0 copy-start.6
  41.0 0.9 copy-start.7
  41.9 0.7 copy-start.8
  65.9 8.7 %collective-permute-start.3 = (bf16[8,3,16,128]{3,2,1,0:T(8,128)(2,1)S(1)}, bf16[8,3,16,128]{3,2,1,0:T(8,128)(2,1)S(1)}, u32[]{:S(2)}, u32[]{:S(2)}) collective-permute-start(bf16[8,3,16,128]{3,2,1,0:T(8,128)(2,1)S(1)} %get-tuple-element.32), channel_id=1, source_target_pairs={{1,0},{2,1},{3,2},{4,3},{5,4},{6,5},{7,6},{8,7},{9,8},{10,9},{11,1... | collective-permute-start | bytes 294920 | tf_op jit(solution)/shard_map/ppermute | solution.py:438
  67.8 8.0 %collective-permute-start.2 = (bf16[8,3,16,128]{3,2,1,0:T(8,128)(2,1)S(1)}, bf16[8,3,16,128]{3,2,1,0:T(8,128)(2,1)S(1)}, u32[]{:S(2)}, u32[]{:S(2)}) collective-permute-start(bf16[8,3,16,128]{3,2,1,0:T(8,128)(2,1)S(1)} %get-tuple-element.33), channel_id=1, source_target_pairs={{0,1},{1,2},{2,3},{3,4},{4,5},{5,6},{6,7},{7,8},{8,9},{9,10},{10,1... | collective-permute-start | bytes 294920 | tf_op jit(solution)/shard_map/ppermute | solution.py:439

commit v3 on v2

--- a/solution.py
+++ b/solution.py
@@ -11,7 +11,8 @@
 HALF = 64
 TAPS = 9
 REACH = 3
-VMEM_BYTES = 36 * 1024 * 1024
+MIB = 1024 * 1024
+GRANT = (36, 36, 36)
 NT = (((1,), (1,)), ((), ()))
 NN = (((1,), (0,)), ((), ()))
 TN = (((0,), (0,)), ((), ()))
@@ -79,8 +80,9 @@
     return (lanes_of((1, 8, LANES)) >= HALF).astype(jnp.int32)
 
 
-def h_forward(shear, base, beta_ref, w_ref, fl, fm, fr, hfeat, pre_ref, f0_out, fm_out, fp_out, beta, stage, f0, fmi, fpl, taps, wt):
+def h_forward(ready, shear, beta_ref, w_ref, fm, base, fl, fr, hfeat, pre_ref, f0_out, fm_out, fp_out, beta, stage, f0, fmi, fpl, taps, wt):
     shears = shear.shape[0]
+    ready()
     spread(beta_ref, beta)
     fill_weights(w_ref, wt)
     first16 = low((16, LANES))
@@ -155,9 +157,10 @@
         body(n // 8 + 8 + REACH, n % 8, False)
 
 
-def h_backward(shear, base, beta_ref, w_ref, pre_ref, f0, fmi, fpl, gm, gl, gr, pay_v, out, pay, beta, dps, sums, edges, dfs, stage, blend, wt):
+def h_backward(ready, shear, beta_ref, w_ref, base, pre_ref, f0, fmi, fpl, gm, gl, gr, pay_v, out, pay, beta, dps, sums, edges, dfs, stage, blend, wt):
     shears = shear.shape[0]
     step = shears * 112
+    ready()
     spread(beta_ref, beta)
     fill_weights(w_ref, wt)
     half = halves()
@@ -243,12 +246,10 @@
             out[y, :, pl.ds(q * LANES, LANES)] = stage[q, pl.ds(y, 8, stride=16), :].astype(BF)
 
 
-def v_both(shear, beta_ref, w_ref, h_ref, cot, out, dvert, pay, beta, own, fv, taps, dps, sums, grads, outs, edges, blend, wt):
+def v_both(ready, shear, beta_ref, w_ref, cot, h_ref, out, dvert, pay, beta, own, fv, taps, dps, sums, grads, outs, edges, blend, wt):
     shears = shear.shape[0]
     wide = 22
     plane = 10 * wide
-    spread(beta_ref, beta)
-    fill_weights(w_ref, wt)
     blend[...] = jnp.zeros(blend.shape, F32)
     first8 = low((8, LANES))
 
@@ -269,6 +270,10 @@
                 sums[pl.ds(j * plane + side + u * wide, REACH)] = rim
             for jk in range(3 * shears):
                 dps[pl.ds(jk * plane + side + u * wide, REACH)] = rim
+
+    ready()
+    spread(beta_ref, beta)
+    fill_weights(w_ref, wt)
 
     @pl.loop(0, 8)
     def _(u):
@@ -370,18 +375,48 @@
                 out[1, :, lanes] = jnp.where(first8, swap(a), b).astype(BF)
 
 
-def call(body, operands, out_shapes, scratch, smem, cost):
+def call(body, fetched, operands, out_shapes, scratch, cost, vmem_mib):
     vmem = pl.BlockSpec(memory_space=pltpu.VMEM)
-    specs = [pl.BlockSpec(memory_space=pltpu.SMEM)] * smem + [vmem] * (len(operands) - smem)
+    specs = [pl.BlockSpec(memory_space=pltpu.HBM)] * len(fetched)
+    specs += [pl.BlockSpec(memory_space=pltpu.SMEM if op.dtype == jnp.int32 else pltpu.VMEM) for op in operands]
+    held = [pltpu.SMEM(fetched[0].shape, fetched[0].dtype)] + [pltpu.VMEM(op.shape, op.dtype) for op in fetched[1:]]
+    count = len(fetched)
+
+    def kernel(*refs):
+        sources, others = refs[:count], refs[count : -count - 1]
+        targets, sem = refs[-count - 1 : -1], refs[-1]
+        copies = [pltpu.make_async_copy(sources[i], targets[i], sem.at[i]) for i in range(count)]
+        for copy in copies:
+            copy.start()
+
+        def ready():
+            for copy in copies:
+                copy.wait()
+
+        body(ready, *targets, *others)
+
     return pl.pallas_call(
-        body,
+        kernel,
         out_shape=out_shapes,
         in_specs=specs,
         out_specs=[vmem] * len(out_shapes),
-        scratch_shapes=scratch,
-        compiler_params=pltpu.CompilerParams(vmem_limit_bytes=VMEM_BYTES),
+        scratch_shapes=list(scratch) + held + [pltpu.SemaphoreType.DMA((count,))],
+        compiler_params=pltpu.CompilerParams(vmem_limit_bytes=int(vmem_mib * MIB)),
         cost_estimate=pl.CostEstimate(flops=cost, bytes_accessed=4_000_000, transcendentals=1_000_000),
-    )(*operands)
+    )(*[pltpu.with_memory_space_constraint(op, pltpu.HBM) for op in fetched], *operands)
+
+
+def unpack(total, w_h, w_v, b_h, b_v):
+    scale = 262144.0**-0.5
+    for at, weight, blend in ((0, w_h, b_h), (5 * HALF, w_v, b_v)):
+        for pair in range(5):
+            block = total[pl.ds(at + pair * HALF, HALF), :] * scale
+            weight[2 * pair] = block[:, :HALF]
+            other = swap(block)[:, :HALF]
+            if pair < 4:
+                weight[2 * pair + 1] = other
+            else:
+                blend[...] = other[: blend.shape[0]]
 
 
 def reduce_all(pay):
@@ -405,18 +440,20 @@
 
     hfeat, pre, f0, fmi, fpl = call(
         h_forward,
-        (shear_set, base, beta_h, w_h, from_left, own, from_right),
+        (shear_set, beta_h, w_h, own),
+        (base, from_left, from_right),
         [sds((8, 8, 16, LANES), BF), sds((shears * 112, 2, 8, LANES), F32)] + [sds((1024, LANES), BF)] * 3,
         [pltpu.VMEM((shears, 8, LANES), F32), pltpu.VMEM((8, 384, LANES), F32)]
         + [pltpu.VMEM((20 * LANES, LANES), BF)] * 3
         + [pltpu.VMEM((TAPS * 160, 2, 8, LANES), F32), pltpu.VMEM((TAPS * LANES, LANES), BF)],
-        2,
         2 * 2560 * LANES * TAPS * LANES,
+        GRANT[0],
     )
     moved = lax.all_to_all(hfeat, "vrow", 0, 0, tiled=True)
     output, dvert, pay_v = call(
         v_both,
-        (shear_set, beta_v, w_v, moved, cotangent),
+        (shear_set, beta_v, w_v, cotangent),
+        (moved,),
         [sds((2, 8, 8192), BF), sds((8, 8, 16, LANES), BF), sds((320, LANES), F32)],
         [
             pltpu.VMEM((shears, 8, LANES), F32),
@@ -431,15 +468,16 @@
             pltpu.VMEM((shears, 8, LANES), F32),
             pltpu.VMEM((TAPS * LANES, LANES), BF),
         ],
-        1,
         6 * 1024 * LANES * TAPS * LANES,
+        GRANT[1],
     )
     grad = lax.all_to_all(dvert, "vrow", 0, 0, tiled=True)
     grad_right = lax.ppermute(grad[:, :REACH], "img", to_left)
     grad_left = lax.ppermute(grad[:, 8 - REACH :], "img", to_right)
     grad_features, pay = call(
         h_backward,
-        (shear_set, base, beta_h, w_h, pre, f0, fmi, fpl, grad, grad_left, grad_right, pay_v),
+        (shear_set, beta_h, w_h),
+        (base, pre, f0, fmi, fpl, grad, grad_left, grad_right, pay_v),
         [sds((16, 8, 1024), BF), sds((640, LANES), F32)],
         [
             pltpu.VMEM((shears, 8, LANES), F32),
@@ -451,26 +489,22 @@
             pltpu.VMEM((shears, 8, LANES), F32),
             pltpu.VMEM((TAPS * LANES, LANES), BF),
         ],
-        2,
         4 * 1024 * LANES * TAPS * LANES,
+        GRANT[2],
     )
-    total = reduce_all(pay) * (262144.0**-0.5)
-
-    def unpack(block):
-        pairs = jnp.stack([block[:, :HALF].reshape(5, HALF, HALF), block[:, HALF:].reshape(5, HALF, HALF)], axis=1)
-        weight = jnp.transpose(pairs.reshape(10, HALF, HALF)[:TAPS].reshape(3, 3, HALF, HALF), (2, 3, 0, 1))
-        return weight, block[4 * HALF : 4 * HALF + shears, HALF:]
-
-    weight_grad_h, beta_grad_h = unpack(total[:320])
-    weight_grad_v, beta_grad_v = unpack(total[320:])
-    return (
-        output,
-        grad_features.reshape(features.shape),
-        weight_grad_h,
-        weight_grad_v,
-        beta_grad_h,
-        beta_grad_v,
-    )
+    vmem = pl.BlockSpec(memory_space=pltpu.VMEM)
+    weights = sds((TAPS, HALF, HALF), F32)
+    w_grad_h, w_grad_v, beta_grad_h, beta_grad_v = pl.pallas_call(
+        unpack,
+        out_shape=[weights, weights] + [sds((shears, HALF), F32)] * 2,
+        in_specs=[vmem],
+        out_specs=[vmem] * 4,
+    )(reduce_all(pay))
+
+    def placed(weight):
+        return jnp.transpose(weight.reshape(3, 3, HALF, HALF), (2, 3, 0, 1))
+
+    return output, grad_features.reshape(features.shape), placed(w_grad_h), placed(w_grad_v), beta_grad_h, beta_grad_v
 
 
 def solution(mesh):

time: 127 us -> 122 us (0.961)
  local copies, waits for them, and re-layouts: 8.1 us -> 0.05 us
  Pallas kernels: 33.9 us -> 37 us
    unnamed x18 -> x0, local copies, waits for them, and re-layouts: 5.75 us -> none
    pallas_call x3 -> x4, Pallas kernels: 33.9 us -> 37 us  [the longest x3 35.1 us: call(): pl.pallas_call(kernel, out_shape=out_shapes, in_specs=specs, out_specs=[v...]
    slice x4 -> x0, local copies, waits for them, and re-layouts: 2.3 us -> none  [the longest x2 1.47 us: unpack(): pairs.reshape(10, HALF, HALF)[:TAPS].reshape(3, 3, HALF, HALF)]
where the time goes in v3:
time: 122 us
  blocking collectives  62.2 us (51%)
  Pallas kernels  37 us (30%)
  starting transfers between devices  14.8 us (12%)
  waiting for transfers between devices  7.02 us (6%)
    pallas_call x3, Pallas kernels, call(): pl.pallas_call(kernel, out_shape=out_shapes, in_specs=specs, out_specs=[v...  35.1 us
    all_to_all x1, blocking collectives, reduce_all(): lax.all_to_all(pay.reshape(16, 40, LANES), 'img', 0, 0, tiled=True).sum(0)  14.9 us
    all_to_all x1, blocking collectives, per_device(): moved = lax.all_to_all(hfeat, 'vrow', 0, 0, tiled=True)  14.8 us
    all_to_all x1, blocking collectives, reduce_all(): lax.all_to_all(jnp.broadcast_to(part[None], (16, 40, LANES)), 'img', 0, 0...  12.8 us
    all_to_all x1, blocking collectives, per_device(): grad = lax.all_to_all(dvert, 'vrow', 0, 0, tiled=True)  10.1 us
    all_to_all x1, blocking collectives, reduce_all(): lax.all_to_all(jnp.broadcast_to(part[None], (8, 40, LANES)), 'vrow', 0, 0...  9.58 us
    ppermute x1, starting transfers between devices, per_device(): grad_left = lax.ppermute(grad[:, 8 - REACH:], 'img', to_right)  6.37 us
    ppermute x1, starting transfers between devices, per_device(): from_right = lax.ppermute(own, 'img', to_left)  3.29 us
  transfers between devices with their start and end apart: 4, of which 4 were waited for; matrix products, arithmetic and copies ran while one was open for 0% of the time, Pallas kernels for 0%

profile of v3, /device:TPU:1, one launch (start us, length us, event | category | flops | bytes accessed | tf_op | source)
XLA Modules:
  0.0 121.8 jit_solution(8396248946576954145)
XLA Ops:
  0.6 3.3 %collective-permute-start.1 = (bf16[16,8,1024]{2,1,0:T(8,128)(2,1)}, bf16[16,8,1024]{2,1,0:T(8,128)(2,1)S(1)}, u32[]{:S(2)}, u32[]{:S(2)}) collective-permute-start(bf16[16,8,1024]{2,1,0:T(8,128)(2,1)} %bitcast.23), channel_id=1, source_target_pairs={{1,0},{2,1},{3,2},{4,3},{5,4},{6,5},{7,6},{8,7},{9,8},{10,9},{11,1... | collective-permute-start | bytes 786440 | tf_op jit(solution)/shard_map/ppermute | solution.py:436
  3.9 3.2 %collective-permute-start = (bf16[16,8,1024]{2,1,0:T(8,128)(2,1)}, bf16[16,8,1024]{2,1,0:T(8,128)(2,1)S(1)}, u32[]{:S(2)}, u32[]{:S(2)}) collective-permute-start(bf16[16,8,1024]{2,1,0:T(8,128)(2,1)} %bitcast.24), channel_id=1, source_target_pairs={{0,1},{1,2},{2,3},{3,4},{4,5},{5,6},{6,7},{7,8},{8,9},{9,10},{10,1... | collective-permute-start | bytes 786440 | tf_op jit(solution)/shard_map/ppermute | solution.py:435
  7.2 2.3 %collective-permute-done.1.refs_6_ = bf16[16,8,1024]{2,1,0:T(8,128)(2,1)S(1)} collective-permute-done((bf16[16,8,1024]{2,1,0:T(8,128)(2,1)}, bf16[16,8,1024]{2,1,0:T(8,128)(2,1)S(1)}, u32[]{:S(2)}, u32[]{:S(2)}) %collective-permute-start.1) | collective-permute-done | bytes 262176 | tf_op jit(solution)/shard_map/ppermute | solution.py:436
  9.5 3.1 %collective-permute-done.refs_5_ = bf16[16,8,1024]{2,1,0:T(8,128)(2,1)S(1)} collective-permute-done((bf16[16,8,1024]{2,1,0:T(8,128)(2,1)}, bf16[16,8,1024]{2,1,0:T(8,128)(2,1)S(1)}, u32[]{:S(2)}, u32[]{:S(2)}) %collective-permute-start) | collective-permute-done | bytes 262176 | tf_op jit(solution)/shard_map/ppermute | solution.py:435
  12.6 10.0 %shard_map.118 = (bf16[8,8,16,128]{3,2,1,0:T(8,128)(2,1)S(1)}, f32[560,2,8,128]{3,2,1,0:T(8,128)S(1)}, bf16[1024,128]{1,0:T(8,128)(2,1)S(1)}, bf16[1024,128]{1,0:T(8,128)(2,1)S(1)}, bf16[1024,128]{1,0:T(8,128)(2,1)S(1)}) custom-call(s32[5]{0:T(128)} %refs_0_.5, f32[5,64]{1,0:T(8,128)} %refs_1_.5, bf16[9,64,64]{2,1,0:T(8,128)(2,1)} %bitcast.19, ...), custom_call_target="tpu_custom_call" | custom-call | flops 754974720 | bytes 4000000 | tf_op jit(solution)/shard_map/pallas_call | solution.py:398
  22.5 14.8 %all_to_all.25.refs_4_ = bf16[8,8,16,128]{3,2,1,0:T(8,128)(2,1)S(1)} all-to-all(bf16[8,8,16,128]{3,2,1,0:T(8,128)(2,1)S(1)} %get-tuple-element.20), channel_id=1, replica_groups=mesh['vrow'=8,'img'=16] {'vrow'}, dimensions={0} | all-to-all | bytes 524288 | tf_op jit(solution)/shard_map/all_to_all | solution.py:452
  37.3 13.5 %shard_map.119 = (bf16[2,8,8192]{2,1,0:T(8,128)(2,1)}, bf16[8,8,16,128]{3,2,1,0:T(8,128)(2,1)S(1)}, f32[320,128]{1,0:T(8,128)S(1)}) custom-call(s32[5]{0:T(128)} %refs_0_.5, f32[5,64]{1,0:T(8,128)} %refs_1_.4, bf16[9,64,64]{2,1,0:T(8,128)(2,1)} %bitcast.27, bf16[2,8,8192]{2,1,0:T(8,128)(2,1)} %refs_3_.1, bf16[8,8,16,128]{3,2,1,0:T(8,128)(2,1)S(1)} %all_to_all.25.refs_4_), custom_call_target="tpu_custom_call" | custom-call | flops 905969664 | bytes 4000000 | tf_op jit(solution)/shard_map/pallas_call | solution.py:398
  50.8 10.1 %all_to_all.26.refs_8_ = bf16[8,8,16,128]{3,2,1,0:T(8,128)(2,1)S(1)} all-to-all(bf16[8,8,16,128]{3,2,1,0:T(8,128)(2,1)S(1)} %get-tuple-element.26), channel_id=1, replica_groups=mesh['vrow'=8,'img'=16] {'vrow'}, dimensions={0} | all-to-all | bytes 524288 | tf_op jit(solution)/shard_map/all_to_all | solution.py:474
  60.9 1.9 %collective-permute-start.3 = (bf16[8,3,16,128]{3,2,1,0:T(8,128)(2,1)S(1)}, bf16[8,3,16,128]{3,2,1,0:T(8,128)(2,1)S(1)}, u32[]{:S(2)}, u32[]{:S(2)}) collective-permute-start(bf16[8,3,16,128]{3,2,1,0:T(8,128)(2,1)S(1)} %get-tuple-element.34), channel_id=1, source_target_pairs={{1,0},{2,1},{3,2},{4,3},{5,4},{6,5},{7,6},{8,7},{9,8},{10,9},{11,1... | collective-permute-start | bytes 294920 | tf_op jit(solution)/shard_map/ppermute | solution.py:475
  62.8 6.4 %collective-permute-start.2 = (bf16[8,3,16,128]{3,2,1,0:T(8,128)(2,1)S(1)}, bf16[8,3,16,128]{3,2,1,0:T(8,128)(2,1)S(1)}, u32[]{:S(2)}, u32[]{:S(2)}) collective-permute-start(bf16[8,3,16,128]{3,2,1,0:T(8,128)(2,1)S(1)} %get-tuple-element.35), channel_id=1, source_target_pairs={{0,1},{1,2},{2,3},{3,4},{4,5},{5,6},{6,7},{7,8},{8,9},{9,10},{10,1... | collective-permute-start | bytes 294920 | tf_op jit(solution)/shard_map/ppermute | solution.py:476
  69.2 0.4 collective-permute-done.3.refs_10_
  69.6 1.3 %collective-permute-done.2.refs_9_ = bf16[8,3,16,128]{3,2,1,0:T(8,128)(2,1)S(1)} collective-permute-done((bf16[8,3,16,128]{3,2,1,0:T(8,128)(2,1)S(1)}, bf16[8,3,16,128]{3,2,1,0:T(8,128)(2,1)S(1)}, u32[]{:S(2)}, u32[]{:S(2)}) %collective-permute-start.2) | collective-permute-done | bytes 98336 | tf_op jit(solution)/shard_map/ppermute | solution.py:476
  70.8 11.6 %shard_map.120 = (bf16[16,8,1024]{2,1,0:T(8,128)(2,1)}, f32[640,128]{1,0:T(8,128)S(1)}) custom-call(s32[5]{0:T(128)} %refs_0_.5, f32[5,64]{1,0:T(8,128)} %refs_1_.5, bf16[9,64,64]{2,1,0:T(8,128)(2,1)} %bitcast.20, s32[1]{0:T(128)} %bitcast.5.refs_4_.refs_3_, f32[560,2,8,128]{3,2,1,0:T(8,128)S(1)} %get-tuple-element.22.refs_4_, ...), custom_call_target="tpu_custom_call" | custom-call | flops 603979776 | bytes 4000000 | tf_op jit(solution)/shard_map/pallas_call | solution.py:398
  82.5 14.9 %all_to_all.27 = f32[16,40,128]{2,1,0:T(8,128)S(1)} all-to-all(f32[16,40,128]{2,1,0:T(8,128)S(1)} %bitcast.17), channel_id=1, replica_groups=mesh['vrow'=8,'img'=16] {'img'}, dimensions={0} | all-to-all | bytes 655360 | tf_op jit(solution)/shard_map/all_to_all | solution.py:423
  97.5 9.6 %all_to_all.28 = f32[8,40,128]{2,1,0:T(8,128)S(1)} all-to-all(f32[8,40,128]{2,1,0:T(8,128)S(1)} %broadcast_in_dim.4), channel_id=1, replica_groups=mesh['vrow'=8,'img'=16] {'vrow'}, dimensions={0} | all-to-all | bytes 327680 | tf_op jit(solution)/shard_map/all_to_all | solution.py:424
  107.1 12.8 %all_to_all.29 = f32[16,40,128]{2,1,0:T(8,128)} all-to-all(f32[16,40,128]{2,1,0:T(8,128)S(1)} %broadcast_in_dim.5), channel_id=1, replica_groups=mesh['vrow'=8,'img'=16] {'img'}, dimensions={0} | all-to-all | bytes 655360 | tf_op jit(solution)/shard_map/all_to_all | solution.py:425
  119.9 1.9 %shard_map.121 = (f32[9,64,64]{2,1,0:T(8,128)}, f32[9,64,64]{2,1,0:T(8,128)}, f32[5,64]{1,0:T(8,128)}, f32[5,64]{1,0:T(8,128)}) custom-call(f32[640,128]{1,0:T(8,128)} %bitcast.18), custom_call_target="tpu_custom_call" | custom-call | tf_op jit(solution)/shard_map/pallas_call | solution.py:497
  (5 shorter events, 0.1 us)
Async XLA Ops:
  0.6 8.8 %collective-permute-start.1 = (bf16[16,8,1024]{2,1,0:T(8,128)(2,1)}, bf16[16,8,1024]{2,1,0:T(8,128)(2,1)S(1)}, u32[]{:S(2)}, u32[]{:S(2)}) collective-permute-start(bf16[16,8,1024]{2,1,0:T(8,128)(2,1)} %bitcast.23), channel_id=1, source_target_pairs={{1,0},{2,1},{3,2},{4,3},{5,4},{6,5},{7,6},{8,7},{9,8},{10,9},{11,1... | collective-permute-start | bytes 786440 | tf_op jit(solution)/shard_map/ppermute | solution.py:436
  3.9 8.6 %collective-permute-start = (bf16[16,8,1024]{2,1,0:T(8,128)(2,1)}, bf16[16,8,1024]{2,1,0:T(8,128)(2,1)S(1)}, u32[]{:S(2)}, u32[]{:S(2)}) collective-permute-start(bf16[16,8,1024]{2,1,0:T(8,128)(2,1)} %bitcast.24), channel_id=1, source_target_pairs={{0,1},{1,2},{2,3},{3,4},{4,5},{5,6},{6,7},{7,8},{8,9},{9,10},{10,1... | collective-permute-start | bytes 786440 | tf_op jit(solution)/shard_map/ppermute | solution.py:435
  60.9 8.7 %collective-permute-start.3 = (bf16[8,3,16,128]{3,2,1,0:T(8,128)(2,1)S(1)}, bf16[8,3,16,128]{3,2,1,0:T(8,128)(2,1)S(1)}, u32[]{:S(2)}, u32[]{:S(2)}) collective-permute-start(bf16[8,3,16,128]{3,2,1,0:T(8,128)(2,1)S(1)} %get-tuple-element.34), channel_id=1, source_target_pairs={{1,0},{2,1},{3,2},{4,3},{5,4},{6,5},{7,6},{8,7},{9,8},{10,9},{11,1... | collective-permute-start | bytes 294920 | tf_op jit(solution)/shard_map/ppermute | solution.py:475
  62.8 8.0 %collective-permute-start.2 = (bf16[8,3,16,128]{3,2,1,0:T(8,128)(2,1)S(1)}, bf16[8,3,16,128]{3,2,1,0:T(8,128)(2,1)S(1)}, u32[]{:S(2)}, u32[]{:S(2)}) collective-permute-start(bf16[8,3,16,128]{3,2,1,0:T(8,128)(2,1)S(1)} %get-tuple-element.35), channel_id=1, source_target_pairs={{0,1},{1,2},{2,3},{3,4},{4,5},{5,6},{6,7},{7,8},{8,9},{9,10},{10,1... | collective-permute-start | bytes 294920 | tf_op jit(solution)/shard_map/ppermute | solution.py:476

commit v4 on v3

--- a/solution.py
+++ b/solution.py
@@ -12,7 +12,7 @@
 TAPS = 9
 REACH = 3
 MIB = 1024 * 1024
-GRANT = (36, 36, 36)
+GRANT = (26, 36, 34, 26, 16)
 NT = (((1,), (1,)), ((), ()))
 NN = (((1,), (0,)), ((), ()))
 TN = (((0,), (0,)), ((), ()))
@@ -80,7 +80,7 @@
     return (lanes_of((1, 8, LANES)) >= HALF).astype(jnp.int32)
 
 
-def h_forward(ready, shear, beta_ref, w_ref, fm, base, fl, fr, hfeat, pre_ref, f0_out, fm_out, fp_out, beta, stage, f0, fmi, fpl, taps, wt):
+def h_forward(ready, shear, beta_ref, w_ref, fm, base, fl, fr, hfeat, pre_ref, taps, f0_out, fm_out, fp_out, beta, stage, f0, fmi, fpl, wt):
     shears = shear.shape[0]
     ready()
     spread(beta_ref, beta)
@@ -123,46 +123,67 @@
 
     half = halves()
 
-    def body(xe, q, local):
-        here = (xe + 3) * 8 + q
-        vrel = half + (2 * q - 8)
-        xg = base[0] + xe - REACH
-        mid = taps[4 * 160 + here]
-        left = taps[3 * 160 - 8 + here]
-        right = taps[5 * 160 + 8 + here]
+    @pl.loop(0, 64)
+    def _(n):
+        q = n % 8
         branch = jnp.zeros((2, 8, LANES), F32)
-        for k in range(shears):
-            d = shear[k]
-            xs = xg - d * vrel
-            a, b = here - d * 8, here + d * 8
-            main = mid + (taps[160 + a] + taps[7 * 160 + b])
-            minus = left + (taps[a - 8] + taps[6 * 160 - 8 + b])
-            plus = right + (taps[2 * 160 + 8 + a] + taps[8 * 160 + 8 + b])
-            pre = main + jnp.where(xs >= 1, minus, 0.0) + jnp.where(xs <= LANES - 2, plus, 0.0)
-            pre_ref[k * 112 + xe * 8 + q] = pre
-            if local:
-                keep = (xs >= 0) & (xs < LANES)
-                branch = branch + jnp.where(keep, beta[k] * gate(pre)[0], 0.0)
-        if local:
-            own = f0[pl.ds(pl.multiple_of(here * 16, 16), 16), :].astype(F32)
-            hfeat[q, xe - REACH] = (own + branch.reshape(16, LANES)).astype(BF)
+        for k, (xs, pre) in enumerate(sheared_taps(shear, base, taps, half, n // 8 + REACH, q)):
+            pre_ref[k * 64 + n] = pre
+            keep = (xs >= 0) & (xs < LANES)
+            branch = branch + jnp.where(keep, beta[k] * gate(pre)[0], 0.0)
+        own = f0[pl.ds(pl.multiple_of(n * 16 + 6 * LANES, 16), 16), :].astype(F32)
+        hfeat[q, n // 8] = (own + branch.reshape(16, LANES)).astype(BF)
+
+
+def sheared_taps(shear, base, taps, half, xe, q):
+    here = (xe + 3) * 8 + q
+    vrel = half + (2 * q - 8)
+    xg = base[0] + xe - REACH
+    mid = taps[4 * 160 + here]
+    left = taps[3 * 160 - 8 + here]
+    right = taps[5 * 160 + 8 + here]
+    found = []
+    for k in range(shear.shape[0]):
+        d = shear[k]
+        xs = xg - d * vrel
+        a, b = here - d * 8, here + d * 8
+        main = mid + (taps[160 + a] + taps[7 * 160 + b])
+        minus = left + (taps[a - 8] + taps[6 * 160 - 8 + b])
+        plus = right + (taps[2 * 160 + 8 + a] + taps[8 * 160 + 8 + b])
+        found.append((xs, main + jnp.where(xs >= 1, minus, 0.0) + jnp.where(xs <= LANES - 2, plus, 0.0)))
+    return found
+
+
+def h_slopes(ready, shear, beta_ref, base, pre_ref, taps, slopes, acts, beta):
+    ready()
+    spread(beta_ref, beta)
+    half = halves()
+
+    def save(k, at, xs, pre, local):
+        act, slope = gate(pre)
+        keep = (xs >= 0) & (xs < LANES)
+        slopes[k * 112 + at] = jnp.where(keep, beta[k] * slope, 0.0)
+        if local is not None:
+            acts[k * 64 + local] = jnp.where(keep, act, 0.0)
 
     @pl.loop(0, 64)
     def _(n):
-        body(n // 8 + REACH, n % 8, True)
+        vrel = half + (2 * (n % 8) - 8)
+        xg = base[0] + n // 8
+        for k in range(shear.shape[0]):
+            save(k, n + REACH * 8, xg - shear[k] * vrel, pre_ref[k * 64 + n], n)
 
     @pl.loop(0, 24)
     def _(n):
-        body(n // 8, n % 8, False)
-        body(n // 8 + 8 + REACH, n % 8, False)
-
-
-def h_backward(ready, shear, beta_ref, w_ref, base, pre_ref, f0, fmi, fpl, gm, gl, gr, pay_v, out, pay, beta, dps, sums, edges, dfs, stage, blend, wt):
+        for xe in (n // 8, n // 8 + 8 + REACH):
+            for k, (xs, pre) in enumerate(sheared_taps(shear, base, taps, half, xe, n % 8)):
+                save(k, xe * 8 + n % 8, xs, pre, None)
+
+
+def h_backward(ready, shear, base, slopes, acts, f0, fmi, fpl, gm, gl, gr, pay_v, pay, edges_out, dps, sums, edges, blend, edges_sem):
     shears = shear.shape[0]
     step = shears * 112
     ready()
-    spread(beta_ref, beta)
-    fill_weights(w_ref, wt)
     half = halves()
     blend[...] = jnp.zeros(blend.shape, F32)
 
@@ -174,15 +195,13 @@
         total = [jnp.zeros((2, 8, LANES), F32) for _ in range(3)]
         for k in range(shears):
             xs = xg - shear[k] * vrel
-            act, slope = gate(pre_ref[k * 112 + here])
-            gk = jnp.where((xs >= 0) & (xs < LANES), g, 0.0)
-            dp = (beta[k] * gk * slope).astype(BF).astype(F32)
+            dp = (slopes[k * 112 + here] * g).astype(BF).astype(F32)
             parts = (jnp.where(xs >= 1, dp, 0.0), dp, jnp.where(xs <= LANES - 2, dp, 0.0))
             for j in range(3):
                 dps[j * step + k * 112 + here] = parts[j]
                 total[j] = total[j] + parts[j]
             if local:
-                blend[k] += jnp.sum(gk * act, axis=0)
+                blend[k] += jnp.sum(g * acts[k * 64 - REACH * 8 + here], axis=0)
         for j in range(3):
             sums[j * 112 + here] = total[j]
 
@@ -215,8 +234,17 @@
             edges[1, at, lanes] = sums[j * 112 - (j - 1) * 8 + here].reshape(16, LANES).astype(BF)
             edges[2, at, lanes] = above[j].reshape(16, LANES).astype(BF)
 
+    copy = pltpu.make_async_copy(edges, edges_out, edges_sem)
+    copy.start()
     pack_grads([mm(ref[...], edges[side], TN) for side, ref in enumerate((fmi, f0, fpl))], blend, pay)
     pay[pl.ds(5 * HALF, 5 * HALF), :] = pay_v[...]
+    copy.wait()
+
+
+def h_finish(ready, w_ref, edges, gm, out, token, dfs, stage, wt):
+    token[...] = jnp.zeros(token.shape, F32)
+    ready()
+    fill_weights(w_ref, wt)
 
     @pl.loop(0, 4)
     def _(x):
@@ -309,21 +337,20 @@
         shared = []
         for k in range(shears):
             d = shear[k]
-            ys = y - d * (u - 4)
-            keep = ((ys >= 0) & (ys < 16)).astype(F32)
-            has_minus = (ys >= 1).astype(F32)
-            has_plus = (ys <= 14).astype(F32)
+            ys = jnp.full((8, LANES), y - d * (u - 4), jnp.int32)
+            keep = (ys >= 0) & (ys < 16)
+            has_minus, has_plus = ys >= 1, ys <= 14
             a, b = here - d, here + d
             main = mid + (taps[plane - wide + a] + taps[7 * plane + wide + b])
             minus = left + (taps[-wide - 1 + a] + taps[6 * plane + wide - 1 + b])
             plus = right + (taps[2 * plane - wide + 1 + a] + taps[8 * plane + wide + 1 + b])
-            act, slope = gate(main + has_minus * minus + has_plus * plus)
-            act = keep * act
+            act, slope = gate(main + jnp.where(has_minus, minus, 0.0) + jnp.where(has_plus, plus, 0.0))
+            act = jnp.where(keep, act, 0.0)
             bk = beta[k]
             branch = branch + bk * act
             shared.append(g * act)
-            dp = (bk * (keep * g) * slope).astype(BF).astype(F32)
-            parts = (has_minus * dp, dp, has_plus * dp)
+            dp = jnp.where(keep, bk * g * slope, 0.0).astype(BF).astype(F32)
+            parts = (jnp.where(has_minus, dp, 0.0), dp, jnp.where(has_plus, dp, 0.0))
             for j in range(3):
                 dps[(j * shears + k) * plane + here] = parts[j]
                 total[j] = total[j] + parts[j]
@@ -375,11 +402,11 @@
                 out[1, :, lanes] = jnp.where(first8, swap(a), b).astype(BF)
 
 
-def call(body, fetched, operands, out_shapes, scratch, cost, vmem_mib):
+def call(body, fetched, operands, out_shapes, scratch, cost, vmem_mib, far=()):
     vmem = pl.BlockSpec(memory_space=pltpu.VMEM)
     specs = [pl.BlockSpec(memory_space=pltpu.HBM)] * len(fetched)
     specs += [pl.BlockSpec(memory_space=pltpu.SMEM if op.dtype == jnp.int32 else pltpu.VMEM) for op in operands]
-    held = [pltpu.SMEM(fetched[0].shape, fetched[0].dtype)] + [pltpu.VMEM(op.shape, op.dtype) for op in fetched[1:]]
+    held = [(pltpu.SMEM if op.dtype == jnp.int32 else pltpu.VMEM)(op.shape, op.dtype) for op in fetched]
     count = len(fetched)
 
     def kernel(*refs):
@@ -399,7 +426,7 @@
         kernel,
         out_shape=out_shapes,
         in_specs=specs,
-        out_specs=[vmem] * len(out_shapes),
+        out_specs=[pl.BlockSpec(memory_space=pltpu.HBM) if i in far else vmem for i in range(len(out_shapes))],
         scratch_shapes=list(scratch) + held + [pltpu.SemaphoreType.DMA((count,))],
         compiler_params=pltpu.CompilerParams(vmem_limit_bytes=int(vmem_mib * MIB)),
         cost_estimate=pl.CostEstimate(flops=cost, bytes_accessed=4_000_000, transcendentals=1_000_000),
@@ -419,8 +446,8 @@
                 blend[...] = other[: blend.shape[0]]
 
 
-def reduce_all(pay):
-    part = lax.all_to_all(pay.reshape(16, 40, LANES), "img", 0, 0, tiled=True).sum(0)
+def reduce_all(pay, zero):
+    part = lax.all_to_all(pay.reshape(16, 40, LANES), "img", 0, 0, tiled=True).sum(0) + zero
     part = lax.all_to_all(jnp.broadcast_to(part[None], (8, 40, LANES)), "vrow", 0, 0, tiled=True).sum(0)
     return lax.all_to_all(jnp.broadcast_to(part[None], (16, 40, LANES)), "img", 0, 0, tiled=True).reshape(640, LANES)
 
@@ -438,18 +465,28 @@
     w_h = jnp.transpose(weight_h, (2, 3, 0, 1)).reshape(TAPS, HALF, HALF)
     w_v = jnp.transpose(weight_v, (2, 3, 0, 1)).reshape(TAPS, HALF, HALF)
 
-    hfeat, pre, f0, fmi, fpl = call(
+    hfeat, pre, taps, f0, fmi, fpl = call(
         h_forward,
         (shear_set, beta_h, w_h, own),
         (base, from_left, from_right),
-        [sds((8, 8, 16, LANES), BF), sds((shears * 112, 2, 8, LANES), F32)] + [sds((1024, LANES), BF)] * 3,
+        [sds((8, 8, 16, LANES), BF), sds((shears * 64, 2, 8, LANES), F32), sds((TAPS * 160, 2, 8, LANES), F32)]
+        + [sds((1024, LANES), BF)] * 3,
         [pltpu.VMEM((shears, 8, LANES), F32), pltpu.VMEM((8, 384, LANES), F32)]
         + [pltpu.VMEM((20 * LANES, LANES), BF)] * 3
-        + [pltpu.VMEM((TAPS * 160, 2, 8, LANES), F32), pltpu.VMEM((TAPS * LANES, LANES), BF)],
+        + [pltpu.VMEM((TAPS * LANES, LANES), BF)],
         2 * 2560 * LANES * TAPS * LANES,
         GRANT[0],
     )
     moved = lax.all_to_all(hfeat, "vrow", 0, 0, tiled=True)
+    slopes, acts = call(
+        h_slopes,
+        (shear_set, beta_h),
+        (base, pre, taps),
+        [sds((shears * 112, 2, 8, LANES), F32), sds((shears * 64, 2, 8, LANES), F32)],
+        [pltpu.VMEM((shears, 8, LANES), F32)],
+        1_000_000,
+        GRANT[3],
+    )
     output, dvert, pay_v = call(
         v_both,
         (shear_set, beta_v, w_v, cotangent),
@@ -474,23 +511,34 @@
     grad = lax.all_to_all(dvert, "vrow", 0, 0, tiled=True)
     grad_right = lax.ppermute(grad[:, :REACH], "img", to_left)
     grad_left = lax.ppermute(grad[:, 8 - REACH :], "img", to_right)
-    grad_features, pay = call(
+    pay, edges_h = call(
         h_backward,
-        (shear_set, beta_h, w_h),
-        (base, pre, f0, fmi, fpl, grad, grad_left, grad_right, pay_v),
-        [sds((16, 8, 1024), BF), sds((640, LANES), F32)],
+        (shear_set,),
+        (base, slopes, acts, f0, fmi, fpl, grad, grad_left, grad_right, pay_v),
+        [sds((640, LANES), F32), pltpu.HBM((3, 1024, 384), BF)],
         [
-            pltpu.VMEM((shears, 8, LANES), F32),
             pltpu.VMEM((3 * shears * 112, 2, 8, LANES), F32),
             pltpu.VMEM((3 * 112, 2, 8, LANES), F32),
             pltpu.VMEM((3, 1024, 384), BF),
+            pltpu.VMEM((shears, 8, LANES), F32),
+            pltpu.SemaphoreType.DMA,
+        ],
+        2 * 1024 * LANES * TAPS * LANES,
+        GRANT[2],
+        (1,),
+    )
+    grad_features, finished = call(
+        h_finish,
+        (w_h, edges_h, grad),
+        (),
+        [sds((16, 8, 1024), BF), sds((40, LANES), F32)],
+        [
             pltpu.VMEM((3, 1024, LANES), F32),
             pltpu.VMEM((8, LANES, LANES), F32),
-            pltpu.VMEM((shears, 8, LANES), F32),
             pltpu.VMEM((TAPS * LANES, LANES), BF),
         ],
-        4 * 1024 * LANES * TAPS * LANES,
-        GRANT[2],
+        2 * 1024 * LANES * TAPS * LANES,
+        GRANT[4],
     )
     vmem = pl.BlockSpec(memory_space=pltpu.VMEM)
     weights = sds((TAPS, HALF, HALF), F32)
@@ -499,7 +547,7 @@
         out_shape=[weights, weights] + [sds((shears, HALF), F32)] * 2,
         in_specs=[vmem],
         out_specs=[vmem] * 4,
-    )(reduce_all(pay))
+    )(reduce_all(pay, finished))
 
     def placed(weight):
         return jnp.transpose(weight.reshape(3, 3, HALF, HALF), (2, 3, 0, 1))

time: 122 us -> 119 us (0.975)
  blocking collectives: 62.2 us -> 47.3 us
  starting transfers between devices: 14.8 us -> 21 us
  Pallas kernels: 37 us -> 40 us
  waiting for transfers between devices: 7.02 us -> 9.03 us
    all_to_all x1 -> x0, blocking collectives: 14.9 us -> none  [reduce_all(): lax.all_to_all(pay.reshape(16, 40, LANES), 'img', 0, 0, tiled=True).sum(0)]
    all_to_all x0 -> x1, starting transfers between devices: none -> 7.32 us  [reduce_all(): lax.all_to_all(pay.reshape(16, 40, LANES), 'img', 0, 0, tiled=True).sum(0)]
    all_to_all x0 -> x1, waiting for transfers between devices: none -> 3.06 us  [reduce_all(): lax.all_to_all(pay.reshape(16, 40, LANES), 'img', 0, 0, tiled=True).sum(0)]
    pallas_call x3 -> x5, Pallas kernels: 35.1 us -> 38.1 us  [call(): pl.pallas_call(kernel, out_shape=out_shapes, in_specs=specs, out_specs=[p...]
    ppermute x1, waiting for transfers between devices: 2.32 us -> 4.29 us  [per_device(): from_right = lax.ppermute(own, 'img', to_left)]
    ppermute x1, waiting for transfers between devices: 3.08 us -> 1.68 us  [per_device(): from_left = lax.ppermute(own, 'img', to_right)]
    ppermute x1, starting transfers between devices: 3.29 us -> 1.92 us  [per_device(): from_right = lax.ppermute(own, 'img', to_left)]
    ppermute x1, starting transfers between devices: 3.21 us -> 4.58 us  [per_device(): from_left = lax.ppermute(own, 'img', to_right)]
  transfers between devices with their start and end apart: 4 -> 5, of which waited for: 4 -> 3; matrix products, arithmetic and copies ran while one was open for 0% -> 0% of each run, Pallas kernels for 0% -> 8%
where the time goes in v4:
time: 119 us; the launch traced here: 118 us
  blocking collectives  47.3 us (40%)
  Pallas kernels  40 us (34%)
  starting transfers between devices  21 us (18%)
  waiting for transfers between devices  9.03 us (8%)
    pallas_call x5, Pallas kernels, call(): pl.pallas_call(kernel, out_shape=out_shapes, in_specs=specs, out_specs=[p...  38.1 us
    all_to_all x1, blocking collectives, per_device(): moved = lax.all_to_all(hfeat, 'vrow', 0, 0, tiled=True)  14.8 us
    all_to_all x1, blocking collectives, reduce_all(): lax.all_to_all(jnp.broadcast_to(part[None], (16, 40, LANES)), 'img', 0, 0...  12.8 us
    all_to_all x1, blocking collectives, per_device(): grad = lax.all_to_all(dvert, 'vrow', 0, 0, tiled=True)  10.1 us
    all_to_all x1, blocking collectives, reduce_all(): lax.all_to_all(jnp.broadcast_to(part[None], (8, 40, LANES)), 'vrow', 0, 0...  9.58 us
    all_to_all x1, starting transfers between devices, reduce_all(): lax.all_to_all(pay.reshape(16, 40, LANES), 'img', 0, 0, tiled=True).sum(0)  7.32 us
    ppermute x1, starting transfers between devices, per_device(): grad_left = lax.ppermute(grad[:, 8 - REACH:], 'img', to_right)  5.26 us
    ppermute x1, starting transfers between devices, per_device(): from_left = lax.ppermute(own, 'img', to_right)  4.58 us
  transfers between devices with their start and end apart: 5, of which 3 were waited for; matrix products, arithmetic and copies ran while one was open for 0% of the time, Pallas kernels for 8%

profile of v4, /device:TPU:1, one launch (start us, length us, event | category | flops | bytes accessed | tf_op | source)
XLA Modules:
  0.0 118.2 jit_solution(9990683147118329997)
XLA Ops:
  0.6 4.6 %collective-permute-start = (bf16[16,8,1024]{2,1,0:T(8,128)(2,1)}, bf16[16,8,1024]{2,1,0:T(8,128)(2,1)S(1)}, u32[]{:S(2)}, u32[]{:S(2)}) collective-permute-start(bf16[16,8,1024]{2,1,0:T(8,128)(2,1)} %bitcast.22), channel_id=1, source_target_pairs={{0,1},{1,2},{2,3},{3,4},{4,5},{5,6},{6,7},{7,8},{8,9},{9,10},{10,1... | collective-permute-start | bytes 786440 | tf_op jit(solution)/shard_map/ppermute | solution.py:462
  5.2 1.9 %collective-permute-start.1 = (bf16[16,8,1024]{2,1,0:T(8,128)(2,1)}, bf16[16,8,1024]{2,1,0:T(8,128)(2,1)S(1)}, u32[]{:S(2)}, u32[]{:S(2)}) collective-permute-start(bf16[16,8,1024]{2,1,0:T(8,128)(2,1)} %bitcast.23), channel_id=1, source_target_pairs={{1,0},{2,1},{3,2},{4,3},{5,4},{6,5},{7,6},{8,7},{9,8},{10,9},{11,1... | collective-permute-start | bytes 786440 | tf_op jit(solution)/shard_map/ppermute | solution.py:463
  7.2 1.7 %collective-permute-done.refs_5_ = bf16[16,8,1024]{2,1,0:T(8,128)(2,1)S(1)} collective-permute-done((bf16[16,8,1024]{2,1,0:T(8,128)(2,1)}, bf16[16,8,1024]{2,1,0:T(8,128)(2,1)S(1)}, u32[]{:S(2)}, u32[]{:S(2)}) %collective-permute-start) | collective-permute-done | bytes 262176 | tf_op jit(solution)/shard_map/ppermute | solution.py:462
  8.8 4.3 %collective-permute-done.1.refs_6_ = bf16[16,8,1024]{2,1,0:T(8,128)(2,1)S(1)} collective-permute-done((bf16[16,8,1024]{2,1,0:T(8,128)(2,1)}, bf16[16,8,1024]{2,1,0:T(8,128)(2,1)S(1)}, u32[]{:S(2)}, u32[]{:S(2)}) %collective-permute-start.1) | collective-permute-done | bytes 262176 | tf_op jit(solution)/shard_map/ppermute | solution.py:463
  13.1 8.8 %shard_map.118 = (bf16[8,8,16,128]{3,2,1,0:T(8,128)(2,1)S(1)}, f32[320,2,8,128]{3,2,1,0:T(8,128)S(1)}, f32[1440,2,8,128]{3,2,1,0:T(8,128)S(1)}, bf16[1024,128]{1...) custom-call(s32[5]{0:T(128)} %refs_0_.7, f32[5,64]{1,0:T(8,128)} %refs_1_.5, ...), custom_call_target="tpu_custom_call" | custom-call | flops 754974720 | bytes 4000000 | tf_op jit(solution)/shard_map/pallas_call | solution.py:425
  22.0 14.8 %all_to_all.25.refs_4_ = bf16[8,8,16,128]{3,2,1,0:T(8,128)(2,1)S(1)} all-to-all(bf16[8,8,16,128]{3,2,1,0:T(8,128)(2,1)S(1)} %get-tuple-element.25), channel_id=1, replica_groups=mesh['vrow'=8,'img'=16] {'vrow'}, dimensions={0} | all-to-all | bytes 524288 | tf_op jit(solution)/shard_map/all_to_all | solution.py:480
  36.8 12.3 %shard_map.119 = (bf16[2,8,8192]{2,1,0:T(8,128)(2,1)}, bf16[8,8,16,128]{3,2,1,0:T(8,128)(2,1)S(1)}, f32[320,128]{1,0:T(8,128)S(1)}) custom-call(s32[5]{0:T(128)} %refs_0_.7, f32[5,64]{1,0:T(8,128)} %refs_1_.4, bf16[9,64,64]{2,1,0:T(8,128)(2,1)} %bitcast.26, bf16[2,8,8192]{2,1,0:T(8,128)(2,1)} %refs_3_.1, bf16[8,8,16,128]{3,2,1,0:T(8,128)(2,1)S(1)} %all_to_all.25.refs_4_), custom_call_target="tpu_custom_call" | custom-call | flops 905969664 | bytes 4000000 | tf_op jit(solution)/shard_map/pallas_call | solution.py:425
  49.1 10.1 %all_to_all.26.refs_7_.refs_2_ = bf16[8,8,16,128]{3,2,1,0:T(8,128)(2,1)S(1)} all-to-all(bf16[8,8,16,128]{3,2,1,0:T(8,128)(2,1)S(1)} %get-tuple-element.34), channel_id=1, replica_groups=mesh['vrow'=8,'img'=16] {'vrow'}, dimensions={0} | all-to-all | bytes 524288 | tf_op jit(solution)/shard_map/all_to_all | solution.py:511
  59.2 0.0 copy-start
  59.2 5.3 %collective-permute-start.2 = (bf16[8,3,16,128]{3,2,1,0:T(8,128)(2,1)S(1)}, bf16[8,3,16,128]{3,2,1,0:T(8,128)(2,1)S(1)}, u32[]{:S(2)}, u32[]{:S(2)}) collective-permute-start(bf16[8,3,16,128]{3,2,1,0:T(8,128)(2,1)S(1)} %get-tuple-element.45), channel_id=1, source_target_pairs={{0,1},{1,2},{2,3},{3,4},{4,5},{5,6},{6,7},{7,8},{8,9},{9,10},{10,1... | collective-permute-start | bytes 294920 | tf_op jit(solution)/shard_map/ppermute | solution.py:513
  64.4 1.9 %collective-permute-start.3 = (bf16[8,3,16,128]{3,2,1,0:T(8,128)(2,1)S(1)}, bf16[8,3,16,128]{3,2,1,0:T(8,128)(2,1)S(1)}, u32[]{:S(2)}, u32[]{:S(2)}) collective-permute-start(bf16[8,3,16,128]{3,2,1,0:T(8,128)(2,1)S(1)} %get-tuple-element.44), channel_id=1, source_target_pairs={{1,0},{2,1},{3,2},{4,3},{5,4},{6,5},{7,6},{8,7},{9,8},{10,9},{11,1... | collective-permute-start | bytes 294920 | tf_op jit(solution)/shard_map/ppermute | solution.py:512
  66.4 4.8 %shard_map.120 = (f32[560,2,8,128]{3,2,1,0:T(8,128)S(1)}, f32[320,2,8,128]{3,2,1,0:T(8,128)S(1)}) custom-call(s32[5]{0:T(128)} %refs_0_.7, f32[5,64]{1,0:T(8,128)} %refs_1_.5, s32[1]{0:T(128)} %bitcast.5.refs_4_.refs_2_.refs_1_, f32[320,2,8,128]{3,2,1,0:T(8,128)S(1)} %get-tuple-element.27.refs_3_, f32[1440,2,8,128]{3,2,1,0:T(8,128)S(1)} %get-tuple-element.28.refs_4_), custom_call_target="tpu_custom_call" | custom-call | flops 1000000 | bytes 4000000 | tf_op jit(solution)/shard_map/pallas_call | solution.py:425
  71.2 0.0 collective-permute-done.2.refs_8_
  71.2 0.0 collective-permute-done.3.refs_9_
  71.2 0.0 copy-done
  71.2 7.3 %shard_map.121 = (f32[640,128]{1,0:T(8,128)}, bf16[3,1024,384]{2,1,0:T(8,128)(2,1)}) custom-call(s32[5]{0:T(128)} %refs_0_.7, s32[1]{0:T(128)} %bitcast.5.refs_4_.refs_2_.refs_1_, f32[560,2,8,128]{3,2,1,0:T(8,128)S(1)} %get-tuple-element.29.refs_2_, f32[320,2,8,128]{3,2,1,0:T(8,128)S(1)} %get-tuple-element.30.refs_3_, ...), custom_call_target="tpu_custom_call" | custom-call | flops 301989888 | bytes 4000000 | tf_op jit(solution)/shard_map/pallas_call | solution.py:425
  78.4 7.3 %all-to-all-start.2 = ((f32[16,40,128]{2,1,0:T(8,128)}), f32[16,40,128]{2,1,0:T(8,128)S(1)}, u32[]{:S(2)}, u32[]{:S(2)}) async-start(f32[16,40,128]{2,1,0:T(8,128)} %bitcast.8), calls=%async_computation.2 | async-start | bytes 655360 | tf_op jit(solution)/shard_map/all_to_all | solution.py:450
  85.8 4.9 %shard_map.122 = (bf16[16,8,1024]{2,1,0:T(8,128)(2,1)}, f32[40,128]{1,0:T(8,128)S(1)}) custom-call(bf16[9,64,64]{2,1,0:T(8,128)(2,1)} %bitcast.19, bf16[3,1024,384]{2,1,0:T(8,128)(2,1)} %get-tuple-element.36.refs_1_, bf16[8,8,16,128]{3,2,1,0:T(8,128)(2,1)} %copy-done), custom_call_target="tpu_custom_call" | custom-call | flops 301989888 | bytes 4000000 | tf_op jit(solution)/shard_map/pallas_call | solution.py:425
  90.7 3.1 %all-to-all-done.2 = f32[16,40,128]{2,1,0:T(8,128)S(1)} async-done(((f32[16,40,128]{2,1,0:T(8,128)}), f32[16,40,128]{2,1,0:T(8,128)S(1)}, u32[]{:S(2)}, u32[]{:S(2)}) %all-to-all-start.2) | async-done | bytes 327712 | tf_op jit(solution)/shard_map/all_to_all | solution.py:450
  93.8 9.6 %all_to_all.27 = f32[8,40,128]{2,1,0:T(8,128)S(1)} all-to-all(f32[8,40,128]{2,1,0:T(8,128)S(1)} %broadcast_in_dim.4), channel_id=1, replica_groups=mesh['vrow'=8,'img'=16] {'vrow'}, dimensions={0} | all-to-all | bytes 327680 | tf_op jit(solution)/shard_map/all_to_all | solution.py:451
  103.4 12.8 %all_to_all.28 = f32[16,40,128]{2,1,0:T(8,128)} all-to-all(f32[16,40,128]{2,1,0:T(8,128)S(1)} %broadcast_in_dim.5), channel_id=1, replica_groups=mesh['vrow'=8,'img'=16] {'img'}, dimensions={0} | all-to-all | bytes 655360 | tf_op jit(solution)/shard_map/all_to_all | solution.py:452
  116.3 1.9 %shard_map.123 = (f32[9,64,64]{2,1,0:T(8,128)}, f32[9,64,64]{2,1,0:T(8,128)}, f32[5,64]{1,0:T(8,128)}, f32[5,64]{1,0:T(8,128)}) custom-call(f32[640,128]{1,0:T(8,128)} %bitcast.17), custom_call_target="tpu_custom_call" | custom-call | tf_op jit(solution)/shard_map/pallas_call | solution.py:545
  (6 shorter events, 0.1 us)
Async XLA Ops:
  0.6 8.2 %collective-permute-start = (bf16[16,8,1024]{2,1,0:T(8,128)(2,1)}, bf16[16,8,1024]{2,1,0:T(8,128)(2,1)S(1)}, u32[]{:S(2)}, u32[]{:S(2)}) collective-permute-start(bf16[16,8,1024]{2,1,0:T(8,128)(2,1)} %bitcast.22), channel_id=1, source_target_pairs={{0,1},{1,2},{2,3},{3,4},{4,5},{5,6},{6,7},{7,8},{8,9},{9,10},{10,1... | collective-permute-start | bytes 786440 | tf_op jit(solution)/shard_map/ppermute | solution.py:462
  5.2 7.9 %collective-permute-start.1 = (bf16[16,8,1024]{2,1,0:T(8,128)(2,1)}, bf16[16,8,1024]{2,1,0:T(8,128)(2,1)S(1)}, u32[]{:S(2)}, u32[]{:S(2)}) collective-permute-start(bf16[16,8,1024]{2,1,0:T(8,128)(2,1)} %bitcast.23), channel_id=1, source_target_pairs={{1,0},{2,1},{3,2},{4,3},{5,4},{6,5},{7,6},{8,7},{9,8},{10,9},{11,1... | collective-permute-start | bytes 786440 | tf_op jit(solution)/shard_map/ppermute | solution.py:463
  59.2 12.0 %copy-start = (bf16[8,8,16,128]{3,2,1,0:T(8,128)(2,1)}, bf16[8,8,16,128]{3,2,1,0:T(8,128)(2,1)S(1)}, u32[]{:S(2)}) copy-start(bf16[8,8,16,128]{3,2,1,0:T(8,128)(2,1)S(1)} %all_to_all.26.refs_7_.refs_2_) | copy-start | bytes 786436
  59.2 12.0 %collective-permute-start.2 = (bf16[8,3,16,128]{3,2,1,0:T(8,128)(2,1)S(1)}, bf16[8,3,16,128]{3,2,1,0:T(8,128)(2,1)S(1)}, u32[]{:S(2)}, u32[]{:S(2)}) collective-permute-start(bf16[8,3,16,128]{3,2,1,0:T(8,128)(2,1)S(1)} %get-tuple-element.45), channel_id=1, source_target_pairs={{0,1},{1,2},{2,3},{3,4},{4,5},{5,6},{6,7},{7,8},{8,9},{9,10},{10,1... | collective-permute-start | bytes 294920 | tf_op jit(solution)/shard_map/ppermute | solution.py:513
  64.4 6.7 %collective-permute-start.3 = (bf16[8,3,16,128]{3,2,1,0:T(8,128)(2,1)S(1)}, bf16[8,3,16,128]{3,2,1,0:T(8,128)(2,1)S(1)}, u32[]{:S(2)}, u32[]{:S(2)}) collective-permute-start(bf16[8,3,16,128]{3,2,1,0:T(8,128)(2,1)S(1)} %get-tuple-element.44), channel_id=1, source_target_pairs={{1,0},{2,1},{3,2},{4,3},{5,4},{6,5},{7,6},{8,7},{9,8},{10,9},{11,1... | collective-permute-start | bytes 294920 | tf_op jit(solution)/shard_map/ppermute | solution.py:512
  78.4 15.3 %all-to-all-start.2 = ((f32[16,40,128]{2,1,0:T(8,128)}), f32[16,40,128]{2,1,0:T(8,128)S(1)}, u32[]{:S(2)}, u32[]{:S(2)}) async-start(f32[16,40,128]{2,1,0:T(8,128)} %bitcast.8), calls=%async_computation.2 | async-start | bytes 655360 | tf_op jit(solution)/shard_map/all_to_all | solution.py:450

commit v5 on v4

--- a/solution.py
+++ b/solution.py
@@ -34,10 +34,12 @@
     return lanes_of(shape) < HALF
 
 
-def fill_weights(w_ref, wt_ref):
+def fill_weights(w_ref, wt_ref, scale=1.0):
     zero = jnp.zeros((HALF, HALF), BF)
     for tap in range(TAPS):
         w = w_ref[tap]
+        if scale != 1.0:
+            w = (w.astype(F32) * scale).astype(BF)
         wt_ref[pl.ds(tap * LANES, HALF), :] = jnp.concatenate([w, zero], axis=1)
         wt_ref[pl.ds(tap * LANES + HALF, HALF), :] = jnp.concatenate([zero, w], axis=1)
 
@@ -70,9 +72,10 @@
         pay_ref[pl.ds(pair * HALF, HALF), :] = value
 
 
-def gate(pre):
-    s = 0.5 * jnp.tanh(0.5 * pre) + 0.5
-    act = pre * s
+def gate(h):
+    t = jnp.tanh(h) + 1.0
+    s = 0.5 * t
+    act = h * t
     return act, s + act * (1.0 - s)
 
 
@@ -84,16 +87,16 @@
     shears = shear.shape[0]
     ready()
     spread(beta_ref, beta)
-    fill_weights(w_ref, wt)
+    fill_weights(w_ref, wt, 0.5)
     first16 = low((16, LANES))
 
-    @pl.loop(0, 16)
+    @pl.loop(0, 16, unroll=2)
     def _(y):
         for part, ref in enumerate((fl, fm, fr)):
             for q in range(8):
                 stage[q, pl.ds(y * 24 + 8 * part, 8), :] = ref[y, :, pl.ds(q * LANES, LANES)].astype(F32)
 
-    @pl.loop(0, 20)
+    @pl.loop(0, 20, unroll=4)
     def _(x):
         own = [stage[q, pl.ds(x + 2, 16, stride=24), :] for q in range(8)]
         turned = [swap(a) for a in own]
@@ -123,13 +126,13 @@
 
     half = halves()
 
-    @pl.loop(0, 64)
+    @pl.loop(0, 64, unroll=8)
     def _(n):
         q = n % 8
         branch = jnp.zeros((2, 8, LANES), F32)
         for k, (xs, pre) in enumerate(sheared_taps(shear, base, taps, half, n // 8 + REACH, q)):
             pre_ref[k * 64 + n] = pre
-            keep = (xs >= 0) & (xs < LANES)
+            keep = xs.astype(jnp.uint32) < LANES
             branch = branch + jnp.where(keep, beta[k] * gate(pre)[0], 0.0)
         own = f0[pl.ds(pl.multiple_of(n * 16 + 6 * LANES, 16), 16), :].astype(F32)
         hfeat[q, n // 8] = (own + branch.reshape(16, LANES)).astype(BF)
@@ -161,12 +164,12 @@
 
     def save(k, at, xs, pre, local):
         act, slope = gate(pre)
-        keep = (xs >= 0) & (xs < LANES)
+        keep = xs.astype(jnp.uint32) < LANES
         slopes[k * 112 + at] = jnp.where(keep, beta[k] * slope, 0.0)
         if local is not None:
             acts[k * 64 + local] = jnp.where(keep, act, 0.0)
 
-    @pl.loop(0, 64)
+    @pl.loop(0, 64, unroll=8)
     def _(n):
         vrel = half + (2 * (n % 8) - 8)
         xg = base[0] + n // 8
@@ -205,7 +208,7 @@
         for j in range(3):
             sums[j * 112 + here] = total[j]
 
-    @pl.loop(0, 64)
+    @pl.loop(0, 64, unroll=8)
     def _(n):
         x, q = n // 8, n % 8
         body(x + REACH, q, gm[q, x], True)
@@ -216,7 +219,7 @@
         body(x, q, gl[q, x], False)
         body(x + 8 + REACH, q, gr[q, x], False)
 
-    @pl.loop(0, 64)
+    @pl.loop(0, 64, unroll=8)
     def _(n):
         here = n + REACH * 8
         at = pl.ds(pl.multiple_of(n * 16, 16), 16)
@@ -254,7 +257,7 @@
 
     first16 = low((16, LANES))
 
-    @pl.loop(0, 8)
+    @pl.loop(0, 8, unroll=2)
     def _(x):
         def piece(side, q):
             if q < 0 or q > 7:
@@ -268,7 +271,7 @@
             total = gm[q, x].astype(F32) + piece(1, q) + turned
             stage[q, pl.ds(x * 16, 16), :] = total
 
-    @pl.loop(0, 16)
+    @pl.loop(0, 16, unroll=2)
     def _(y):
         for q in range(8):
             out[y, :, pl.ds(q * LANES, LANES)] = stage[q, pl.ds(y, 8, stride=16), :].astype(BF)
@@ -301,9 +304,9 @@
 
     ready()
     spread(beta_ref, beta)
-    fill_weights(w_ref, wt)
-
-    @pl.loop(0, 8)
+    fill_weights(w_ref, wt, 0.5)
+
+    @pl.loop(0, 8, unroll=2)
     def _(u):
         for x in range(8):
             own[u, pl.ds(x * 16, 16), :] = h_ref[u, x].astype(F32)
@@ -338,7 +341,7 @@
         for k in range(shears):
             d = shear[k]
             ys = jnp.full((8, LANES), y - d * (u - 4), jnp.int32)
-            keep = (ys >= 0) & (ys < 16)
+            keep = ys.astype(jnp.uint32) < 16
             has_minus, has_plus = ys >= 1, ys <= 14
             a, b = here - d, here + d
             main = mid + (taps[plane - wide + a] + taps[7 * plane + wide + b])
@@ -359,14 +362,14 @@
         outs[u, y] = own[u, pl.ds(y, 8, stride=16), :] + branch
         return shared
 
-    @pl.loop(0, 64)
+    @pl.loop(0, 64, unroll=8)
     def _(n):
         u, y = n // 8, (n % 8) * 2
         first, second = body(u, y), body(u, y + 1)
         for k in range(shears):
             blend[k] += first[k] + second[k]
 
-    @pl.loop(0, 64)
+    @pl.loop(0, 64, unroll=4)
     def _(n):
         here = (n // 8 + 1) * wide + REACH + (n % 8) * 2
         at = pl.ds(pl.multiple_of(n * 16, 16), 16)
@@ -386,12 +389,12 @@
 
     pack_grads([mm(fv[...], edges[:, pl.ds(side * 384, 384)], TN) for side in range(3)], blend, pay)
 
-    @pl.loop(0, 4)
-    def _(n):
-        rows = pl.ds(pl.multiple_of(n * 256, 256), 256)
-        back = mm(edges[rows, :], wt[...], NN).reshape(2, LANES, LANES)
-        for e in range(2):
-            u = 2 * n + e
+    @pl.loop(0, 2)
+    def _(n):
+        rows = pl.ds(pl.multiple_of(n * 512, 512), 512)
+        back = 2.0 * mm(edges[rows, :], wt[...], NN).reshape(4, LANES, LANES)
+        for e in range(4):
+            u = 4 * n + e
             own[u] = grads[u].reshape(LANES, LANES) + back[e]
             for x in range(8):
                 dvert[u, x] = own[u, pl.ds(x, 16, stride=8), :].astype(BF)

time: 119 us -> 113 us (0.950)
  Pallas kernels: 40 us -> 33.1 us
    pallas_call x5, Pallas kernels: 38.1 us -> 31.2 us  [call(): pl.pallas_call(kernel, out_shape=out_shapes, in_specs=specs, out_specs=[p...]
  transfers between devices with their start and end apart: 5 -> 5, of which waited for: 3 -> 4; matrix products, arithmetic and copies ran while one was open for 0% -> 0% of each run, Pallas kernels for 8% -> 7%
where the time goes in v5:
time: 113 us; the launch traced here: 112 us
  blocking collectives  47.3 us (42%)
  Pallas kernels  33.1 us (29%)
  starting transfers between devices  21.1 us (19%)
  waiting for transfers between devices  9.66 us (9%)
    pallas_call x5, Pallas kernels, call(): pl.pallas_call(kernel, out_shape=out_shapes, in_specs=specs, out_specs=[p...  31.2 us
    all_to_all x1, blocking collectives, per_device(): moved = lax.all_to_all(hfeat, 'vrow', 0, 0, tiled=True)  14.8 us
    all_to_all x1, blocking collectives, reduce_all(): lax.all_to_all(jnp.broadcast_to(part[None], (16, 40, LANES)), 'img', 0, 0...  12.8 us
    all_to_all x1, blocking collectives, per_device(): grad = lax.all_to_all(dvert, 'vrow', 0, 0, tiled=True)  10.1 us
    all_to_all x1, blocking collectives, reduce_all(): lax.all_to_all(jnp.broadcast_to(part[None], (8, 40, LANES)), 'vrow', 0, 0...  9.58 us
    all_to_all x1, starting transfers between devices, reduce_all(): lax.all_to_all(pay.reshape(16, 40, LANES), 'img', 0, 0, tiled=True).sum(0)  7.4 us
    ppermute x1, starting transfers between devices, per_device(): grad_left = lax.ppermute(grad[:, 8 - REACH:], 'img', to_right)  5.26 us
    ppermute x1, starting transfers between devices, per_device(): from_left = lax.ppermute(own, 'img', to_right)  4.58 us
  transfers between devices with their start and end apart: 5, of which 4 were waited for; matrix products, arithmetic and copies ran while one was open for 0% of the time, Pallas kernels for 7%

profile of v5, /device:TPU:1, one launch (start us, length us, event | category | flops | bytes accessed | tf_op | source)
XLA Modules:
  0.0 112.0 jit_solution(4037878377506788784)
XLA Ops:
  0.6 4.6 %collective-permute-start = (bf16[16,8,1024]{2,1,0:T(8,128)(2,1)}, bf16[16,8,1024]{2,1,0:T(8,128)(2,1)S(1)}, u32[]{:S(2)}, u32[]{:S(2)}) collective-permute-start(bf16[16,8,1024]{2,1,0:T(8,128)(2,1)} %bitcast.22), channel_id=1, source_target_pairs={{0,1},{1,2},{2,3},{3,4},{4,5},{5,6},{6,7},{7,8},{8,9},{9,10},{10,1... | collective-permute-start | bytes 786440 | tf_op jit(solution)/shard_map/ppermute | solution.py:465
  5.2 1.9 %collective-permute-start.1 = (bf16[16,8,1024]{2,1,0:T(8,128)(2,1)}, bf16[16,8,1024]{2,1,0:T(8,128)(2,1)S(1)}, u32[]{:S(2)}, u32[]{:S(2)}) collective-permute-start(bf16[16,8,1024]{2,1,0:T(8,128)(2,1)} %bitcast.23), channel_id=1, source_target_pairs={{1,0},{2,1},{3,2},{4,3},{5,4},{6,5},{7,6},{8,7},{9,8},{10,9},{11,1... | collective-permute-start | bytes 786440 | tf_op jit(solution)/shard_map/ppermute | solution.py:466
  7.2 1.7 %collective-permute-done.refs_5_ = bf16[16,8,1024]{2,1,0:T(8,128)(2,1)S(1)} collective-permute-done((bf16[16,8,1024]{2,1,0:T(8,128)(2,1)}, bf16[16,8,1024]{2,1,0:T(8,128)(2,1)S(1)}, u32[]{:S(2)}, u32[]{:S(2)}) %collective-permute-start) | collective-permute-done | bytes 262176 | tf_op jit(solution)/shard_map/ppermute | solution.py:465
  8.8 4.3 %collective-permute-done.1.refs_6_ = bf16[16,8,1024]{2,1,0:T(8,128)(2,1)S(1)} collective-permute-done((bf16[16,8,1024]{2,1,0:T(8,128)(2,1)}, bf16[16,8,1024]{2,1,0:T(8,128)(2,1)S(1)}, u32[]{:S(2)}, u32[]{:S(2)}) %collective-permute-start.1) | collective-permute-done | bytes 262176 | tf_op jit(solution)/shard_map/ppermute | solution.py:466
  13.1 6.2 %shard_map.118 = (bf16[8,8,16,128]{3,2,1,0:T(8,128)(2,1)S(1)}, f32[320,2,8,128]{3,2,1,0:T(8,128)S(1)}, f32[1440,2,8,128]{3,2,1,0:T(8,128)S(1)}, bf16[1024,128]{1...) custom-call(s32[5]{0:T(128)} %refs_0_.7, f32[5,64]{1,0:T(8,128)} %refs_1_.5, ...), custom_call_target="tpu_custom_call" | custom-call | flops 754974720 | bytes 4000000 | tf_op jit(solution)/shard_map/pallas_call | solution.py:428
  19.4 14.8 %all_to_all.25.refs_4_ = bf16[8,8,16,128]{3,2,1,0:T(8,128)(2,1)S(1)} all-to-all(bf16[8,8,16,128]{3,2,1,0:T(8,128)(2,1)S(1)} %get-tuple-element.25), channel_id=1, replica_groups=mesh['vrow'=8,'img'=16] {'vrow'}, dimensions={0} | all-to-all | bytes 524288 | tf_op jit(solution)/shard_map/all_to_all | solution.py:483
  34.2 10.7 %shard_map.119 = (bf16[2,8,8192]{2,1,0:T(8,128)(2,1)}, bf16[8,8,16,128]{3,2,1,0:T(8,128)(2,1)S(1)}, f32[320,128]{1,0:T(8,128)S(1)}) custom-call(s32[5]{0:T(128)} %refs_0_.7, f32[5,64]{1,0:T(8,128)} %refs_1_.4, bf16[9,64,64]{2,1,0:T(8,128)(2,1)} %bitcast.26, bf16[2,8,8192]{2,1,0:T(8,128)(2,1)} %refs_3_.1, bf16[8,8,16,128]{3,2,1,0:T(8,128)(2,1)S(1)} %all_to_all.25.refs_4_), custom_call_target="tpu_custom_call" | custom-call | flops 905969664 | bytes 4000000 | tf_op jit(solution)/shard_map/pallas_call | solution.py:428
  44.9 10.1 %all_to_all.26.refs_7_.refs_2_ = bf16[8,8,16,128]{3,2,1,0:T(8,128)(2,1)S(1)} all-to-all(bf16[8,8,16,128]{3,2,1,0:T(8,128)(2,1)S(1)} %get-tuple-element.34), channel_id=1, replica_groups=mesh['vrow'=8,'img'=16] {'vrow'}, dimensions={0} | all-to-all | bytes 524288 | tf_op jit(solution)/shard_map/all_to_all | solution.py:514
  54.9 0.0 copy-start
  54.9 5.3 %collective-permute-start.2 = (bf16[8,3,16,128]{3,2,1,0:T(8,128)(2,1)S(1)}, bf16[8,3,16,128]{3,2,1,0:T(8,128)(2,1)S(1)}, u32[]{:S(2)}, u32[]{:S(2)}) collective-permute-start(bf16[8,3,16,128]{3,2,1,0:T(8,128)(2,1)S(1)} %get-tuple-element.45), channel_id=1, source_target_pairs={{0,1},{1,2},{2,3},{3,4},{4,5},{5,6},{6,7},{7,8},{8,9},{9,10},{10,1... | collective-permute-start | bytes 294920 | tf_op jit(solution)/shard_map/ppermute | solution.py:516
  60.2 1.9 %collective-permute-start.3 = (bf16[8,3,16,128]{3,2,1,0:T(8,128)(2,1)S(1)}, bf16[8,3,16,128]{3,2,1,0:T(8,128)(2,1)S(1)}, u32[]{:S(2)}, u32[]{:S(2)}) collective-permute-start(bf16[8,3,16,128]{3,2,1,0:T(8,128)(2,1)S(1)} %get-tuple-element.44), channel_id=1, source_target_pairs={{1,0},{2,1},{3,2},{4,3},{5,4},{6,5},{7,6},{8,7},{9,8},{10,9},{11,1... | collective-permute-start | bytes 294920 | tf_op jit(solution)/shard_map/ppermute | solution.py:515
  62.1 3.8 %shard_map.120 = (f32[560,2,8,128]{3,2,1,0:T(8,128)S(1)}, f32[320,2,8,128]{3,2,1,0:T(8,128)S(1)}) custom-call(s32[5]{0:T(128)} %refs_0_.7, f32[5,64]{1,0:T(8,128)} %refs_1_.5, s32[1]{0:T(128)} %bitcast.5.refs_4_.refs_2_.refs_1_, f32[320,2,8,128]{3,2,1,0:T(8,128)S(1)} %get-tuple-element.27.refs_3_, f32[1440,2,8,128]{3,2,1,0:T(8,128)S(1)} %get-tuple-element.28.refs_4_), custom_call_target="tpu_custom_call" | custom-call | flops 1000000 | bytes 4000000 | tf_op jit(solution)/shard_map/pallas_call | solution.py:428
  65.9 0.0 collective-permute-done.2.refs_8_
  65.9 0.2 collective-permute-done.3.refs_9_
  66.1 0.0 copy-done
  66.1 6.0 %shard_map.121 = (f32[640,128]{1,0:T(8,128)}, bf16[3,1024,384]{2,1,0:T(8,128)(2,1)}) custom-call(s32[5]{0:T(128)} %refs_0_.7, s32[1]{0:T(128)} %bitcast.5.refs_4_.refs_2_.refs_1_, f32[560,2,8,128]{3,2,1,0:T(8,128)S(1)} %get-tuple-element.29.refs_2_, f32[320,2,8,128]{3,2,1,0:T(8,128)S(1)} %get-tuple-element.30.refs_3_, ...), custom_call_target="tpu_custom_call" | custom-call | flops 301989888 | bytes 4000000 | tf_op jit(solution)/shard_map/pallas_call | solution.py:428
  72.2 7.4 %all-to-all-start.2 = ((f32[16,40,128]{2,1,0:T(8,128)}), f32[16,40,128]{2,1,0:T(8,128)S(1)}, u32[]{:S(2)}, u32[]{:S(2)}) async-start(f32[16,40,128]{2,1,0:T(8,128)} %bitcast.8), calls=%async_computation.2 | async-start | bytes 655360 | tf_op jit(solution)/shard_map/all_to_all | solution.py:453
  79.6 4.5 %shard_map.122 = (bf16[16,8,1024]{2,1,0:T(8,128)(2,1)}, f32[40,128]{1,0:T(8,128)S(1)}) custom-call(bf16[9,64,64]{2,1,0:T(8,128)(2,1)} %bitcast.19, bf16[3,1024,384]{2,1,0:T(8,128)(2,1)} %get-tuple-element.36.refs_1_, bf16[8,8,16,128]{3,2,1,0:T(8,128)(2,1)} %copy-done), custom_call_target="tpu_custom_call" | custom-call | flops 301989888 | bytes 4000000 | tf_op jit(solution)/shard_map/pallas_call | solution.py:428
  84.1 3.5 %all-to-all-done.2 = f32[16,40,128]{2,1,0:T(8,128)S(1)} async-done(((f32[16,40,128]{2,1,0:T(8,128)}), f32[16,40,128]{2,1,0:T(8,128)S(1)}, u32[]{:S(2)}, u32[]{:S(2)}) %all-to-all-start.2) | async-done | bytes 327712 | tf_op jit(solution)/shard_map/all_to_all | solution.py:453
  87.6 9.6 %all_to_all.27 = f32[8,40,128]{2,1,0:T(8,128)S(1)} all-to-all(f32[8,40,128]{2,1,0:T(8,128)S(1)} %broadcast_in_dim.4), channel_id=1, replica_groups=mesh['vrow'=8,'img'=16] {'vrow'}, dimensions={0} | all-to-all | bytes 327680 | tf_op jit(solution)/shard_map/all_to_all | solution.py:454
  97.2 12.8 %all_to_all.28 = f32[16,40,128]{2,1,0:T(8,128)} all-to-all(f32[16,40,128]{2,1,0:T(8,128)S(1)} %broadcast_in_dim.5), channel_id=1, replica_groups=mesh['vrow'=8,'img'=16] {'img'}, dimensions={0} | all-to-all | bytes 655360 | tf_op jit(solution)/shard_map/all_to_all | solution.py:455
  110.1 1.9 %shard_map.123 = (f32[9,64,64]{2,1,0:T(8,128)}, f32[9,64,64]{2,1,0:T(8,128)}, f32[5,64]{1,0:T(8,128)}, f32[5,64]{1,0:T(8,128)}) custom-call(f32[640,128]{1,0:T(8,128)} %bitcast.17), custom_call_target="tpu_custom_call" | custom-call | tf_op jit(solution)/shard_map/pallas_call | solution.py:548
  (6 shorter events, 0.1 us)
Async XLA Ops:
  0.6 8.2 %collective-permute-start = (bf16[16,8,1024]{2,1,0:T(8,128)(2,1)}, bf16[16,8,1024]{2,1,0:T(8,128)(2,1)S(1)}, u32[]{:S(2)}, u32[]{:S(2)}) collective-permute-start(bf16[16,8,1024]{2,1,0:T(8,128)(2,1)} %bitcast.22), channel_id=1, source_target_pairs={{0,1},{1,2},{2,3},{3,4},{4,5},{5,6},{6,7},{7,8},{8,9},{9,10},{10,1... | collective-permute-start | bytes 786440 | tf_op jit(solution)/shard_map/ppermute | solution.py:465
  5.2 7.9 %collective-permute-start.1 = (bf16[16,8,1024]{2,1,0:T(8,128)(2,1)}, bf16[16,8,1024]{2,1,0:T(8,128)(2,1)S(1)}, u32[]{:S(2)}, u32[]{:S(2)}) collective-permute-start(bf16[16,8,1024]{2,1,0:T(8,128)(2,1)} %bitcast.23), channel_id=1, source_target_pairs={{1,0},{2,1},{3,2},{4,3},{5,4},{6,5},{7,6},{8,7},{9,8},{10,9},{11,1... | collective-permute-start | bytes 786440 | tf_op jit(solution)/shard_map/ppermute | solution.py:466
  54.9 11.2 %copy-start = (bf16[8,8,16,128]{3,2,1,0:T(8,128)(2,1)}, bf16[8,8,16,128]{3,2,1,0:T(8,128)(2,1)S(1)}, u32[]{:S(2)}) copy-start(bf16[8,8,16,128]{3,2,1,0:T(8,128)(2,1)S(1)} %all_to_all.26.refs_7_.refs_2_) | copy-start | bytes 786436
  54.9 11.0 %collective-permute-start.2 = (bf16[8,3,16,128]{3,2,1,0:T(8,128)(2,1)S(1)}, bf16[8,3,16,128]{3,2,1,0:T(8,128)(2,1)S(1)}, u32[]{:S(2)}, u32[]{:S(2)}) collective-permute-start(bf16[8,3,16,128]{3,2,1,0:T(8,128)(2,1)S(1)} %get-tuple-element.45), channel_id=1, source_target_pairs={{0,1},{1,2},{2,3},{3,4},{4,5},{5,6},{6,7},{7,8},{8,9},{9,10},{10,1... | collective-permute-start | bytes 294920 | tf_op jit(solution)/shard_map/ppermute | solution.py:516
  60.2 5.9 %collective-permute-start.3 = (bf16[8,3,16,128]{3,2,1,0:T(8,128)(2,1)S(1)}, bf16[8,3,16,128]{3,2,1,0:T(8,128)(2,1)S(1)}, u32[]{:S(2)}, u32[]{:S(2)}) collective-permute-start(bf16[8,3,16,128]{3,2,1,0:T(8,128)(2,1)S(1)} %get-tuple-element.44), channel_id=1, source_target_pairs={{1,0},{2,1},{3,2},{4,3},{5,4},{6,5},{7,6},{8,7},{9,8},{10,9},{11,1... | collective-permute-start | bytes 294920 | tf_op jit(solution)/shard_map/ppermute | solution.py:515
  72.2 15.4 %all-to-all-start.2 = ((f32[16,40,128]{2,1,0:T(8,128)}), f32[16,40,128]{2,1,0:T(8,128)S(1)}, u32[]{:S(2)}, u32[]{:S(2)}) async-start(f32[16,40,128]{2,1,0:T(8,128)} %bitcast.8), calls=%async_computation.2 | async-start | bytes 655360 | tf_op jit(solution)/shard_map/all_to_all | solution.py:453

commit v6 on v5

--- a/solution.py
+++ b/solution.py
@@ -5,14 +5,17 @@
 from jax.experimental.pallas import tpu as pltpu
 from jax.sharding import PartitionSpec as P
 
+
 BF = jnp.bfloat16
 F32 = jnp.float32
 LANES = 128
 HALF = 64
 TAPS = 9
 REACH = 3
+WIDE = 8 + 2 * REACH
+PLANE = WIDE * 8
 MIB = 1024 * 1024
-GRANT = (26, 36, 34, 26, 16)
+GRANT = (26, 36, 34, 20, 12)
 NT = (((1,), (1,)), ((), ()))
 NN = (((1,), (0,)), ((), ()))
 TN = (((0,), (0,)), ((), ()))
@@ -83,7 +86,7 @@
     return (lanes_of((1, 8, LANES)) >= HALF).astype(jnp.int32)
 
 
-def h_forward(ready, shear, beta_ref, w_ref, fm, base, fl, fr, hfeat, pre_ref, taps, f0_out, fm_out, fp_out, beta, stage, f0, fmi, fpl, wt):
+def h_forward(ready, shear, beta_ref, w_ref, fm, base, fl, fr, hfeat, pre_ref, f0, fmi, fpl, beta, stage, taps, wt):
     shears = shear.shape[0]
     ready()
     spread(beta_ref, beta)
@@ -96,9 +99,9 @@
             for q in range(8):
                 stage[q, pl.ds(y * 24 + 8 * part, 8), :] = ref[y, :, pl.ds(q * LANES, LANES)].astype(F32)
 
-    @pl.loop(0, 20, unroll=4)
+    @pl.loop(0, WIDE, unroll=2)
     def _(x):
-        own = [stage[q, pl.ds(x + 2, 16, stride=24), :] for q in range(8)]
+        own = [stage[q, pl.ds(x + 8 - REACH, 16, stride=24), :] for q in range(8)]
         turned = [swap(a) for a in own]
         zero = jnp.zeros((16, LANES), F32)
         moved = [
@@ -111,154 +114,115 @@
             fmi[at, :] = moved[q]
             fpl[at, :] = moved[q + 1]
 
-    @pl.loop(0, 5)
-    def _(n):
-        at = pl.ds(pl.multiple_of(n * 512, 512), 512)
+    @pl.loop(0, 4)
+    def _(n):
+        at = pl.ds(pl.multiple_of(n * 448, 448), 448)
         for side, ref in enumerate((fmi, f0, fpl)):
             product = mm(ref[at, :], wt[pl.ds(side * 384, 384), :], NT)
             for j in range(3):
-                part = product[:, j * LANES : (j + 1) * LANES].reshape(32, 2, 8, LANES)
-                taps[pl.ds((3 * side + j) * 160 + n * 32, 32)] = part
-
-    f0_out[...] = f0[pl.ds(6 * LANES, 1024), :]
-    fm_out[...] = fmi[pl.ds(6 * LANES, 1024), :]
-    fp_out[...] = fpl[pl.ds(6 * LANES, 1024), :]
+                part = product[:, j * LANES : (j + 1) * LANES].reshape(28, 2, 8, LANES)
+                taps[pl.ds((3 * side + j) * PLANE + n * 28, 28)] = part
 
     half = halves()
 
     @pl.loop(0, 64, unroll=8)
     def _(n):
         q = n % 8
+        here = n + REACH * 8
+        vrel = half + (2 * q - 8)
+        xg = base[0] + n // 8
+        mid = taps[4 * PLANE + here]
+        left = taps[3 * PLANE - 8 + here]
+        right = taps[5 * PLANE + 8 + here]
         branch = jnp.zeros((2, 8, LANES), F32)
-        for k, (xs, pre) in enumerate(sheared_taps(shear, base, taps, half, n // 8 + REACH, q)):
+        for k in range(shears):
+            d = shear[k]
+            xs = xg - d * vrel
+            a, b = here - d * 8, here + d * 8
+            main = mid + (taps[PLANE + a] + taps[7 * PLANE + b])
+            minus = left + (taps[a - 8] + taps[6 * PLANE - 8 + b])
+            plus = right + (taps[2 * PLANE + 8 + a] + taps[8 * PLANE + 8 + b])
+            pre = main + jnp.where(xs >= 1, minus, 0.0) + jnp.where(xs <= LANES - 2, plus, 0.0)
             pre_ref[k * 64 + n] = pre
             keep = xs.astype(jnp.uint32) < LANES
             branch = branch + jnp.where(keep, beta[k] * gate(pre)[0], 0.0)
-        own = f0[pl.ds(pl.multiple_of(n * 16 + 6 * LANES, 16), 16), :].astype(F32)
+        own = f0[pl.ds(pl.multiple_of(here * 16, 16), 16), :].astype(F32)
         hfeat[q, n // 8] = (own + branch.reshape(16, LANES)).astype(BF)
 
 
-def sheared_taps(shear, base, taps, half, xe, q):
-    here = (xe + 3) * 8 + q
-    vrel = half + (2 * q - 8)
-    xg = base[0] + xe - REACH
-    mid = taps[4 * 160 + here]
-    left = taps[3 * 160 - 8 + here]
-    right = taps[5 * 160 + 8 + here]
-    found = []
-    for k in range(shear.shape[0]):
-        d = shear[k]
-        xs = xg - d * vrel
-        a, b = here - d * 8, here + d * 8
-        main = mid + (taps[160 + a] + taps[7 * 160 + b])
-        minus = left + (taps[a - 8] + taps[6 * 160 - 8 + b])
-        plus = right + (taps[2 * 160 + 8 + a] + taps[8 * 160 + 8 + b])
-        found.append((xs, main + jnp.where(xs >= 1, minus, 0.0) + jnp.where(xs <= LANES - 2, plus, 0.0)))
-    return found
-
-
-def h_slopes(ready, shear, beta_ref, base, pre_ref, taps, slopes, acts, beta):
+def h_backward(ready, shear, beta_ref, base, pre_ref, f0, fmi, fpl, gm, pay_v, pay, out0, out1, out2, beta, dps, sums, edges, blend, edges_sem):
+    shears = shear.shape[0]
     ready()
     spread(beta_ref, beta)
     half = halves()
-
-    def save(k, at, xs, pre, local):
-        act, slope = gate(pre)
-        keep = xs.astype(jnp.uint32) < LANES
-        slopes[k * 112 + at] = jnp.where(keep, beta[k] * slope, 0.0)
-        if local is not None:
-            acts[k * 64 + local] = jnp.where(keep, act, 0.0)
+    blend[...] = jnp.zeros(blend.shape, F32)
+    for gap in range(3 * shears + 1):
+        dps[pl.ds(gap * PLANE, 48)] = jnp.zeros((48, 2, 8, LANES), F32)
+    for gap in range(4):
+        sums[pl.ds(gap * 96, 32)] = jnp.zeros((32, 2, 8, LANES), F32)
 
     @pl.loop(0, 64, unroll=8)
     def _(n):
-        vrel = half + (2 * (n % 8) - 8)
-        xg = base[0] + n // 8
-        for k in range(shear.shape[0]):
-            save(k, n + REACH * 8, xg - shear[k] * vrel, pre_ref[k * 64 + n], n)
-
-    @pl.loop(0, 24)
-    def _(n):
-        for xe in (n // 8, n // 8 + 8 + REACH):
-            for k, (xs, pre) in enumerate(sheared_taps(shear, base, taps, half, xe, n % 8)):
-                save(k, xe * 8 + n % 8, xs, pre, None)
-
-
-def h_backward(ready, shear, base, slopes, acts, f0, fmi, fpl, gm, gl, gr, pay_v, pay, edges_out, dps, sums, edges, blend, edges_sem):
-    shears = shear.shape[0]
-    step = shears * 112
-    ready()
-    half = halves()
-    blend[...] = jnp.zeros(blend.shape, F32)
-
-    def body(xe, q, g, local):
-        here = xe * 8 + q
-        g = g.astype(F32).reshape(2, 8, LANES)
+        x, q = n // 8, n % 8
+        g = gm[q, x].astype(F32).reshape(2, 8, LANES)
         vrel = half + (2 * q - 8)
-        xg = base[0] + xe - REACH
+        xg = base[0] + x
         total = [jnp.zeros((2, 8, LANES), F32) for _ in range(3)]
         for k in range(shears):
             xs = xg - shear[k] * vrel
-            dp = (slopes[k * 112 + here] * g).astype(BF).astype(F32)
+            act, slope = gate(pre_ref[k * 64 + n])
+            gk = jnp.where(xs.astype(jnp.uint32) < LANES, g, 0.0)
+            dp = (beta[k] * gk * slope).astype(BF).astype(F32)
             parts = (jnp.where(xs >= 1, dp, 0.0), dp, jnp.where(xs <= LANES - 2, dp, 0.0))
             for j in range(3):
-                dps[j * step + k * 112 + here] = parts[j]
+                dps[(j * shears + k) * PLANE + 48 + n] = parts[j]
                 total[j] = total[j] + parts[j]
-            if local:
-                blend[k] += jnp.sum(g * acts[k * 64 - REACH * 8 + here], axis=0)
+            blend[k] += jnp.sum(gk * act, axis=0)
         for j in range(3):
-            sums[j * 112 + here] = total[j]
-
-    @pl.loop(0, 64, unroll=8)
-    def _(n):
-        x, q = n // 8, n % 8
-        body(x + REACH, q, gm[q, x], True)
-
-    @pl.loop(0, 24)
-    def _(n):
-        x, q = n // 8, n % 8
-        body(x, q, gl[q, x], False)
-        body(x + 8 + REACH, q, gr[q, x], False)
-
-    @pl.loop(0, 64, unroll=8)
-    def _(n):
-        here = n + REACH * 8
+            sums[j * 96 + 32 + n] = total[j]
+
+    @pl.loop(0, WIDE * 8, unroll=8)
+    def _(n):
         at = pl.ds(pl.multiple_of(n * 16, 16), 16)
         below = [jnp.zeros((2, 8, LANES), F32) for _ in range(3)]
         above = [jnp.zeros((2, 8, LANES), F32) for _ in range(3)]
         for k in range(shears):
             d = shear[k]
-            up, down = here + d * 8, here - d * 8
-            for j in range(3):
-                below[j] = below[j] + dps[j * step + k * 112 - (j - 1) * 8 + up]
-                above[j] = above[j] + dps[j * step + k * 112 - (j - 1) * 8 + down]
+            up, down = n + d * 8, n - d * 8
+            for j in range(3):
+                offset = (j * shears + k) * PLANE + 48 - REACH * 8 - (j - 1) * 8
+                below[j] = below[j] + dps[offset + up]
+                above[j] = above[j] + dps[offset + down]
         for j in range(3):
             lanes = pl.ds(j * LANES, LANES)
-            edges[0, at, lanes] = below[j].reshape(16, LANES).astype(BF)
-            edges[1, at, lanes] = sums[j * 112 - (j - 1) * 8 + here].reshape(16, LANES).astype(BF)
-            edges[2, at, lanes] = above[j].reshape(16, LANES).astype(BF)
-
-    copy = pltpu.make_async_copy(edges, edges_out, edges_sem)
-    copy.start()
+            middle = sums[j * 96 + 32 - REACH * 8 - (j - 1) * 8 + n]
+            for side, value in enumerate((below[j], middle, above[j])):
+                edges[side, at, lanes] = value.reshape(16, LANES).astype(BF)
+
+    copies = [pltpu.make_async_copy(edges.at[i], out, edges_sem.at[i]) for i, out in enumerate((out0, out1, out2))]
+    for copy in copies:
+        copy.start()
     pack_grads([mm(ref[...], edges[side], TN) for side, ref in enumerate((fmi, f0, fpl))], blend, pay)
     pay[pl.ds(5 * HALF, 5 * HALF), :] = pay_v[...]
-    copy.wait()
-
-
-def h_finish(ready, w_ref, edges, gm, out, token, dfs, stage, wt):
+    for copy in copies:
+        copy.wait()
+
+
+def h_inputs(ready, w_ref, edges0, edges1, edges2, own, to_left, to_right, token, dfs, wt):
     token[...] = jnp.zeros(token.shape, F32)
-    ready()
+    ready(0)
     fill_weights(w_ref, wt)
-
-    @pl.loop(0, 4)
-    def _(x):
-        at = pl.ds(pl.multiple_of(x * 256, 256), 256)
-        for side in range(3):
-            dfs[side, at, :] = mm(edges[side, at, :], wt[pl.ds(side * 384, 384), :], NN)
+    for side, edges in enumerate((edges0, edges1, edges2)):
+        ready(side + 1)
+
+        @pl.loop(0, 4)
+        def _(n):
+            at = pl.ds(pl.multiple_of(n * 448, 448), 448)
+            dfs[side, at, :] = mm(edges[at, :], wt[pl.ds(side * 384, 384), :], NN)
 
     first16 = low((16, LANES))
 
-    @pl.loop(0, 8, unroll=2)
-    def _(x):
+    def column(x, out, at):
         def piece(side, q):
             if q < 0 or q > 7:
                 return jnp.zeros((16, LANES), F32)
@@ -267,8 +231,26 @@
         for q in range(8):
             upper = piece(0, q) + piece(2, q - 1)
             lower = piece(0, q + 1) + piece(2, q)
-            turned = swap(jnp.where(first16, lower, upper))
-            total = gm[q, x].astype(F32) + piece(1, q) + turned
+            out[at, q] = piece(1, q) + swap(jnp.where(first16, lower, upper))
+
+    for x in range(REACH):
+        column(x, to_left, x)
+        column(x + 8 + REACH, to_right, x)
+
+    @pl.loop(0, 8)
+    def _(x):
+        column(x + REACH, own, x)
+
+
+def h_finish(ready, own, gm, from_left, from_right, out, stage):
+    ready()
+    for x in range(8):
+        for q in range(8):
+            total = gm[q, x].astype(F32) + own[x, q]
+            if x < REACH:
+                total = total + from_left[x, q]
+            if x >= 8 - REACH:
+                total = total + from_right[x - 8 + REACH, q]
             stage[q, pl.ds(x * 16, 16), :] = total
 
     @pl.loop(0, 16, unroll=2)
@@ -419,9 +401,9 @@
         for copy in copies:
             copy.start()
 
-        def ready():
-            for copy in copies:
-                copy.wait()
+        def ready(*which):
+            for i in which or range(count):
+                copies[i].wait()
 
         body(ready, *targets, *others)
 
@@ -450,12 +432,14 @@
 
 
 def reduce_all(pay, zero):
-    part = lax.all_to_all(pay.reshape(16, 40, LANES), "img", 0, 0, tiled=True).sum(0) + zero
-    part = lax.all_to_all(jnp.broadcast_to(part[None], (8, 40, LANES)), "vrow", 0, 0, tiled=True).sum(0)
-    return lax.all_to_all(jnp.broadcast_to(part[None], (16, 40, LANES)), "img", 0, 0, tiled=True).reshape(640, LANES)
-
-
-def per_device(features, weight_h, weight_v, beta_h, beta_v, shear_set, cotangent):
+    part = lax.all_to_all(pay.reshape(16, 40, LANES), "img", 0, 0, tiled=True)
+    part = jnp.broadcast_to((part.sum(0) + zero)[None], (8, 40, LANES))
+    part = lax.all_to_all(part, "vrow", 0, 0, tiled=True)
+    part = jnp.broadcast_to(part.sum(0)[None], (16, 40, LANES))
+    return lax.all_to_all(part, "img", 0, 0, tiled=True).reshape(640, LANES)
+
+
+def whole_step(features, weight_h, weight_v, beta_h, beta_v, shear_set, cotangent):
     shears = shear_set.shape[0]
     img = lax.axis_size("img")
     sds = jax.ShapeDtypeStruct
@@ -468,28 +452,21 @@
     w_h = jnp.transpose(weight_h, (2, 3, 0, 1)).reshape(TAPS, HALF, HALF)
     w_v = jnp.transpose(weight_v, (2, 3, 0, 1)).reshape(TAPS, HALF, HALF)
 
-    hfeat, pre, taps, f0, fmi, fpl = call(
+    hfeat, pre, f0, fmi, fpl = call(
         h_forward,
         (shear_set, beta_h, w_h, own),
         (base, from_left, from_right),
-        [sds((8, 8, 16, LANES), BF), sds((shears * 64, 2, 8, LANES), F32), sds((TAPS * 160, 2, 8, LANES), F32)]
-        + [sds((1024, LANES), BF)] * 3,
-        [pltpu.VMEM((shears, 8, LANES), F32), pltpu.VMEM((8, 384, LANES), F32)]
-        + [pltpu.VMEM((20 * LANES, LANES), BF)] * 3
-        + [pltpu.VMEM((TAPS * LANES, LANES), BF)],
-        2 * 2560 * LANES * TAPS * LANES,
+        [sds((8, 8, 16, LANES), BF), sds((shears * 64, 2, 8, LANES), F32)] + [sds((WIDE * LANES, LANES), BF)] * 3,
+        [
+            pltpu.VMEM((shears, 8, LANES), F32),
+            pltpu.VMEM((8, 384, LANES), F32),
+            pltpu.VMEM((TAPS * PLANE, 2, 8, LANES), F32),
+            pltpu.VMEM((TAPS * LANES, LANES), BF),
+        ],
+        2 * WIDE * LANES * LANES * TAPS * LANES,
         GRANT[0],
     )
     moved = lax.all_to_all(hfeat, "vrow", 0, 0, tiled=True)
-    slopes, acts = call(
-        h_slopes,
-        (shear_set, beta_h),
-        (base, pre, taps),
-        [sds((shears * 112, 2, 8, LANES), F32), sds((shears * 64, 2, 8, LANES), F32)],
-        [pltpu.VMEM((shears, 8, LANES), F32)],
-        1_000_000,
-        GRANT[3],
-    )
     output, dvert, pay_v = call(
         v_both,
         (shear_set, beta_v, w_v, cotangent),
@@ -512,35 +489,41 @@
         GRANT[1],
     )
     grad = lax.all_to_all(dvert, "vrow", 0, 0, tiled=True)
-    grad_right = lax.ppermute(grad[:, :REACH], "img", to_left)
-    grad_left = lax.ppermute(grad[:, 8 - REACH :], "img", to_right)
-    pay, edges_h = call(
+    pay, *edges_h = call(
         h_backward,
-        (shear_set,),
-        (base, slopes, acts, f0, fmi, fpl, grad, grad_left, grad_right, pay_v),
-        [sds((640, LANES), F32), pltpu.HBM((3, 1024, 384), BF)],
+        (shear_set, beta_h),
+        (base, pre, f0, fmi, fpl, grad, pay_v),
+        [sds((640, LANES), F32)] + [pltpu.HBM((WIDE * LANES, 384), BF)] * 3,
         [
-            pltpu.VMEM((3 * shears * 112, 2, 8, LANES), F32),
-            pltpu.VMEM((3 * 112, 2, 8, LANES), F32),
-            pltpu.VMEM((3, 1024, 384), BF),
             pltpu.VMEM((shears, 8, LANES), F32),
-            pltpu.SemaphoreType.DMA,
+            pltpu.VMEM((3 * shears * PLANE + 48, 2, 8, LANES), F32),
+            pltpu.VMEM((3 * 96 + 32, 2, 8, LANES), F32),
+            pltpu.VMEM((3, WIDE * LANES, 384), BF),
+            pltpu.VMEM((shears, 8, LANES), F32),
+            pltpu.SemaphoreType.DMA((3,)),
         ],
-        2 * 1024 * LANES * TAPS * LANES,
+        2 * WIDE * LANES * LANES * TAPS * LANES,
         GRANT[2],
-        (1,),
+        (1, 2, 3),
     )
-    grad_features, finished = call(
+    back, halo_left, halo_right, inputs_done = call(
+        h_inputs,
+        (w_h, *edges_h),
+        (),
+        [pltpu.HBM((8, 8, 16, LANES), F32)] + [pltpu.HBM((REACH, 8, 16, LANES), F32)] * 2 + [sds((40, LANES), F32)],
+        [pltpu.VMEM((3, WIDE * LANES, LANES), F32), pltpu.VMEM((TAPS * LANES, LANES), BF)],
+        2 * WIDE * LANES * LANES * TAPS * LANES,
+        GRANT[3],
+    )
+    halo_from_right = lax.ppermute(halo_left, "img", to_left)
+    halo_from_left = lax.ppermute(halo_right, "img", to_right)
+    (grad_features,) = call(
         h_finish,
-        (w_h, edges_h, grad),
-        (),
-        [sds((16, 8, 1024), BF), sds((40, LANES), F32)],
-        [
-            pltpu.VMEM((3, 1024, LANES), F32),
-            pltpu.VMEM((8, LANES, LANES), F32),
-            pltpu.VMEM((TAPS * LANES, LANES), BF),
-        ],
-        2 * 1024 * LANES * TAPS * LANES,
+        (back, grad),
+        (halo_from_left, halo_from_right),
+        [sds((16, 8, 1024), BF)],
+        [pltpu.VMEM((8, LANES, LANES), F32)],
+        1_000_000,
         GRANT[4],
     )
     vmem = pl.BlockSpec(memory_space=pltpu.VMEM)
@@ -550,7 +533,8 @@
         out_shape=[weights, weights] + [sds((shears, HALF), F32)] * 2,
         in_specs=[vmem],
         out_specs=[vmem] * 4,
-    )(reduce_all(pay, finished))
+        compiler_params=pltpu.CompilerParams(vmem_limit_bytes=6 * MIB),
+    )(reduce_all(pay, inputs_done))
 
     def placed(weight):
         return jnp.transpose(weight.reshape(3, 3, HALF, HALF), (2, 3, 0, 1))
@@ -561,7 +545,7 @@
 def solution(mesh):
     placed = (P("vrow", None, "img", None), P(), P(), P(), P(), P(), P("vrow", "img", None))
     return jax.shard_map(
-        per_device,
+        whole_step,
         mesh=mesh,
         in_specs=placed,
         out_specs=(P("vrow", "img", None), P("vrow", None, "img", None), P(), P(), P(), P()),

time: 113 us -> 109 us (0.965)
  blocking collectives: 47.3 us -> 34.9 us
  starting transfers between devices: 21.1 us -> 25.8 us
  waiting for transfers between devices: 9.66 us -> 12.2 us
    all_to_all x4 -> x3, blocking collectives: 47.3 us -> 34.9 us  [the longest x1 14.8 us: whole_step(): moved = lax.all_to_all(hfeat, 'vrow', 0, 0, tiled=True)]
    all_to_all x1 -> x2, starting transfers between devices: 7.4 us -> 13.8 us  [the longest x1 8.65 us: reduce_all(): part = lax.all_to_all(pay.reshape(16, 40, LANES), 'img', 0, 0, tiled=True)]
    ppermute x4, waiting for transfers between devices: 6.16 us -> 10.5 us  [the longest x1 3.08 us: whole_step(): from_left = lax.ppermute(own, 'img', to_right)]
    all_to_all x1 -> x2, waiting for transfers between devices: 3.5 us -> 1.75 us  [the longest x1 1.75 us: reduce_all(): part = lax.all_to_all(pay.reshape(16, 40, LANES), 'img', 0, 0, tiled=True)]
    ppermute x4, starting transfers between devices: 13.7 us -> 12 us  [the longest x1 3.55 us: whole_step(): halo_from_left = lax.ppermute(halo_right, 'img', to_right)]
    pallas_call x5, Pallas kernels: 31.2 us -> 32.5 us  [call(): pl.pallas_call(kernel, out_shape=out_shapes, in_specs=specs, out_specs=[p...]
  transfers between devices with their start and end apart: 5 -> 6, of which waited for: 4 -> 5; matrix products, arithmetic and copies ran while one was open for 0% -> 0% of each run, Pallas kernels for 7% -> 8%
where the time goes in v6:
time: 109 us; the launch traced here: 108 us
  blocking collectives  34.9 us (32%)
  Pallas kernels  33.4 us (31%)
  starting transfers between devices  25.8 us (24%)
  waiting for transfers between devices  12.2 us (11%)
    pallas_call x5, Pallas kernels, call(): pl.pallas_call(kernel, out_shape=out_shapes, in_specs=specs, out_specs=[p...  32.5 us
    all_to_all x1, blocking collectives, whole_step(): moved = lax.all_to_all(hfeat, 'vrow', 0, 0, tiled=True)  14.8 us
    all_to_all x1, blocking collectives, whole_step(): grad = lax.all_to_all(dvert, 'vrow', 0, 0, tiled=True)  10.1 us
    all_to_all x1, blocking collectives, reduce_all(): part = lax.all_to_all(part, 'vrow', 0, 0, tiled=True)  10 us
    all_to_all x1, starting transfers between devices, reduce_all(): part = lax.all_to_all(pay.reshape(16, 40, LANES), 'img', 0, 0, tiled=True)  8.65 us
    all_to_all x1, starting transfers between devices, reduce_all(): return lax.all_to_all(part, 'img', 0, 0, tiled=True).reshape(640, LANES)  5.16 us
    ppermute x1, starting transfers between devices, whole_step(): halo_from_left = lax.ppermute(halo_right, 'img', to_right)  3.55 us
    ppermute x1, starting transfers between devices, whole_step(): from_right = lax.ppermute(own, 'img', to_left)  3.29 us
  transfers between devices with their start and end apart: 6, of which 5 were waited for; matrix products, arithmetic and copies ran while one was open for 0% of the time, Pallas kernels for 8%

profile of v6, /device:TPU:1, one launch (start us, length us, event | category | flops | bytes accessed | tf_op | source)
XLA Modules:
  0.0 107.9 jit_solution(4555203379371053812)
XLA Ops:
  0.6 3.3 %collective-permute-start.1 = (bf16[16,8,1024]{2,1,0:T(8,128)(2,1)}, bf16[16,8,1024]{2,1,0:T(8,128)(2,1)S(1)}, u32[]{:S(2)}, u32[]{:S(2)}) collective-permute-start(bf16[16,8,1024]{2,1,0:T(8,128)(2,1)} %bitcast.22), channel_id=1, source_target_pairs={{1,0},{2,1},{3,2},{4,3},{5,4},{6,5},{7,6},{8,7},{9,8},{10,9},{11,1... | collective-permute-start | bytes 786440 | tf_op jit(solution)/shard_map/ppermute | solution.py:450
  3.9 3.2 %collective-permute-start = (bf16[16,8,1024]{2,1,0:T(8,128)(2,1)}, bf16[16,8,1024]{2,1,0:T(8,128)(2,1)S(1)}, u32[]{:S(2)}, u32[]{:S(2)}) collective-permute-start(bf16[16,8,1024]{2,1,0:T(8,128)(2,1)} %bitcast.23), channel_id=1, source_target_pairs={{0,1},{1,2},{2,3},{3,4},{4,5},{5,6},{6,7},{7,8},{8,9},{9,10},{10,1... | collective-permute-start | bytes 786440 | tf_op jit(solution)/shard_map/ppermute | solution.py:449
  7.2 2.3 %collective-permute-done.1.refs_6_ = bf16[16,8,1024]{2,1,0:T(8,128)(2,1)S(1)} collective-permute-done((bf16[16,8,1024]{2,1,0:T(8,128)(2,1)}, bf16[16,8,1024]{2,1,0:T(8,128)(2,1)S(1)}, u32[]{:S(2)}, u32[]{:S(2)}) %collective-permute-start.1) | collective-permute-done | bytes 262176 | tf_op jit(solution)/shard_map/ppermute | solution.py:450
  9.5 3.1 %collective-permute-done.refs_5_ = bf16[16,8,1024]{2,1,0:T(8,128)(2,1)S(1)} collective-permute-done((bf16[16,8,1024]{2,1,0:T(8,128)(2,1)}, bf16[16,8,1024]{2,1,0:T(8,128)(2,1)S(1)}, u32[]{:S(2)}, u32[]{:S(2)}) %collective-permute-start) | collective-permute-done | bytes 262176 | tf_op jit(solution)/shard_map/ppermute | solution.py:449
  12.6 5.7 %shard_map.118 = (bf16[8,8,16,128]{3,2,1,0:T(8,128)(2,1)S(1)}, f32[320,2,8,128]{3,2,1,0:T(8,128)S(1)}, bf16[1792,128]{1,0:T(8,128)(2,1)S(1)}, bf16[1792,128]{1,0:T(8,128)(2,1)S(1)}, bf16[1792,128]{1,0:T(8,128)(2,1)S(1)}) custom-call(s32[5]{0:T(128)} %refs_0_.5, f32[5,64]{1,0:T(8,128)} %refs_1_.5, bf16[9,64,64]{2,1,0:T(8,128)(2,1)} %bitcast.18, ...), custom_call_target="tpu_custom_call" | custom-call | flops 528482304 | bytes 4000000 | tf_op jit(solution)/shard_map/pallas_call | solution.py:410
  18.3 14.8 %all_to_all.25.refs_4_ = bf16[8,8,16,128]{3,2,1,0:T(8,128)(2,1)S(1)} all-to-all(bf16[8,8,16,128]{3,2,1,0:T(8,128)(2,1)S(1)} %get-tuple-element.26), channel_id=1, replica_groups=mesh['vrow'=8,'img'=16] {'vrow'}, dimensions={0} | all-to-all | bytes 524288 | tf_op jit(solution)/shard_map/all_to_all | solution.py:469
  33.1 10.7 %shard_map.119 = (bf16[2,8,8192]{2,1,0:T(8,128)(2,1)}, bf16[8,8,16,128]{3,2,1,0:T(8,128)(2,1)S(1)}, f32[320,128]{1,0:T(8,128)S(1)}) custom-call(s32[5]{0:T(128)} %refs_0_.5, f32[5,64]{1,0:T(8,128)} %refs_1_.4, bf16[9,64,64]{2,1,0:T(8,128)(2,1)} %bitcast.25, bf16[2,8,8192]{2,1,0:T(8,128)(2,1)} %refs_3_.1, bf16[8,8,16,128]{3,2,1,0:T(8,128)(2,1)S(1)} %all_to_all.25.refs_4_), custom_call_target="tpu_custom_call" | custom-call | flops 905969664 | bytes 4000000 | tf_op jit(solution)/shard_map/pallas_call | solution.py:410
  43.8 10.1 %all_to_all.26.refs_7_.refs_1_ = bf16[8,8,16,128]{3,2,1,0:T(8,128)(2,1)S(1)} all-to-all(bf16[8,8,16,128]{3,2,1,0:T(8,128)(2,1)S(1)} %get-tuple-element.32), channel_id=1, replica_groups=mesh['vrow'=8,'img'=16] {'vrow'}, dimensions={0} | all-to-all | bytes 524288 | tf_op jit(solution)/shard_map/all_to_all | solution.py:491
  53.8 0.0 copy-start
  53.8 7.8 %shard_map.120 = (f32[640,128]{1,0:T(8,128)}, bf16[1792,384]{1,0:T(8,128)(2,1)}, bf16[1792,384]{1,0:T(8,128)(2,1)}, bf16[1792,384]{1,0:T(8,128)(2,1)}) custom-call(s32[5]{0:T(128)} %refs_0_.5, f32[5,64]{1,0:T(8,128)} %refs_1_.5, s32[1]{0:T(128)} %bitcast.5.refs_4_.refs_2_, f32[320,2,8,128]{3,2,1,0:T(8,128)S(1)} %get-tuple-element.28.refs_3_, ...), custom_call_target="tpu_custom_call" | custom-call | flops 528482304 | bytes 4000000 | tf_op jit(solution)/shard_map/pallas_call | solution.py:410
  61.6 0.0 copy-done
  61.6 8.7 %all-to-all-start.2 = ((f32[16,40,128]{2,1,0:T(8,128)}), f32[16,40,128]{2,1,0:T(8,128)S(1)}, u32[]{:S(2)}, u32[]{:S(2)}) async-start(f32[16,40,128]{2,1,0:T(8,128)} %bitcast.8), calls=%async_computation.2 | async-start | bytes 655360 | tf_op jit(solution)/shard_map/all_to_all | solution.py:435
  70.3 6.2 %shard_map.121 = (f32[8,8,16,128]{3,2,1,0:T(8,128)}, f32[3,8,16,128]{3,2,1,0:T(8,128)}, f32[3,8,16,128]{3,2,1,0:T(8,128)}, f32[40,128]{1,0:T(8,128)S(1)}) custom-call(bf16[9,64,64]{2,1,0:T(8,128)(2,1)} %bitcast.19, bf16[1792,384]{1,0:T(8,128)(2,1)} %get-tuple-element.34.refs_1_, bf16[1792,384]{1,0:T(8,128)(2,1)} %get-tuple-element.35.refs_2_, ...), custom_call_target="tpu_custom_call" | custom-call | flops 528482304 | bytes 4000000 | tf_op jit(solution)/shard_map/pallas_call | solution.py:410
  76.5 0.0 copy-start.2
  76.5 0.0 copy-start.1
  76.5 1.7 %all-to-all-done.2 = f32[16,40,128]{2,1,0:T(8,128)S(1)} async-done(((f32[16,40,128]{2,1,0:T(8,128)}), f32[16,40,128]{2,1,0:T(8,128)S(1)}, u32[]{:S(2)}, u32[]{:S(2)}) %all-to-all-start.2) | async-done | bytes 327712 | tf_op jit(solution)/shard_map/all_to_all | solution.py:435
  78.3 10.0 %all_to_all.27 = f32[8,40,128]{2,1,0:T(8,128)S(1)} all-to-all(f32[8,40,128]{2,1,0:T(8,128)S(1)} %broadcast_in_dim.4), channel_id=1, replica_groups=mesh['vrow'=8,'img'=16] {'vrow'}, dimensions={0} | all-to-all | bytes 327680 | tf_op jit(solution)/shard_map/all_to_all | solution.py:437
  88.4 0.8 broadcast_in_dim.5
  89.2 5.2 %all-to-all-start.4 = ((f32[16,40,128]{2,1,0:T(8,128)}), f32[16,40,128]{2,1,0:T(8,128)S(1)}, u32[]{:S(2)}, u32[]{:S(2)}) async-start(f32[16,40,128]{2,1,0:T(8,128)} %broadcast_in_dim.5), calls=%async_computation.4 | async-start | bytes 655360 | tf_op jit(solution)/shard_map/all_to_all | solution.py:439
  94.3 0.0 copy-done.2
  94.3 3.5 %collective-permute-start.2 = (f32[3,8,16,128]{3,2,1,0:T(8,128)S(1)}, f32[3,8,16,128]{3,2,1,0:T(8,128)S(1)}, u32[]{:S(2)}, u32[]{:S(2)}) collective-permute-start(f32[3,8,16,128]{3,2,1,0:T(8,128)S(1)} %copy-done.2), channel_id=1, source_target_pairs={{0,1},{1,2},{2,3},{3,4},{4,5},{5,6},{6,7},{7,8},{8,9},{9,10},{10,1... | collective-permute-start | bytes 589832 | tf_op jit(solution)/shard_map/ppermute | solution.py:519
  97.9 0.0 copy-done.1
  97.9 1.9 %collective-permute-start.3 = (f32[3,8,16,128]{3,2,1,0:T(8,128)S(1)}, f32[3,8,16,128]{3,2,1,0:T(8,128)S(1)}, u32[]{:S(2)}, u32[]{:S(2)}) collective-permute-start(f32[3,8,16,128]{3,2,1,0:T(8,128)S(1)} %copy-done.1), channel_id=1, source_target_pairs={{1,0},{2,1},{3,2},{4,3},{5,4},{6,5},{7,6},{8,7},{9,8},{10,9},{11,1... | collective-permute-start | bytes 589832 | tf_op jit(solution)/shard_map/ppermute | solution.py:518
  99.8 2.6 %collective-permute-done.2.refs_2_ = f32[3,8,16,128]{3,2,1,0:T(8,128)S(1)} collective-permute-done((f32[3,8,16,128]{3,2,1,0:T(8,128)S(1)}, f32[3,8,16,128]{3,2,1,0:T(8,128)S(1)}, u32[]{:S(2)}, u32[]{:S(2)}) %collective-permute-start.2) | collective-permute-done | bytes 196640 | tf_op jit(solution)/shard_map/ppermute | solution.py:519
  102.5 2.4 %collective-permute-done.3.refs_3_ = f32[3,8,16,128]{3,2,1,0:T(8,128)S(1)} collective-permute-done((f32[3,8,16,128]{3,2,1,0:T(8,128)S(1)}, f32[3,8,16,128]{3,2,1,0:T(8,128)S(1)}, u32[]{:S(2)}, u32[]{:S(2)}) %collective-permute-start.3) | collective-permute-done | bytes 196640 | tf_op jit(solution)/shard_map/ppermute | solution.py:518
  104.9 2.1 %shard_map.122 = bf16[16,8,1024]{2,1,0:T(8,128)(2,1)} custom-call(f32[8,8,16,128]{3,2,1,0:T(8,128)} %get-tuple-element.37.refs_0_, bf16[8,8,16,128]{3,2,1,0:T(8,128)(2,1)} %copy-done, f32[3,8,16,128]{3,2,1,0:T(8,128)S(1)} %collective-permute-done.2.refs_2_, f32[3,8,16,128]{3,2,1,0:T(8,128)S(1)} %collective-permute-done.3.refs_3_), custom_call_target="tpu_custom_call" | custom-call | flops 1000000 | bytes 4000000 | tf_op jit(solution)/shard_map/pallas_call | solution.py:410
  107.0 0.0 all-to-all-done.4
  107.0 0.9 shard_map.123
  (4 shorter events, 0.1 us)
Async XLA Ops:
  0.6 8.8 %collective-permute-start.1 = (bf16[16,8,1024]{2,1,0:T(8,128)(2,1)}, bf16[16,8,1024]{2,1,0:T(8,128)(2,1)S(1)}, u32[]{:S(2)}, u32[]{:S(2)}) collective-permute-start(bf16[16,8,1024]{2,1,0:T(8,128)(2,1)} %bitcast.22), channel_id=1, source_target_pairs={{1,0},{2,1},{3,2},{4,3},{5,4},{6,5},{7,6},{8,7},{9,8},{10,9},{11,1... | collective-permute-start | bytes 786440 | tf_op jit(solution)/shard_map/ppermute | solution.py:450
  3.9 8.6 %collective-permute-start = (bf16[16,8,1024]{2,1,0:T(8,128)(2,1)}, bf16[16,8,1024]{2,1,0:T(8,128)(2,1)S(1)}, u32[]{:S(2)}, u32[]{:S(2)}) collective-permute-start(bf16[16,8,1024]{2,1,0:T(8,128)(2,1)} %bitcast.23), channel_id=1, source_target_pairs={{0,1},{1,2},{2,3},{3,4},{4,5},{5,6},{6,7},{7,8},{8,9},{9,10},{10,1... | collective-permute-start | bytes 786440 | tf_op jit(solution)/shard_map/ppermute | solution.py:449
  53.8 7.8 %copy-start = (bf16[8,8,16,128]{3,2,1,0:T(8,128)(2,1)}, bf16[8,8,16,128]{3,2,1,0:T(8,128)(2,1)S(1)}, u32[]{:S(2)}) copy-start(bf16[8,8,16,128]{3,2,1,0:T(8,128)(2,1)S(1)} %all_to_all.26.refs_7_.refs_1_) | copy-start | bytes 786436
  61.6 16.6 %all-to-all-start.2 = ((f32[16,40,128]{2,1,0:T(8,128)}), f32[16,40,128]{2,1,0:T(8,128)S(1)}, u32[]{:S(2)}, u32[]{:S(2)}) async-start(f32[16,40,128]{2,1,0:T(8,128)} %bitcast.8), calls=%async_computation.2 | async-start | bytes 655360 | tf_op jit(solution)/shard_map/all_to_all | solution.py:435
  76.5 17.8 %copy-start.2 = (f32[3,8,16,128]{3,2,1,0:T(8,128)S(1)}, f32[3,8,16,128]{3,2,1,0:T(8,128)}, u32[]{:S(2)}) copy-start(f32[3,8,16,128]{3,2,1,0:T(8,128)} %get-tuple-element.38) | copy-start | bytes 589828
  76.5 21.4 %copy-start.1 = (f32[3,8,16,128]{3,2,1,0:T(8,128)S(1)}, f32[3,8,16,128]{3,2,1,0:T(8,128)}, u32[]{:S(2)}) copy-start(f32[3,8,16,128]{3,2,1,0:T(8,128)} %get-tuple-element.39) | copy-start | bytes 589828
  89.2 17.8 %all-to-all-start.4 = ((f32[16,40,128]{2,1,0:T(8,128)}), f32[16,40,128]{2,1,0:T(8,128)S(1)}, u32[]{:S(2)}, u32[]{:S(2)}) async-start(f32[16,40,128]{2,1,0:T(8,128)} %broadcast_in_dim.5), calls=%async_computation.4 | async-start | bytes 655360 | tf_op jit(solution)/shard_map/all_to_all | solution.py:439
  94.3 8.1 %collective-permute-start.2 = (f32[3,8,16,128]{3,2,1,0:T(8,128)S(1)}, f32[3,8,16,128]{3,2,1,0:T(8,128)S(1)}, u32[]{:S(2)}, u32[]{:S(2)}) collective-permute-start(f32[3,8,16,128]{3,2,1,0:T(8,128)S(1)} %copy-done.2), channel_id=1, source_target_pairs={{0,1},{1,2},{2,3},{3,4},{4,5},{5,6},{6,7},{7,8},{8,9},{9,10},{10,1... | collective-permute-start | bytes 589832 | tf_op jit(solution)/shard_map/ppermute | solution.py:519
  97.9 7.0 %collective-permute-start.3 = (f32[3,8,16,128]{3,2,1,0:T(8,128)S(1)}, f32[3,8,16,128]{3,2,1,0:T(8,128)S(1)}, u32[]{:S(2)}, u32[]{:S(2)}) collective-permute-start(f32[3,8,16,128]{3,2,1,0:T(8,128)S(1)} %copy-done.1), channel_id=1, source_target_pairs={{1,0},{2,1},{3,2},{4,3},{5,4},{6,5},{7,6},{8,7},{9,8},{10,9},{11,1... | collective-permute-start | bytes 589832 | tf_op jit(solution)/shard_map/ppermute | solution.py:518

commit v7 on v6

--- a/solution.py
+++ b/solution.py
@@ -95,9 +95,9 @@
 
     @pl.loop(0, 16, unroll=2)
     def _(y):
-        for part, ref in enumerate((fl, fm, fr)):
+        for start, rows, ref in ((4, 4, fl), (8, 8, fm), (16, 4, fr)):
             for q in range(8):
-                stage[q, pl.ds(y * 24 + 8 * part, 8), :] = ref[y, :, pl.ds(q * LANES, LANES)].astype(F32)
+                stage[q, pl.ds(y * 24 + start, rows), :] = ref[y, :, pl.ds(q * LANES, LANES)].astype(F32)
 
     @pl.loop(0, WIDE, unroll=2)
     def _(x):
@@ -156,13 +156,11 @@
     spread(beta_ref, beta)
     half = halves()
     blend[...] = jnp.zeros(blend.shape, F32)
-    for gap in range(3 * shears + 1):
-        dps[pl.ds(gap * PLANE, 48)] = jnp.zeros((48, 2, 8, LANES), F32)
-    for gap in range(4):
-        sums[pl.ds(gap * 96, 32)] = jnp.zeros((32, 2, 8, LANES), F32)
 
     @pl.loop(0, 64, unroll=8)
     def _(n):
+        dps[pl.ds((n // 4) * PLANE + (n % 4) * 12, 12)] = jnp.zeros((12, 2, 8, LANES), F32)
+        sums[pl.ds((n // 16) * 96 + (n % 16) * 2, 2)] = jnp.zeros((2, 2, 8, LANES), F32)
         x, q = n // 8, n % 8
         g = gm[q, x].astype(F32).reshape(2, 8, LANES)
         vrel = half + (2 * q - 8)
@@ -431,11 +429,18 @@
                 blend[...] = other[: blend.shape[0]]
 
 
+def added(parts):
+    total = parts[0]
+    for i in range(1, parts.shape[0]):
+        total = total + parts[i]
+    return total
+
+
 def reduce_all(pay, zero):
     part = lax.all_to_all(pay.reshape(16, 40, LANES), "img", 0, 0, tiled=True)
-    part = jnp.broadcast_to((part.sum(0) + zero)[None], (8, 40, LANES))
+    part = jnp.broadcast_to((added(part) + zero)[None], (8, 40, LANES))
     part = lax.all_to_all(part, "vrow", 0, 0, tiled=True)
-    part = jnp.broadcast_to(part.sum(0)[None], (16, 40, LANES))
+    part = jnp.broadcast_to(added(part)[None], (16, 40, LANES))
     return lax.all_to_all(part, "img", 0, 0, tiled=True).reshape(640, LANES)
 
 
@@ -446,8 +451,8 @@
     own = features.reshape(16, 8, 1024)
     to_right = [(i, i + 1) for i in range(img - 1)]
     to_left = [(i + 1, i) for i in range(img - 1)]
-    from_left = lax.ppermute(own, "img", to_right)
-    from_right = lax.ppermute(own, "img", to_left)
+    from_left = lax.ppermute(own[:, 4:], "img", to_right)
+    from_right = lax.ppermute(own[:, :4], "img", to_left)
     base = (lax.axis_index("img") * 8).astype(jnp.int32).reshape(1)
     w_h = jnp.transpose(weight_h, (2, 3, 0, 1)).reshape(TAPS, HALF, HALF)
     w_v = jnp.transpose(weight_v, (2, 3, 0, 1)).reshape(TAPS, HALF, HALF)

time: 109 us -> 107 us (0.982)
  waiting for transfers between devices: 12.2 us -> 9.08 us
  local copies, waits for them, and re-layouts: 0.78 us -> 1.91 us
  blocking collectives: 34.9 us -> 36 us
    ppermute x2, waiting for transfers between devices: 5.4 us -> 2.27 us  [the longest x1 1.57 us: whole_step(): from_left = lax.ppermute(own[:, 4:], 'img', to_right)]
    slice x0 -> x1, local copies, waits for them, and re-layouts: none -> 1.14 us  [whole_step(): from_right = lax.ppermute(own[:, :4], 'img', to_left)]
    all_to_all x1, blocking collectives: 10.1 us -> 11.2 us  [whole_step(): grad = lax.all_to_all(dvert, 'vrow', 0, 0, tiled=True)]
where the time goes in v7:
time: 107 us; the launch traced here: 106 us
  blocking collectives  36 us (34%)
  Pallas kernels  33.2 us (31%)
  starting transfers between devices  25.5 us (24%)
  waiting for transfers between devices  9.08 us (8%)
  local copies, waits for them, and re-layouts  1.91 us (2%)
    pallas_call x5, Pallas kernels, call(): pl.pallas_call(kernel, out_shape=out_shapes, in_specs=specs, out_specs=[p...  32.3 us
    all_to_all x1, blocking collectives, whole_step(): moved = lax.all_to_all(hfeat, 'vrow', 0, 0, tiled=True)  15.2 us
    all_to_all x1, blocking collectives, whole_step(): grad = lax.all_to_all(dvert, 'vrow', 0, 0, tiled=True)  11.2 us
    all_to_all x1, blocking collectives, reduce_all(): part = lax.all_to_all(part, 'vrow', 0, 0, tiled=True)  9.58 us
    all_to_all x1, starting transfers between devices, reduce_all(): part = lax.all_to_all(pay.reshape(16, 40, LANES), 'img', 0, 0, tiled=True)  8.25 us
    all_to_all x1, starting transfers between devices, reduce_all(): return lax.all_to_all(part, 'img', 0, 0, tiled=True).reshape(640, LANES)  5.29 us
    ppermute x1, starting transfers between devices, whole_step(): halo_from_left = lax.ppermute(halo_right, 'img', to_right)  3.54 us
    ppermute x1, starting transfers between devices, whole_step(): from_right = lax.ppermute(own[:, :4], 'img', to_left)  3.29 us
  transfers between devices with their start and end apart: 6, of which 5 were waited for; matrix products, arithmetic and copies ran while one was open for 0% of the time, Pallas kernels for 8%

profile of v7, /device:TPU:1, one launch (start us, length us, event | category | flops | bytes accessed | tf_op | source)
XLA Modules:
  0.0 106.5 jit_solution(5799778335597292266)
XLA Ops:
  0.6 1.1 %fusion.3 = (bf16[16,4,1024]{2,1,0:T(4,128)(2,1)S(1)}, bf16[16,4,1024]{2,1,0:T(4,128)(2,1)S(1)}) fusion(bf16[16,8,1024]{2,1,0:T(8,128)(2,1)} %bitcast.24), kind=kLoop, calls=%fused_computation.25 | loop fusion | bytes 524288 | tf_op jit(solution)/shard_map/slice | solution.py:455
  1.8 3.3 %collective-permute-start.1 = (bf16[16,4,1024]{2,1,0:T(4,128)(2,1)S(1)}, bf16[16,4,1024]{2,1,0:T(4,128)(2,1)S(1)}, u32[]{:S(2)}, u32[]{:S(2)}) collective-permute-start(bf16[16,4,1024]{2,1,0:T(4,128)(2,1)S(1)} %get-tuple-element.46), channel_id=1, source_target_pairs={{1,0},{2,1},{3,2},{4,3},{5,4},{6,5},{7,6},{8,7},{9,8},{10,9},{11,1... | collective-permute-start | bytes 393224 | tf_op jit(solution)/shard_map/ppermute | solution.py:455
  5.1 3.2 %collective-permute-start = (bf16[16,4,1024]{2,1,0:T(4,128)(2,1)S(1)}, bf16[16,4,1024]{2,1,0:T(4,128)(2,1)S(1)}, u32[]{:S(2)}, u32[]{:S(2)}) collective-permute-start(bf16[16,4,1024]{2,1,0:T(4,128)(2,1)S(1)} %get-tuple-element.47), channel_id=1, source_target_pairs={{0,1},{1,2},{2,3},{3,4},{4,5},{5,6},{6,7},{7,8},{8,9},{9,10},{10,1... | collective-permute-start | bytes 393224 | tf_op jit(solution)/shard_map/ppermute | solution.py:454
  8.3 0.7 collective-permute-done.1.refs_6_
  9.0 1.6 %collective-permute-done.refs_5_ = bf16[16,4,1024]{2,1,0:T(4,128)(2,1)S(1)} collective-permute-done((bf16[16,4,1024]{2,1,0:T(4,128)(2,1)S(1)}, bf16[16,4,1024]{2,1,0:T(4,128)(2,1)S(1)}, u32[]{:S(2)}, u32[]{:S(2)}) %collective-permute-start) | collective-permute-done | bytes 131104 | tf_op jit(solution)/shard_map/ppermute | solution.py:454
  10.6 5.8 %shard_map.118 = (bf16[8,8,16,128]{3,2,1,0:T(8,128)(2,1)S(1)}, f32[320,2,8,128]{3,2,1,0:T(8,128)S(1)}, bf16[1792,128]{1,0:T(8,128)(2,1)S(1)}, bf16[1792,128]{1,0:T(8,128)(2,1)S(1)}, bf16[1792,128]{1,0:T(8,128)(2,1)S(1)}) custom-call(s32[5]{0:T(128)} %refs_0_.5, f32[5,64]{1,0:T(8,128)} %refs_1_.5, bf16[9,64,64]{2,1,0:T(8,128)(2,1)} %bitcast.26, ...), custom_call_target="tpu_custom_call" | custom-call | flops 528482304 | bytes 4000000 | tf_op jit(solution)/shard_map/pallas_call | solution.py:408
  16.3 15.2 %all_to_all.25.refs_4_ = bf16[8,8,16,128]{3,2,1,0:T(8,128)(2,1)S(1)} all-to-all(bf16[8,8,16,128]{3,2,1,0:T(8,128)(2,1)S(1)} %get-tuple-element.26), channel_id=1, replica_groups=mesh['vrow'=8,'img'=16] {'vrow'}, dimensions={0} | all-to-all | bytes 524288 | tf_op jit(solution)/shard_map/all_to_all | solution.py:474
  31.6 10.7 %shard_map.119 = (bf16[2,8,8192]{2,1,0:T(8,128)(2,1)}, bf16[8,8,16,128]{3,2,1,0:T(8,128)(2,1)S(1)}, f32[320,128]{1,0:T(8,128)S(1)}) custom-call(s32[5]{0:T(128)} %refs_0_.5, f32[5,64]{1,0:T(8,128)} %refs_1_.4, bf16[9,64,64]{2,1,0:T(8,128)(2,1)} %bitcast.30, bf16[2,8,8192]{2,1,0:T(8,128)(2,1)} %refs_3_.1, bf16[8,8,16,128]{3,2,1,0:T(8,128)(2,1)S(1)} %all_to_all.25.refs_4_), custom_call_target="tpu_custom_call" | custom-call | flops 905969664 | bytes 4000000 | tf_op jit(solution)/shard_map/pallas_call | solution.py:408
  42.3 11.2 %all_to_all.26.refs_7_.refs_1_ = bf16[8,8,16,128]{3,2,1,0:T(8,128)(2,1)S(1)} all-to-all(bf16[8,8,16,128]{3,2,1,0:T(8,128)(2,1)S(1)} %get-tuple-element.32), channel_id=1, replica_groups=mesh['vrow'=8,'img'=16] {'vrow'}, dimensions={0} | all-to-all | bytes 524288 | tf_op jit(solution)/shard_map/all_to_all | solution.py:496
  53.5 0.0 copy-start
  53.5 7.5 %shard_map.120 = (f32[640,128]{1,0:T(8,128)}, bf16[1792,384]{1,0:T(8,128)(2,1)}, bf16[1792,384]{1,0:T(8,128)(2,1)}, bf16[1792,384]{1,0:T(8,128)(2,1)}) custom-call(s32[5]{0:T(128)} %refs_0_.5, f32[5,64]{1,0:T(8,128)} %refs_1_.5, s32[1]{0:T(128)} %bitcast.5.refs_4_.refs_2_, f32[320,2,8,128]{3,2,1,0:T(8,128)S(1)} %get-tuple-element.28.refs_3_, ...), custom_call_target="tpu_custom_call" | custom-call | flops 528482304 | bytes 4000000 | tf_op jit(solution)/shard_map/pallas_call | solution.py:408
  61.0 0.0 copy-done
  61.0 8.3 %all-to-all-start.2 = ((f32[16,40,128]{2,1,0:T(8,128)}), f32[16,40,128]{2,1,0:T(8,128)S(1)}, u32[]{:S(2)}, u32[]{:S(2)}) async-start(f32[16,40,128]{2,1,0:T(8,128)} %bitcast.8), calls=%async_computation.2 | async-start | bytes 655360 | tf_op jit(solution)/shard_map/all_to_all | solution.py:440
  69.2 6.2 %shard_map.121 = (f32[8,8,16,128]{3,2,1,0:T(8,128)}, f32[3,8,16,128]{3,2,1,0:T(8,128)}, f32[3,8,16,128]{3,2,1,0:T(8,128)}, f32[40,128]{1,0:T(8,128)S(1)}) custom-call(bf16[9,64,64]{2,1,0:T(8,128)(2,1)} %bitcast.27, bf16[1792,384]{1,0:T(8,128)(2,1)} %get-tuple-element.34.refs_1_, bf16[1792,384]{1,0:T(8,128)(2,1)} %get-tuple-element.35.refs_2_, ...), custom_call_target="tpu_custom_call" | custom-call | flops 528482304 | bytes 4000000 | tf_op jit(solution)/shard_map/pallas_call | solution.py:408
  75.4 0.0 copy-start.2
  75.5 0.0 copy-start.1
  75.5 1.7 %all-to-all-done.2 = f32[16,40,128]{2,1,0:T(8,128)S(1)} async-done(((f32[16,40,128]{2,1,0:T(8,128)}), f32[16,40,128]{2,1,0:T(8,128)S(1)}, u32[]{:S(2)}, u32[]{:S(2)}) %all-to-all-start.2) | async-done | bytes 327712 | tf_op jit(solution)/shard_map/all_to_all | solution.py:440
  77.3 9.6 %all_to_all.27 = f32[8,40,128]{2,1,0:T(8,128)S(1)} all-to-all(f32[8,40,128]{2,1,0:T(8,128)S(1)} %broadcast_in_dim.6), channel_id=1, replica_groups=mesh['vrow'=8,'img'=16] {'vrow'}, dimensions={0} | all-to-all | bytes 327680 | tf_op jit(solution)/shard_map/all_to_all | solution.py:442
  86.9 0.7 broadcast_in_dim.16
  87.6 5.3 %all-to-all-start.4 = ((f32[16,40,128]{2,1,0:T(8,128)}), f32[16,40,128]{2,1,0:T(8,128)S(1)}, u32[]{:S(2)}, u32[]{:S(2)}) async-start(f32[16,40,128]{2,1,0:T(8,128)} %broadcast_in_dim.16), calls=%async_computation.4 | async-start | bytes 655360 | tf_op jit(solution)/shard_map/all_to_all | solution.py:444
  92.9 0.0 copy-done.2
  92.9 3.5 %collective-permute-start.2 = (f32[3,8,16,128]{3,2,1,0:T(8,128)S(1)}, f32[3,8,16,128]{3,2,1,0:T(8,128)S(1)}, u32[]{:S(2)}, u32[]{:S(2)}) collective-permute-start(f32[3,8,16,128]{3,2,1,0:T(8,128)S(1)} %copy-done.2), channel_id=1, source_target_pairs={{0,1},{1,2},{2,3},{3,4},{4,5},{5,6},{6,7},{7,8},{8,9},{9,10},{10,1... | collective-permute-start | bytes 589832 | tf_op jit(solution)/shard_map/ppermute | solution.py:524
  96.4 0.0 copy-done.1
  96.5 1.9 %collective-permute-start.3 = (f32[3,8,16,128]{3,2,1,0:T(8,128)S(1)}, f32[3,8,16,128]{3,2,1,0:T(8,128)S(1)}, u32[]{:S(2)}, u32[]{:S(2)}) collective-permute-start(f32[3,8,16,128]{3,2,1,0:T(8,128)S(1)} %copy-done.1), channel_id=1, source_target_pairs={{1,0},{2,1},{3,2},{4,3},{5,4},{6,5},{7,6},{8,7},{9,8},{10,9},{11,1... | collective-permute-start | bytes 589832 | tf_op jit(solution)/shard_map/ppermute | solution.py:523
  98.4 2.6 %collective-permute-done.2.refs_2_ = f32[3,8,16,128]{3,2,1,0:T(8,128)S(1)} collective-permute-done((f32[3,8,16,128]{3,2,1,0:T(8,128)S(1)}, f32[3,8,16,128]{3,2,1,0:T(8,128)S(1)}, u32[]{:S(2)}, u32[]{:S(2)}) %collective-permute-start.2) | collective-permute-done | bytes 196640 | tf_op jit(solution)/shard_map/ppermute | solution.py:524
  101.0 2.4 %collective-permute-done.3.refs_3_ = f32[3,8,16,128]{3,2,1,0:T(8,128)S(1)} collective-permute-done((f32[3,8,16,128]{3,2,1,0:T(8,128)S(1)}, f32[3,8,16,128]{3,2,1,0:T(8,128)S(1)}, u32[]{:S(2)}, u32[]{:S(2)}) %collective-permute-start.3) | collective-permute-done | bytes 196640 | tf_op jit(solution)/shard_map/ppermute | solution.py:523
  103.4 2.1 %shard_map.122 = bf16[16,8,1024]{2,1,0:T(8,128)(2,1)} custom-call(f32[8,8,16,128]{3,2,1,0:T(8,128)} %get-tuple-element.37.refs_0_, bf16[8,8,16,128]{3,2,1,0:T(8,128)(2,1)} %copy-done, f32[3,8,16,128]{3,2,1,0:T(8,128)S(1)} %collective-permute-done.2.refs_2_, f32[3,8,16,128]{3,2,1,0:T(8,128)S(1)} %collective-permute-done.3.refs_3_), custom_call_target="tpu_custom_call" | custom-call | flops 1000000 | bytes 4000000 | tf_op jit(solution)/shard_map/pallas_call | solution.py:408
  105.6 0.0 all-to-all-done.4
  105.6 0.9 shard_map.123
  (3 shorter events, 0.1 us)
Async XLA Ops:
  1.8 7.2 %collective-permute-start.1 = (bf16[16,4,1024]{2,1,0:T(4,128)(2,1)S(1)}, bf16[16,4,1024]{2,1,0:T(4,128)(2,1)S(1)}, u32[]{:S(2)}, u32[]{:S(2)}) collective-permute-start(bf16[16,4,1024]{2,1,0:T(4,128)(2,1)S(1)} %get-tuple-element.46), channel_id=1, source_target_pairs={{1,0},{2,1},{3,2},{4,3},{5,4},{6,5},{7,6},{8,7},{9,8},{10,9},{11,1... | collective-permute-start | bytes 393224 | tf_op jit(solution)/shard_map/ppermute | solution.py:455
  5.1 5.5 %collective-permute-start = (bf16[16,4,1024]{2,1,0:T(4,128)(2,1)S(1)}, bf16[16,4,1024]{2,1,0:T(4,128)(2,1)S(1)}, u32[]{:S(2)}, u32[]{:S(2)}) collective-permute-start(bf16[16,4,1024]{2,1,0:T(4,128)(2,1)S(1)} %get-tuple-element.47), channel_id=1, source_target_pairs={{0,1},{1,2},{2,3},{3,4},{4,5},{5,6},{6,7},{7,8},{8,9},{9,10},{10,1... | collective-permute-start | bytes 393224 | tf_op jit(solution)/shard_map/ppermute | solution.py:454
  53.5 7.5 %copy-start = (bf16[8,8,16,128]{3,2,1,0:T(8,128)(2,1)}, bf16[8,8,16,128]{3,2,1,0:T(8,128)(2,1)S(1)}, u32[]{:S(2)}) copy-start(bf16[8,8,16,128]{3,2,1,0:T(8,128)(2,1)S(1)} %all_to_all.26.refs_7_.refs_1_) | copy-start | bytes 786436
  61.0 16.2 %all-to-all-start.2 = ((f32[16,40,128]{2,1,0:T(8,128)}), f32[16,40,128]{2,1,0:T(8,128)S(1)}, u32[]{:S(2)}, u32[]{:S(2)}) async-start(f32[16,40,128]{2,1,0:T(8,128)} %bitcast.8), calls=%async_computation.2 | async-start | bytes 655360 | tf_op jit(solution)/shard_map/all_to_all | solution.py:440
  75.4 17.5 %copy-start.2 = (f32[3,8,16,128]{3,2,1,0:T(8,128)S(1)}, f32[3,8,16,128]{3,2,1,0:T(8,128)}, u32[]{:S(2)}) copy-start(f32[3,8,16,128]{3,2,1,0:T(8,128)} %get-tuple-element.38) | copy-start | bytes 589828
  75.5 21.0 %copy-start.1 = (f32[3,8,16,128]{3,2,1,0:T(8,128)S(1)}, f32[3,8,16,128]{3,2,1,0:T(8,128)}, u32[]{:S(2)}) copy-start(f32[3,8,16,128]{3,2,1,0:T(8,128)} %get-tuple-element.39) | copy-start | bytes 589828
  87.6 18.0 %all-to-all-start.4 = ((f32[16,40,128]{2,1,0:T(8,128)}), f32[16,40,128]{2,1,0:T(8,128)S(1)}, u32[]{:S(2)}, u32[]{:S(2)}) async-start(f32[16,40,128]{2,1,0:T(8,128)} %broadcast_in_dim.16), calls=%async_computation.4 | async-start | bytes 655360 | tf_op jit(solution)/shard_map/all_to_all | solution.py:444
  92.9 8.1 %collective-permute-start.2 = (f32[3,8,16,128]{3,2,1,0:T(8,128)S(1)}, f32[3,8,16,128]{3,2,1,0:T(8,128)S(1)}, u32[]{:S(2)}, u32[]{:S(2)}) collective-permute-start(f32[3,8,16,128]{3,2,1,0:T(8,128)S(1)} %copy-done.2), channel_id=1, source_target_pairs={{0,1},{1,2},{2,3},{3,4},{4,5},{5,6},{6,7},{7,8},{8,9},{9,10},{10,1... | collective-permute-start | bytes 589832 | tf_op jit(solution)/shard_map/ppermute | solution.py:524
  96.5 7.0 %collective-permute-start.3 = (f32[3,8,16,128]{3,2,1,0:T(8,128)S(1)}, f32[3,8,16,128]{3,2,1,0:T(8,128)S(1)}, u32[]{:S(2)}, u32[]{:S(2)}) collective-permute-start(f32[3,8,16,128]{3,2,1,0:T(8,128)S(1)} %copy-done.1), channel_id=1, source_target_pairs={{1,0},{2,1},{3,2},{4,3},{5,4},{6,5},{7,6},{8,7},{9,8},{10,9},{11,1... | collective-permute-start | bytes 589832 | tf_op jit(solution)/shard_map/ppermute | solution.py:523

commit v8 on v7

--- a/solution.py
+++ b/solution.py
@@ -72,7 +72,7 @@
         value = jnp.concatenate([both[:HALF], both[HALF:]], axis=1)
         if pair == 4:
             value = jnp.where(first, value, blend)
-        pay_ref[pl.ds(pair * HALF, HALF), :] = value
+        pay_ref[pl.ds(pair * HALF, HALF), :] = value.astype(pay_ref.dtype)
 
 
 def gate(h):
@@ -150,7 +150,7 @@
         hfeat[q, n // 8] = (own + branch.reshape(16, LANES)).astype(BF)
 
 
-def h_backward(ready, shear, beta_ref, base, pre_ref, f0, fmi, fpl, gm, pay_v, pay, out0, out1, out2, beta, dps, sums, edges, blend, edges_sem):
+def h_backward(ready, shear, beta_ref, base, pre_ref, f0, fmi, fpl, gm, pay_v, pay, rim0, rim1, rim2, out0, out1, out2, beta, dps, sums, edges, blend, edges_sem):
     shears = shear.shape[0]
     ready()
     spread(beta_ref, beta)
@@ -197,7 +197,12 @@
             for side, value in enumerate((below[j], middle, above[j])):
                 edges[side, at, lanes] = value.reshape(16, LANES).astype(BF)
 
-    copies = [pltpu.make_async_copy(edges.at[i], out, edges_sem.at[i]) for i, out in enumerate((out0, out1, out2))]
+    side = REACH * LANES
+    copies = []
+    for i, (rim, out) in enumerate(((rim0, out0), (rim1, out1), (rim2, out2))):
+        pieces = ((0, side, rim.at[pl.ds(0, side)]), (side + 1024, side, rim.at[pl.ds(side, side)]), (side, 1024, out))
+        for e, (start, rows, target) in enumerate(pieces):
+            copies.append(pltpu.make_async_copy(edges.at[i, pl.ds(start, rows)], target, edges_sem.at[3 * i + e]))
     for copy in copies:
         copy.start()
     pack_grads([mm(ref[...], edges[side], TN) for side, ref in enumerate((fmi, f0, fpl))], blend, pay)
@@ -206,45 +211,48 @@
         copy.wait()
 
 
-def h_inputs(ready, w_ref, edges0, edges1, edges2, own, to_left, to_right, token, dfs, wt):
-    token[...] = jnp.zeros(token.shape, F32)
+def back_through(ready, w_ref, edges, dfs, wt, chunk):
     ready(0)
     fill_weights(w_ref, wt)
-    for side, edges in enumerate((edges0, edges1, edges2)):
+    for side in range(3):
         ready(side + 1)
-
-        @pl.loop(0, 4)
-        def _(n):
-            at = pl.ds(pl.multiple_of(n * 448, 448), 448)
-            dfs[side, at, :] = mm(edges[at, :], wt[pl.ds(side * 384, 384), :], NN)
-
+        for start in range(0, dfs.shape[1], chunk):
+            rows = pl.ds(start, chunk)
+            dfs[side, rows, :] = mm(edges[side][rows, :], wt[pl.ds(side * 384, 384), :], NN)
+
+
+def column(dfs, x):
     first16 = low((16, LANES))
 
-    def column(x, out, at):
-        def piece(side, q):
-            if q < 0 or q > 7:
-                return jnp.zeros((16, LANES), F32)
-            return dfs[side, pl.ds(pl.multiple_of(x * LANES + q * 16, 16), 16), :]
-
-        for q in range(8):
-            upper = piece(0, q) + piece(2, q - 1)
-            lower = piece(0, q + 1) + piece(2, q)
-            out[at, q] = piece(1, q) + swap(jnp.where(first16, lower, upper))
-
+    def piece(side, q):
+        if q < 0 or q > 7:
+            return jnp.zeros((16, LANES), F32)
+        return dfs[side, pl.ds(pl.multiple_of(x * LANES + q * 16, 16), 16), :]
+
+    found = []
+    for q in range(8):
+        upper = piece(0, q) + piece(2, q - 1)
+        lower = piece(0, q + 1) + piece(2, q)
+        found.append(piece(1, q) + swap(jnp.where(first16, lower, upper)))
+    return found
+
+
+def h_rims(ready, w_ref, edges0, edges1, edges2, to_left, to_right, token, dfs, wt):
+    token[...] = jnp.zeros(token.shape, F32)
+    back_through(ready, w_ref, (edges0, edges1, edges2), dfs, wt, 768)
     for x in range(REACH):
-        column(x, to_left, x)
-        column(x + 8 + REACH, to_right, x)
-
-    @pl.loop(0, 8)
-    def _(x):
-        column(x + REACH, own, x)
-
-
-def h_finish(ready, own, gm, from_left, from_right, out, stage):
-    ready()
+        for q, value in enumerate(column(dfs, x)):
+            to_left[x, q] = value
+        for q, value in enumerate(column(dfs, x + REACH)):
+            to_right[x, q] = value
+
+
+def h_finish(ready, w_ref, edges0, edges1, edges2, gm, from_left, from_right, out, dfs, stage, wt):
+    back_through(ready, w_ref, (edges0, edges1, edges2), dfs, wt, 512)
+    ready(4)
     for x in range(8):
-        for q in range(8):
-            total = gm[q, x].astype(F32) + own[x, q]
+        for q, value in enumerate(column(dfs, x)):
+            total = gm[q, x].astype(F32) + value
             if x < REACH:
                 total = total + from_left[x, q]
             if x >= 8 - REACH:
@@ -438,7 +446,7 @@
 
 def reduce_all(pay, zero):
     part = lax.all_to_all(pay.reshape(16, 40, LANES), "img", 0, 0, tiled=True)
-    part = jnp.broadcast_to((added(part) + zero)[None], (8, 40, LANES))
+    part = jnp.broadcast_to((added(part.astype(F32)) + zero)[None], (8, 40, LANES))
     part = lax.all_to_all(part, "vrow", 0, 0, tiled=True)
     part = jnp.broadcast_to(added(part)[None], (16, 40, LANES))
     return lax.all_to_all(part, "img", 0, 0, tiled=True).reshape(640, LANES)
@@ -476,7 +484,7 @@
         v_both,
         (shear_set, beta_v, w_v, cotangent),
         (moved,),
-        [sds((2, 8, 8192), BF), sds((8, 8, 16, LANES), BF), sds((320, LANES), F32)],
+        [sds((2, 8, 8192), BF), sds((8, 8, 16, LANES), BF), sds((320, LANES), BF)],
         [
             pltpu.VMEM((shears, 8, LANES), F32),
             pltpu.VMEM((8, LANES, LANES), F32),
@@ -494,41 +502,41 @@
         GRANT[1],
     )
     grad = lax.all_to_all(dvert, "vrow", 0, 0, tiled=True)
-    pay, *edges_h = call(
+    pay, rim0, rim1, rim2, *edges_h = call(
         h_backward,
         (shear_set, beta_h),
         (base, pre, f0, fmi, fpl, grad, pay_v),
-        [sds((640, LANES), F32)] + [pltpu.HBM((WIDE * LANES, 384), BF)] * 3,
+        [sds((640, LANES), BF)] + [pltpu.HBM((2 * REACH * LANES, 384), BF)] * 3 + [pltpu.HBM((1024, 384), BF)] * 3,
         [
             pltpu.VMEM((shears, 8, LANES), F32),
             pltpu.VMEM((3 * shears * PLANE + 48, 2, 8, LANES), F32),
             pltpu.VMEM((3 * 96 + 32, 2, 8, LANES), F32),
             pltpu.VMEM((3, WIDE * LANES, 384), BF),
             pltpu.VMEM((shears, 8, LANES), F32),
-            pltpu.SemaphoreType.DMA((3,)),
+            pltpu.SemaphoreType.DMA((9,)),
         ],
         2 * WIDE * LANES * LANES * TAPS * LANES,
         GRANT[2],
-        (1, 2, 3),
+        (1, 2, 3, 4, 5, 6),
     )
-    back, halo_left, halo_right, inputs_done = call(
-        h_inputs,
-        (w_h, *edges_h),
+    halo_left, halo_right, rims_done = call(
+        h_rims,
+        (w_h, rim0, rim1, rim2),
         (),
-        [pltpu.HBM((8, 8, 16, LANES), F32)] + [pltpu.HBM((REACH, 8, 16, LANES), F32)] * 2 + [sds((40, LANES), F32)],
-        [pltpu.VMEM((3, WIDE * LANES, LANES), F32), pltpu.VMEM((TAPS * LANES, LANES), BF)],
-        2 * WIDE * LANES * LANES * TAPS * LANES,
+        [pltpu.HBM((REACH, 8, 16, LANES), F32)] * 2 + [sds((40, LANES), F32)],
+        [pltpu.VMEM((3, 2 * REACH * LANES, LANES), F32), pltpu.VMEM((TAPS * LANES, LANES), BF)],
+        2 * 2 * REACH * LANES * LANES * TAPS * LANES,
         GRANT[3],
     )
     halo_from_right = lax.ppermute(halo_left, "img", to_left)
     halo_from_left = lax.ppermute(halo_right, "img", to_right)
     (grad_features,) = call(
         h_finish,
-        (back, grad),
+        (w_h, *edges_h, grad),
         (halo_from_left, halo_from_right),
         [sds((16, 8, 1024), BF)],
-        [pltpu.VMEM((8, LANES, LANES), F32)],
-        1_000_000,
+        [pltpu.VMEM((3, 1024, LANES), F32), pltpu.VMEM((8, LANES, LANES), F32), pltpu.VMEM((TAPS * LANES, LANES), BF)],
+        2 * 1024 * LANES * TAPS * LANES,
         GRANT[4],
     )
     vmem = pl.BlockSpec(memory_space=pltpu.VMEM)
@@ -539,7 +547,7 @@
         in_specs=[vmem],
         out_specs=[vmem] * 4,
         compiler_params=pltpu.CompilerParams(vmem_limit_bytes=6 * MIB),
-    )(reduce_all(pay, inputs_done))
+    )(reduce_all(pay, rims_done))
 
     def placed(weight):
         return jnp.transpose(weight.reshape(3, 3, HALF, HALF), (2, 3, 0, 1))

time: 107 us -> 107 us (level)
  waiting for transfers between devices: 9.08 us -> 10.9 us
  Pallas kernels: 33.2 us -> 31.6 us
    all_to_all x1, waiting for transfers between devices: 1.74 us -> 3.39 us  [reduce_all(): part = lax.all_to_all(pay.reshape(16, 40, LANES), 'img', 0, 0, tiled=True)]
    pallas_call x5, Pallas kernels: 32.3 us -> 30.6 us  [call(): pl.pallas_call(kernel, out_shape=out_shapes, in_specs=specs, out_specs=[p...]
  transfers between devices with their start and end apart: 6 -> 6, of which waited for: 5 -> 5; matrix products, arithmetic and copies ran while one was open for 0% -> 0% of each run, Pallas kernels for 8% -> 6%
where the time goes in v8:
time: 107 us; the launch traced here: 106 us
  blocking collectives  36 us (34%)
  Pallas kernels  31.6 us (30%)
  starting transfers between devices  25.2 us (24%)
  waiting for transfers between devices  10.9 us (10%)
  local copies, waits for them, and re-layouts  1.94 us (2%)
    pallas_call x5, Pallas kernels, call(): pl.pallas_call(kernel, out_shape=out_shapes, in_specs=specs, out_specs=[p...  30.6 us
    all_to_all x1, blocking collectives, whole_step(): moved = lax.all_to_all(hfeat, 'vrow', 0, 0, tiled=True)  15.2 us
    all_to_all x1, blocking collectives, whole_step(): grad = lax.all_to_all(dvert, 'vrow', 0, 0, tiled=True)  11.2 us
    all_to_all x1, blocking collectives, reduce_all(): part = lax.all_to_all(part, 'vrow', 0, 0, tiled=True)  9.58 us
    all_to_all x1, starting transfers between devices, reduce_all(): part = lax.all_to_all(pay.reshape(16, 40, LANES), 'img', 0, 0, tiled=True)  8.26 us
    all_to_all x1, starting transfers between devices, reduce_all(): return lax.all_to_all(part, 'img', 0, 0, tiled=True).reshape(640, LANES)  5.02 us
    ppermute x1, starting transfers between devices, whole_step(): halo_from_left = lax.ppermute(halo_right, 'img', to_right)  3.53 us
    all_to_all x1, waiting for transfers between devices, reduce_all(): part = lax.all_to_all(pay.reshape(16, 40, LANES), 'img', 0, 0, tiled=True)  3.39 us
  transfers between devices with their start and end apart: 6, of which 5 were waited for; matrix products, arithmetic and copies ran while one was open for 0% of the time, Pallas kernels for 6%

profile of v8, /device:TPU:1, one launch (start us, length us, event | category | flops | bytes accessed | tf_op | source)
XLA Modules:
  0.0 106.5 jit_solution(18382741066806835678)
XLA Ops:
  0.6 1.2 %fusion.3 = (bf16[16,4,1024]{2,1,0:T(4,128)(2,1)S(1)}, bf16[16,4,1024]{2,1,0:T(4,128)(2,1)S(1)}) fusion(bf16[16,8,1024]{2,1,0:T(8,128)(2,1)} %bitcast.27), kind=kLoop, calls=%fused_computation.25 | loop fusion | bytes 524288 | tf_op jit(solution)/shard_map/slice | solution.py:463
  1.8 3.3 %collective-permute-start.1 = (bf16[16,4,1024]{2,1,0:T(4,128)(2,1)S(1)}, bf16[16,4,1024]{2,1,0:T(4,128)(2,1)S(1)}, u32[]{:S(2)}, u32[]{:S(2)}) collective-permute-start(bf16[16,4,1024]{2,1,0:T(4,128)(2,1)S(1)} %get-tuple-element.50), channel_id=1, source_target_pairs={{1,0},{2,1},{3,2},{4,3},{5,4},{6,5},{7,6},{8,7},{9,8},{10,9},{11,1... | collective-permute-start | bytes 393224 | tf_op jit(solution)/shard_map/ppermute | solution.py:463
  5.1 3.2 %collective-permute-start = (bf16[16,4,1024]{2,1,0:T(4,128)(2,1)S(1)}, bf16[16,4,1024]{2,1,0:T(4,128)(2,1)S(1)}, u32[]{:S(2)}, u32[]{:S(2)}) collective-permute-start(bf16[16,4,1024]{2,1,0:T(4,128)(2,1)S(1)} %get-tuple-element.51), channel_id=1, source_target_pairs={{0,1},{1,2},{2,3},{3,4},{4,5},{5,6},{6,7},{7,8},{8,9},{9,10},{10,1... | collective-permute-start | bytes 393224 | tf_op jit(solution)/shard_map/ppermute | solution.py:462
  8.3 0.7 collective-permute-done.1.refs_6_
  9.0 1.6 %collective-permute-done.refs_5_ = bf16[16,4,1024]{2,1,0:T(4,128)(2,1)S(1)} collective-permute-done((bf16[16,4,1024]{2,1,0:T(4,128)(2,1)S(1)}, bf16[16,4,1024]{2,1,0:T(4,128)(2,1)S(1)}, u32[]{:S(2)}, u32[]{:S(2)}) %collective-permute-start) | collective-permute-done | bytes 131104 | tf_op jit(solution)/shard_map/ppermute | solution.py:462
  10.6 5.8 %shard_map.118 = (bf16[8,8,16,128]{3,2,1,0:T(8,128)(2,1)S(1)}, f32[320,2,8,128]{3,2,1,0:T(8,128)S(1)}, bf16[1792,128]{1,0:T(8,128)(2,1)S(1)}, bf16[1792,128]{1,0:T(8,128)(2,1)S(1)}, bf16[1792,128]{1,0:T(8,128)(2,1)S(1)}) custom-call(s32[5]{0:T(128)} %refs_0_.5, f32[5,64]{1,0:T(8,128)} %refs_1_.5, bf16[9,64,64]{2,1,0:T(8,128)(2,1)} %bitcast.24, ...), custom_call_target="tpu_custom_call" | custom-call | flops 528482304 | bytes 4000000 | tf_op jit(solution)/shard_map/pallas_call | solution.py:416
  16.4 15.2 %all_to_all.25.refs_4_ = bf16[8,8,16,128]{3,2,1,0:T(8,128)(2,1)S(1)} all-to-all(bf16[8,8,16,128]{3,2,1,0:T(8,128)(2,1)S(1)} %get-tuple-element.28), channel_id=1, replica_groups=mesh['vrow'=8,'img'=16] {'vrow'}, dimensions={0} | all-to-all | bytes 524288 | tf_op jit(solution)/shard_map/all_to_all | solution.py:482
  31.6 10.7 %shard_map.119 = (bf16[2,8,8192]{2,1,0:T(8,128)(2,1)}, bf16[8,8,16,128]{3,2,1,0:T(8,128)(2,1)S(1)}, bf16[320,128]{1,0:T(8,128)(2,1)S(1)}) custom-call(s32[5]{0:T(128)} %refs_0_.5, f32[5,64]{1,0:T(8,128)} %refs_1_.4, bf16[9,64,64]{2,1,0:T(8,128)(2,1)} %bitcast.32, bf16[2,8,8192]{2,1,0:T(8,128)(2,1)} %refs_3_.1, bf16[8,8,16,128]{3,2,1,0:T(8,128)(2,1)S(1)} %all_to_all.25.refs_4_), custom_call_target="tpu_custom_call" | custom-call | flops 905969664 | bytes 4000000 | tf_op jit(solution)/shard_map/pallas_call | solution.py:416
  42.3 11.2 %all_to_all.26.refs_7_.refs_4_ = bf16[8,8,16,128]{3,2,1,0:T(8,128)(2,1)S(1)} all-to-all(bf16[8,8,16,128]{3,2,1,0:T(8,128)(2,1)S(1)} %get-tuple-element.34), channel_id=1, replica_groups=mesh['vrow'=8,'img'=16] {'vrow'}, dimensions={0} | all-to-all | bytes 524288 | tf_op jit(solution)/shard_map/all_to_all | solution.py:504
  53.5 0.0 copy-start
  53.5 7.7 %shard_map.120 = (bf16[640,128]{1,0:T(8,128)(2,1)}, bf16[768,384]{1,0:T(8,128)(2,1)}, bf16[768,384]{1,0:T(8,128)(2,1)}, bf16[768,384]{1,0:T(8,128)(2,1)}, bf16[1...) custom-call(s32[5]{0:T(128)} %refs_0_.5, f32[5,64]{1,0:T(8,128)} %refs_1_.5, ...), custom_call_target="tpu_custom_call" | custom-call | flops 528482304 | bytes 4000000 | tf_op jit(solution)/shard_map/pallas_call | solution.py:416
  61.2 8.3 %all-to-all-start.2 = ((bf16[16,40,128]{2,1,0:T(8,128)(2,1)}), bf16[16,40,128]{2,1,0:T(8,128)(2,1)S(1)}, u32[]{:S(2)}, u32[]{:S(2)}) async-start(bf16[16,40,128]{2,1,0:T(8,128)(2,1)} %bitcast.8), calls=%async_computation.2 | async-start | bytes 327680 | tf_op jit(solution)/shard_map/all_to_all | solution.py:448
  69.4 3.0 %shard_map.121 = (f32[3,8,16,128]{3,2,1,0:T(8,128)}, f32[3,8,16,128]{3,2,1,0:T(8,128)}, f32[40,128]{1,0:T(8,128)S(1)}) custom-call(bf16[9,64,64]{2,1,0:T(8,128)(2,1)} %bitcast.25, bf16[768,384]{1,0:T(8,128)(2,1)} %get-tuple-element.39.refs_1_, bf16[768,384]{1,0:T(8,128)(2,1)} %get-tuple-element.40.refs_2_, bf16[768,384]{1,0:T(8,128)(2,1)} %get-tuple-element.41.refs_3_), custom_call_target="tpu_custom_call" | custom-call | flops 226492416 | bytes 4000000 | tf_op jit(solution)/shard_map/pallas_call | solution.py:416
  72.5 0.0 copy-done
  72.5 3.4 %all-to-all-done.2 = bf16[16,40,128]{2,1,0:T(8,128)(2,1)S(1)} async-done(((bf16[16,40,128]{2,1,0:T(8,128)(2,1)}), bf16[16,40,128]{2,1,0:T(8,128)(2,1)S(1)}, u32[]{:S(2)}, u32[]{:S(2)}) %all-to-all-start.2) | async-done | bytes 163872 | tf_op jit(solution)/shard_map/all_to_all | solution.py:448
  76.0 9.6 %all_to_all.27 = f32[8,40,128]{2,1,0:T(8,128)S(1)} all-to-all(f32[8,40,128]{2,1,0:T(8,128)S(1)} %broadcast_in_dim.6), channel_id=1, replica_groups=mesh['vrow'=8,'img'=16] {'vrow'}, dimensions={0} | all-to-all | bytes 327680 | tf_op jit(solution)/shard_map/all_to_all | solution.py:450
  85.6 0.7 broadcast_in_dim.16
  86.3 5.0 %all-to-all-start.4 = ((f32[16,40,128]{2,1,0:T(8,128)}), f32[16,40,128]{2,1,0:T(8,128)S(1)}, u32[]{:S(2)}, u32[]{:S(2)}) async-start(f32[16,40,128]{2,1,0:T(8,128)} %broadcast_in_dim.16), calls=%async_computation.4 | async-start | bytes 655360 | tf_op jit(solution)/shard_map/all_to_all | solution.py:452
  91.3 3.5 %collective-permute-start.2 = (f32[3,8,16,128]{3,2,1,0:T(8,128)}, f32[3,8,16,128]{3,2,1,0:T(8,128)S(1)}, u32[]{:S(2)}, u32[]{:S(2)}) collective-permute-start(f32[3,8,16,128]{3,2,1,0:T(8,128)} %get-tuple-element.42), channel_id=1, source_target_pairs={{0,1},{1,2},{2,3},{3,4},{4,5},{5,6},{6,7},{7,8},{8,9},{9,10},{10,1... | collective-permute-start | bytes 589832 | tf_op jit(solution)/shard_map/ppermute | solution.py:532
  94.9 1.9 %collective-permute-start.3 = (f32[3,8,16,128]{3,2,1,0:T(8,128)}, f32[3,8,16,128]{3,2,1,0:T(8,128)S(1)}, u32[]{:S(2)}, u32[]{:S(2)}) collective-permute-start(f32[3,8,16,128]{3,2,1,0:T(8,128)} %get-tuple-element.43), channel_id=1, source_target_pairs={{1,0},{2,1},{3,2},{4,3},{5,4},{6,5},{7,6},{8,7},{9,8},{10,9},{11,1... | collective-permute-start | bytes 589832 | tf_op jit(solution)/shard_map/ppermute | solution.py:531
  96.8 2.8 %collective-permute-done.2.refs_5_ = f32[3,8,16,128]{3,2,1,0:T(8,128)S(1)} collective-permute-done((f32[3,8,16,128]{3,2,1,0:T(8,128)}, f32[3,8,16,128]{3,2,1,0:T(8,128)S(1)}, u32[]{:S(2)}, u32[]{:S(2)}) %collective-permute-start.2) | collective-permute-done | bytes 196640 | tf_op jit(solution)/shard_map/ppermute | solution.py:532
  99.6 2.5 %collective-permute-done.3.refs_6_ = f32[3,8,16,128]{3,2,1,0:T(8,128)S(1)} collective-permute-done((f32[3,8,16,128]{3,2,1,0:T(8,128)}, f32[3,8,16,128]{3,2,1,0:T(8,128)S(1)}, u32[]{:S(2)}, u32[]{:S(2)}) %collective-permute-start.3) | collective-permute-done | bytes 196640 | tf_op jit(solution)/shard_map/ppermute | solution.py:531
  102.1 3.5 %shard_map.122 = bf16[16,8,1024]{2,1,0:T(8,128)(2,1)} custom-call(bf16[9,64,64]{2,1,0:T(8,128)(2,1)} %bitcast.26, bf16[1024,384]{1,0:T(8,128)(2,1)} %get-tuple-element.36.refs_1_, bf16[1024,384]{1,0:T(8,128)(2,1)} %get-tuple-element.37.refs_2_, bf16[1024,384]{1,0:T(8,128)(2,1)} %get-tuple-element.38.refs_3_, bf16[8,8,16,128]{3,2,1,0:T(8,128)(2,1)} %copy-done, ...), custom_call_target="tpu_custom_call" | custom-call | flops 301989888 | bytes 4000000 | tf_op jit(solution)/shard_map/pallas_call | solution.py:416
  105.6 0.0 all-to-all-done.4
  105.6 0.9 shard_map.123
  (4 shorter events, 0.1 us)
Async XLA Ops:
  1.8 7.2 %collective-permute-start.1 = (bf16[16,4,1024]{2,1,0:T(4,128)(2,1)S(1)}, bf16[16,4,1024]{2,1,0:T(4,128)(2,1)S(1)}, u32[]{:S(2)}, u32[]{:S(2)}) collective-permute-start(bf16[16,4,1024]{2,1,0:T(4,128)(2,1)S(1)} %get-tuple-element.50), channel_id=1, source_target_pairs={{1,0},{2,1},{3,2},{4,3},{5,4},{6,5},{7,6},{8,7},{9,8},{10,9},{11,1... | collective-permute-start | bytes 393224 | tf_op jit(solution)/shard_map/ppermute | solution.py:463
  5.1 5.5 %collective-permute-start = (bf16[16,4,1024]{2,1,0:T(4,128)(2,1)S(1)}, bf16[16,4,1024]{2,1,0:T(4,128)(2,1)S(1)}, u32[]{:S(2)}, u32[]{:S(2)}) collective-permute-start(bf16[16,4,1024]{2,1,0:T(4,128)(2,1)S(1)} %get-tuple-element.51), channel_id=1, source_target_pairs={{0,1},{1,2},{2,3},{3,4},{4,5},{5,6},{6,7},{7,8},{8,9},{9,10},{10,1... | collective-permute-start | bytes 393224 | tf_op jit(solution)/shard_map/ppermute | solution.py:462
  53.5 19.0 %copy-start = (bf16[8,8,16,128]{3,2,1,0:T(8,128)(2,1)}, bf16[8,8,16,128]{3,2,1,0:T(8,128)(2,1)S(1)}, u32[]{:S(2)}) copy-start(bf16[8,8,16,128]{3,2,1,0:T(8,128)(2,1)S(1)} %all_to_all.26.refs_7_.refs_4_) | copy-start | bytes 786436
  61.2 14.7 %all-to-all-start.2 = ((bf16[16,40,128]{2,1,0:T(8,128)(2,1)}), bf16[16,40,128]{2,1,0:T(8,128)(2,1)S(1)}, u32[]{:S(2)}, u32[]{:S(2)}) async-start(bf16[16,40,128]{2,1,0:T(8,128)(2,1)} %bitcast.8), calls=%async_computation.2 | async-start | bytes 327680 | tf_op jit(solution)/shard_map/all_to_all | solution.py:448
  86.3 19.3 %all-to-all-start.4 = ((f32[16,40,128]{2,1,0:T(8,128)}), f32[16,40,128]{2,1,0:T(8,128)S(1)}, u32[]{:S(2)}, u32[]{:S(2)}) async-start(f32[16,40,128]{2,1,0:T(8,128)} %broadcast_in_dim.16), calls=%async_computation.4 | async-start | bytes 655360 | tf_op jit(solution)/shard_map/all_to_all | solution.py:452
  91.3 8.3 %collective-permute-start.2 = (f32[3,8,16,128]{3,2,1,0:T(8,128)}, f32[3,8,16,128]{3,2,1,0:T(8,128)S(1)}, u32[]{:S(2)}, u32[]{:S(2)}) collective-permute-start(f32[3,8,16,128]{3,2,1,0:T(8,128)} %get-tuple-element.42), channel_id=1, source_target_pairs={{0,1},{1,2},{2,3},{3,4},{4,5},{5,6},{6,7},{7,8},{8,9},{9,10},{10,1... | collective-permute-start | bytes 589832 | tf_op jit(solution)/shard_map/ppermute | solution.py:532
  94.9 7.2 %collective-permute-start.3 = (f32[3,8,16,128]{3,2,1,0:T(8,128)}, f32[3,8,16,128]{3,2,1,0:T(8,128)S(1)}, u32[]{:S(2)}, u32[]{:S(2)}) collective-permute-start(f32[3,8,16,128]{3,2,1,0:T(8,128)} %get-tuple-element.43), channel_id=1, source_target_pairs={{1,0},{2,1},{3,2},{4,3},{5,4},{6,5},{7,6},{8,7},{9,8},{10,9},{11,1... | collective-permute-start | bytes 589832 | tf_op jit(solution)/shard_map/ppermute | solution.py:531

commit v9 on v8

--- a/solution.py
+++ b/solution.py
@@ -357,23 +357,24 @@
         for k in range(shears):
             blend[k] += first[k] + second[k]
 
-    @pl.loop(0, 64, unroll=4)
-    def _(n):
-        here = (n // 8 + 1) * wide + REACH + (n % 8) * 2
-        at = pl.ds(pl.multiple_of(n * 16, 16), 16)
-        below = [jnp.zeros((2, 8, LANES), F32) for _ in range(3)]
-        above = [jnp.zeros((2, 8, LANES), F32) for _ in range(3)]
-        for k in range(shears):
-            d = shear[k]
-            up, down = here + d, here - d
-            for j in range(3):
-                offset = (j * shears + k) * plane - (j - 1)
-                below[j] = below[j] + dps[pl.ds(offset + wide + up, 2)]
-                above[j] = above[j] + dps[pl.ds(offset - wide + down, 2)]
-        for j in range(3):
-            middle = sums[pl.ds(j * plane - (j - 1) + here, 2)]
-            for side, value in enumerate((below[j], middle, above[j])):
-                edges[at, pl.ds((3 * side + j) * LANES, LANES)] = value.reshape(16, LANES).astype(BF)
+    @pl.loop(0, 8)
+    def _(u):
+        for step in range(8):
+            here = (u + 1) * wide + (REACH + 2 * step)
+            at = pl.ds(pl.multiple_of(u * LANES + step * 16, 16), 16)
+            below = [jnp.zeros((2, 8, LANES), F32) for _ in range(3)]
+            above = [jnp.zeros((2, 8, LANES), F32) for _ in range(3)]
+            for k in range(shears):
+                d = shear[k]
+                up, down = here + d, here - d
+                for j in range(3):
+                    offset = (j * shears + k) * plane - (j - 1)
+                    below[j] = below[j] + dps[pl.ds(offset + wide + up, 2)]
+                    above[j] = above[j] + dps[pl.ds(offset - wide + down, 2)]
+            for j in range(3):
+                middle = sums[pl.ds(j * plane - (j - 1) + here, 2)]
+                for side, value in enumerate((below[j], middle, above[j])):
+                    edges[at, pl.ds((3 * side + j) * LANES, LANES)] = value.reshape(16, LANES).astype(BF)
 
     pack_grads([mm(fv[...], edges[:, pl.ds(side * 384, 384)], TN) for side in range(3)], blend, pay)
 

time: 107 us -> 107 us (level)
  no operation moved by 1% of the time
where the time goes in v9:
time: 107 us; the launch traced here: 106 us
  blocking collectives  36 us (34%)
  Pallas kernels  31.2 us (29%)
  starting transfers between devices  25.2 us (24%)
  waiting for transfers between devices  10.9 us (10%)
  local copies, waits for them, and re-layouts  1.94 us (2%)
    pallas_call x5, Pallas kernels, call(): pl.pallas_call(kernel, out_shape=out_shapes, in_specs=specs, out_specs=[p...  30.3 us
    all_to_all x1, blocking collectives, whole_step(): moved = lax.all_to_all(hfeat, 'vrow', 0, 0, tiled=True)  15.2 us
    all_to_all x1, blocking collectives, whole_step(): grad = lax.all_to_all(dvert, 'vrow', 0, 0, tiled=True)  11.2 us
    all_to_all x1, blocking collectives, reduce_all(): part = lax.all_to_all(part, 'vrow', 0, 0, tiled=True)  9.58 us
    all_to_all x1, starting transfers between devices, reduce_all(): part = lax.all_to_all(pay.reshape(16, 40, LANES), 'img', 0, 0, tiled=True)  8.26 us
    all_to_all x1, starting transfers between devices, reduce_all(): return lax.all_to_all(part, 'img', 0, 0, tiled=True).reshape(640, LANES)  5.02 us
    ppermute x1, starting transfers between devices, whole_step(): halo_from_left = lax.ppermute(halo_right, 'img', to_right)  3.53 us
    all_to_all x1, waiting for transfers between devices, reduce_all(): part = lax.all_to_all(pay.reshape(16, 40, LANES), 'img', 0, 0, tiled=True)  3.39 us
  transfers between devices with their start and end apart: 6, of which 5 were waited for; matrix products, arithmetic and copies ran while one was open for 0% of the time, Pallas kernels for 6%

profile of v9, /device:TPU:1, one launch (start us, length us, event | category | flops | bytes accessed | tf_op | source)
XLA Modules:
  0.0 106.1 jit_solution(7372352593795708318)
XLA Ops:
  0.6 1.2 %fusion.3 = (bf16[16,4,1024]{2,1,0:T(4,128)(2,1)S(1)}, bf16[16,4,1024]{2,1,0:T(4,128)(2,1)S(1)}) fusion(bf16[16,8,1024]{2,1,0:T(8,128)(2,1)} %bitcast.27), kind=kLoop, calls=%fused_computation.25 | loop fusion | bytes 524288 | tf_op jit(solution)/shard_map/slice | solution.py:464
  1.8 3.3 %collective-permute-start.1 = (bf16[16,4,1024]{2,1,0:T(4,128)(2,1)S(1)}, bf16[16,4,1024]{2,1,0:T(4,128)(2,1)S(1)}, u32[]{:S(2)}, u32[]{:S(2)}) collective-permute-start(bf16[16,4,1024]{2,1,0:T(4,128)(2,1)S(1)} %get-tuple-element.50), channel_id=1, source_target_pairs={{1,0},{2,1},{3,2},{4,3},{5,4},{6,5},{7,6},{8,7},{9,8},{10,9},{11,1... | collective-permute-start | bytes 393224 | tf_op jit(solution)/shard_map/ppermute | solution.py:464
  5.1 3.2 %collective-permute-start = (bf16[16,4,1024]{2,1,0:T(4,128)(2,1)S(1)}, bf16[16,4,1024]{2,1,0:T(4,128)(2,1)S(1)}, u32[]{:S(2)}, u32[]{:S(2)}) collective-permute-start(bf16[16,4,1024]{2,1,0:T(4,128)(2,1)S(1)} %get-tuple-element.51), channel_id=1, source_target_pairs={{0,1},{1,2},{2,3},{3,4},{4,5},{5,6},{6,7},{7,8},{8,9},{9,10},{10,1... | collective-permute-start | bytes 393224 | tf_op jit(solution)/shard_map/ppermute | solution.py:463
  8.3 0.7 collective-permute-done.1.refs_6_
  9.0 1.6 %collective-permute-done.refs_5_ = bf16[16,4,1024]{2,1,0:T(4,128)(2,1)S(1)} collective-permute-done((bf16[16,4,1024]{2,1,0:T(4,128)(2,1)S(1)}, bf16[16,4,1024]{2,1,0:T(4,128)(2,1)S(1)}, u32[]{:S(2)}, u32[]{:S(2)}) %collective-permute-start) | collective-permute-done | bytes 131104 | tf_op jit(solution)/shard_map/ppermute | solution.py:463
  10.6 5.8 %shard_map.118 = (bf16[8,8,16,128]{3,2,1,0:T(8,128)(2,1)S(1)}, f32[320,2,8,128]{3,2,1,0:T(8,128)S(1)}, bf16[1792,128]{1,0:T(8,128)(2,1)S(1)}, bf16[1792,128]{1,0:T(8,128)(2,1)S(1)}, bf16[1792,128]{1,0:T(8,128)(2,1)S(1)}) custom-call(s32[5]{0:T(128)} %refs_0_.5, f32[5,64]{1,0:T(8,128)} %refs_1_.5, bf16[9,64,64]{2,1,0:T(8,128)(2,1)} %bitcast.24, ...), custom_call_target="tpu_custom_call" | custom-call | flops 528482304 | bytes 4000000 | tf_op jit(solution)/shard_map/pallas_call | solution.py:417
  16.4 15.2 %all_to_all.25.refs_4_ = bf16[8,8,16,128]{3,2,1,0:T(8,128)(2,1)S(1)} all-to-all(bf16[8,8,16,128]{3,2,1,0:T(8,128)(2,1)S(1)} %get-tuple-element.28), channel_id=1, replica_groups=mesh['vrow'=8,'img'=16] {'vrow'}, dimensions={0} | all-to-all | bytes 524288 | tf_op jit(solution)/shard_map/all_to_all | solution.py:483
  31.6 10.3 %shard_map.119 = (bf16[2,8,8192]{2,1,0:T(8,128)(2,1)}, bf16[8,8,16,128]{3,2,1,0:T(8,128)(2,1)S(1)}, bf16[320,128]{1,0:T(8,128)(2,1)S(1)}) custom-call(s32[5]{0:T(128)} %refs_0_.5, f32[5,64]{1,0:T(8,128)} %refs_1_.4, bf16[9,64,64]{2,1,0:T(8,128)(2,1)} %bitcast.32, bf16[2,8,8192]{2,1,0:T(8,128)(2,1)} %refs_3_.1, bf16[8,8,16,128]{3,2,1,0:T(8,128)(2,1)S(1)} %all_to_all.25.refs_4_), custom_call_target="tpu_custom_call" | custom-call | flops 905969664 | bytes 4000000 | tf_op jit(solution)/shard_map/pallas_call | solution.py:417
  41.9 11.2 %all_to_all.26.refs_7_.refs_4_ = bf16[8,8,16,128]{3,2,1,0:T(8,128)(2,1)S(1)} all-to-all(bf16[8,8,16,128]{3,2,1,0:T(8,128)(2,1)S(1)} %get-tuple-element.34), channel_id=1, replica_groups=mesh['vrow'=8,'img'=16] {'vrow'}, dimensions={0} | all-to-all | bytes 524288 | tf_op jit(solution)/shard_map/all_to_all | solution.py:505
  53.1 0.0 copy-start
  53.1 7.7 %shard_map.120 = (bf16[640,128]{1,0:T(8,128)(2,1)}, bf16[768,384]{1,0:T(8,128)(2,1)}, bf16[768,384]{1,0:T(8,128)(2,1)}, bf16[768,384]{1,0:T(8,128)(2,1)}, bf16[1...) custom-call(s32[5]{0:T(128)} %refs_0_.5, f32[5,64]{1,0:T(8,128)} %refs_1_.5, ...), custom_call_target="tpu_custom_call" | custom-call | flops 528482304 | bytes 4000000 | tf_op jit(solution)/shard_map/pallas_call | solution.py:417
  60.8 8.3 %all-to-all-start.2 = ((bf16[16,40,128]{2,1,0:T(8,128)(2,1)}), bf16[16,40,128]{2,1,0:T(8,128)(2,1)S(1)}, u32[]{:S(2)}, u32[]{:S(2)}) async-start(bf16[16,40,128]{2,1,0:T(8,128)(2,1)} %bitcast.8), calls=%async_computation.2 | async-start | bytes 327680 | tf_op jit(solution)/shard_map/all_to_all | solution.py:449
  69.1 3.0 %shard_map.121 = (f32[3,8,16,128]{3,2,1,0:T(8,128)}, f32[3,8,16,128]{3,2,1,0:T(8,128)}, f32[40,128]{1,0:T(8,128)S(1)}) custom-call(bf16[9,64,64]{2,1,0:T(8,128)(2,1)} %bitcast.25, bf16[768,384]{1,0:T(8,128)(2,1)} %get-tuple-element.39.refs_1_, bf16[768,384]{1,0:T(8,128)(2,1)} %get-tuple-element.40.refs_2_, bf16[768,384]{1,0:T(8,128)(2,1)} %get-tuple-element.41.refs_3_), custom_call_target="tpu_custom_call" | custom-call | flops 226492416 | bytes 4000000 | tf_op jit(solution)/shard_map/pallas_call | solution.py:417
  72.1 0.0 copy-done
  72.1 3.4 %all-to-all-done.2 = bf16[16,40,128]{2,1,0:T(8,128)(2,1)S(1)} async-done(((bf16[16,40,128]{2,1,0:T(8,128)(2,1)}), bf16[16,40,128]{2,1,0:T(8,128)(2,1)S(1)}, u32[]{:S(2)}, u32[]{:S(2)}) %all-to-all-start.2) | async-done | bytes 163872 | tf_op jit(solution)/shard_map/all_to_all | solution.py:449
  75.6 9.6 %all_to_all.27 = f32[8,40,128]{2,1,0:T(8,128)S(1)} all-to-all(f32[8,40,128]{2,1,0:T(8,128)S(1)} %broadcast_in_dim.6), channel_id=1, replica_groups=mesh['vrow'=8,'img'=16] {'vrow'}, dimensions={0} | all-to-all | bytes 327680 | tf_op jit(solution)/shard_map/all_to_all | solution.py:451
  85.2 0.7 broadcast_in_dim.16
  85.9 5.0 %all-to-all-start.4 = ((f32[16,40,128]{2,1,0:T(8,128)}), f32[16,40,128]{2,1,0:T(8,128)S(1)}, u32[]{:S(2)}, u32[]{:S(2)}) async-start(f32[16,40,128]{2,1,0:T(8,128)} %broadcast_in_dim.16), calls=%async_computation.4 | async-start | bytes 655360 | tf_op jit(solution)/shard_map/all_to_all | solution.py:453
  91.0 3.5 %collective-permute-start.2 = (f32[3,8,16,128]{3,2,1,0:T(8,128)}, f32[3,8,16,128]{3,2,1,0:T(8,128)S(1)}, u32[]{:S(2)}, u32[]{:S(2)}) collective-permute-start(f32[3,8,16,128]{3,2,1,0:T(8,128)} %get-tuple-element.42), channel_id=1, source_target_pairs={{0,1},{1,2},{2,3},{3,4},{4,5},{5,6},{6,7},{7,8},{8,9},{9,10},{10,1... | collective-permute-start | bytes 589832 | tf_op jit(solution)/shard_map/ppermute | solution.py:533
  94.5 1.9 %collective-permute-start.3 = (f32[3,8,16,128]{3,2,1,0:T(8,128)}, f32[3,8,16,128]{3,2,1,0:T(8,128)S(1)}, u32[]{:S(2)}, u32[]{:S(2)}) collective-permute-start(f32[3,8,16,128]{3,2,1,0:T(8,128)} %get-tuple-element.43), channel_id=1, source_target_pairs={{1,0},{2,1},{3,2},{4,3},{5,4},{6,5},{7,6},{8,7},{9,8},{10,9},{11,1... | collective-permute-start | bytes 589832 | tf_op jit(solution)/shard_map/ppermute | solution.py:532
  96.4 2.8 %collective-permute-done.2.refs_5_ = f32[3,8,16,128]{3,2,1,0:T(8,128)S(1)} collective-permute-done((f32[3,8,16,128]{3,2,1,0:T(8,128)}, f32[3,8,16,128]{3,2,1,0:T(8,128)S(1)}, u32[]{:S(2)}, u32[]{:S(2)}) %collective-permute-start.2) | collective-permute-done | bytes 196640 | tf_op jit(solution)/shard_map/ppermute | solution.py:533
  99.2 2.5 %collective-permute-done.3.refs_6_ = f32[3,8,16,128]{3,2,1,0:T(8,128)S(1)} collective-permute-done((f32[3,8,16,128]{3,2,1,0:T(8,128)}, f32[3,8,16,128]{3,2,1,0:T(8,128)S(1)}, u32[]{:S(2)}, u32[]{:S(2)}) %collective-permute-start.3) | collective-permute-done | bytes 196640 | tf_op jit(solution)/shard_map/ppermute | solution.py:532
  101.7 3.5 %shard_map.122 = bf16[16,8,1024]{2,1,0:T(8,128)(2,1)} custom-call(bf16[9,64,64]{2,1,0:T(8,128)(2,1)} %bitcast.26, bf16[1024,384]{1,0:T(8,128)(2,1)} %get-tuple-element.36.refs_1_, bf16[1024,384]{1,0:T(8,128)(2,1)} %get-tuple-element.37.refs_2_, bf16[1024,384]{1,0:T(8,128)(2,1)} %get-tuple-element.38.refs_3_, bf16[8,8,16,128]{3,2,1,0:T(8,128)(2,1)} %copy-done, ...), custom_call_target="tpu_custom_call" | custom-call | flops 301989888 | bytes 4000000 | tf_op jit(solution)/shard_map/pallas_call | solution.py:417
  105.2 0.0 all-to-all-done.4
  105.2 0.9 shard_map.123
  (4 shorter events, 0.1 us)
Async XLA Ops:
  1.8 7.2 %collective-permute-start.1 = (bf16[16,4,1024]{2,1,0:T(4,128)(2,1)S(1)}, bf16[16,4,1024]{2,1,0:T(4,128)(2,1)S(1)}, u32[]{:S(2)}, u32[]{:S(2)}) collective-permute-start(bf16[16,4,1024]{2,1,0:T(4,128)(2,1)S(1)} %get-tuple-element.50), channel_id=1, source_target_pairs={{1,0},{2,1},{3,2},{4,3},{5,4},{6,5},{7,6},{8,7},{9,8},{10,9},{11,1... | collective-permute-start | bytes 393224 | tf_op jit(solution)/shard_map/ppermute | solution.py:464
  5.1 5.5 %collective-permute-start = (bf16[16,4,1024]{2,1,0:T(4,128)(2,1)S(1)}, bf16[16,4,1024]{2,1,0:T(4,128)(2,1)S(1)}, u32[]{:S(2)}, u32[]{:S(2)}) collective-permute-start(bf16[16,4,1024]{2,1,0:T(4,128)(2,1)S(1)} %get-tuple-element.51), channel_id=1, source_target_pairs={{0,1},{1,2},{2,3},{3,4},{4,5},{5,6},{6,7},{7,8},{8,9},{9,10},{10,1... | collective-permute-start | bytes 393224 | tf_op jit(solution)/shard_map/ppermute | solution.py:463
  53.1 19.0 %copy-start = (bf16[8,8,16,128]{3,2,1,0:T(8,128)(2,1)}, bf16[8,8,16,128]{3,2,1,0:T(8,128)(2,1)S(1)}, u32[]{:S(2)}) copy-start(bf16[8,8,16,128]{3,2,1,0:T(8,128)(2,1)S(1)} %all_to_all.26.refs_7_.refs_4_) | copy-start | bytes 786436
  60.8 14.7 %all-to-all-start.2 = ((bf16[16,40,128]{2,1,0:T(8,128)(2,1)}), bf16[16,40,128]{2,1,0:T(8,128)(2,1)S(1)}, u32[]{:S(2)}, u32[]{:S(2)}) async-start(bf16[16,40,128]{2,1,0:T(8,128)(2,1)} %bitcast.8), calls=%async_computation.2 | async-start | bytes 327680 | tf_op jit(solution)/shard_map/all_to_all | solution.py:449
  85.9 19.3 %all-to-all-start.4 = ((f32[16,40,128]{2,1,0:T(8,128)}), f32[16,40,128]{2,1,0:T(8,128)S(1)}, u32[]{:S(2)}, u32[]{:S(2)}) async-start(f32[16,40,128]{2,1,0:T(8,128)} %broadcast_in_dim.16), calls=%async_computation.4 | async-start | bytes 655360 | tf_op jit(solution)/shard_map/all_to_all | solution.py:453
  91.0 8.3 %collective-permute-start.2 = (f32[3,8,16,128]{3,2,1,0:T(8,128)}, f32[3,8,16,128]{3,2,1,0:T(8,128)S(1)}, u32[]{:S(2)}, u32[]{:S(2)}) collective-permute-start(f32[3,8,16,128]{3,2,1,0:T(8,128)} %get-tuple-element.42), channel_id=1, source_target_pairs={{0,1},{1,2},{2,3},{3,4},{4,5},{5,6},{6,7},{7,8},{8,9},{9,10},{10,1... | collective-permute-start | bytes 589832 | tf_op jit(solution)/shard_map/ppermute | solution.py:533
  94.5 7.2 %collective-permute-start.3 = (f32[3,8,16,128]{3,2,1,0:T(8,128)}, f32[3,8,16,128]{3,2,1,0:T(8,128)S(1)}, u32[]{:S(2)}, u32[]{:S(2)}) collective-permute-start(f32[3,8,16,128]{3,2,1,0:T(8,128)} %get-tuple-element.43), channel_id=1, source_target_pairs={{1,0},{2,1},{3,2},{4,3},{5,4},{6,5},{7,6},{8,7},{9,8},{10,9},{11,1... | collective-permute-start | bytes 589832 | tf_op jit(solution)/shard_map/ppermute | solution.py:532

commit v10 on v9

--- a/solution.py
+++ b/solution.py
@@ -125,29 +125,30 @@
 
     half = halves()
 
-    @pl.loop(0, 64, unroll=8)
-    def _(n):
-        q = n % 8
-        here = n + REACH * 8
-        vrel = half + (2 * q - 8)
-        xg = base[0] + n // 8
-        mid = taps[4 * PLANE + here]
-        left = taps[3 * PLANE - 8 + here]
-        right = taps[5 * PLANE + 8 + here]
-        branch = jnp.zeros((2, 8, LANES), F32)
-        for k in range(shears):
-            d = shear[k]
-            xs = xg - d * vrel
-            a, b = here - d * 8, here + d * 8
-            main = mid + (taps[PLANE + a] + taps[7 * PLANE + b])
-            minus = left + (taps[a - 8] + taps[6 * PLANE - 8 + b])
-            plus = right + (taps[2 * PLANE + 8 + a] + taps[8 * PLANE + 8 + b])
-            pre = main + jnp.where(xs >= 1, minus, 0.0) + jnp.where(xs <= LANES - 2, plus, 0.0)
-            pre_ref[k * 64 + n] = pre
-            keep = xs.astype(jnp.uint32) < LANES
-            branch = branch + jnp.where(keep, beta[k] * gate(pre)[0], 0.0)
-        own = f0[pl.ds(pl.multiple_of(here * 16, 16), 16), :].astype(F32)
-        hfeat[q, n // 8] = (own + branch.reshape(16, LANES)).astype(BF)
+    @pl.loop(0, 8)
+    def _(x):
+        for q in range(8):
+            n = x * 8 + q
+            here = n + REACH * 8
+            vrel = half + (2 * q - 8)
+            xg = base[0] + x
+            mid = taps[4 * PLANE + here]
+            left = taps[3 * PLANE - 8 + here]
+            right = taps[5 * PLANE + 8 + here]
+            branch = jnp.zeros((2, 8, LANES), F32)
+            for k in range(shears):
+                d = shear[k]
+                xs = xg - d * vrel
+                a, b = here - d * 8, here + d * 8
+                main = mid + (taps[PLANE + a] + taps[7 * PLANE + b])
+                minus = left + (taps[a - 8] + taps[6 * PLANE - 8 + b])
+                plus = right + (taps[2 * PLANE + 8 + a] + taps[8 * PLANE + 8 + b])
+                pre = main + jnp.where(xs >= 1, minus, 0.0) + jnp.where(xs <= LANES - 2, plus, 0.0)
+                pre_ref[k * 64 + n] = pre
+                keep = xs.astype(jnp.uint32) < LANES
+                branch = branch + jnp.where(keep, beta[k] * gate(pre)[0], 0.0)
+            own = f0[pl.ds(pl.multiple_of(here * 16, 16), 16), :].astype(F32)
+            hfeat[q, x] = (own + branch.reshape(16, LANES)).astype(BF)
 
 
 def h_backward(ready, shear, beta_ref, base, pre_ref, f0, fmi, fpl, gm, pay_v, pay, rim0, rim1, rim2, out0, out1, out2, beta, dps, sums, edges, blend, edges_sem):
@@ -157,27 +158,28 @@
     half = halves()
     blend[...] = jnp.zeros(blend.shape, F32)
 
-    @pl.loop(0, 64, unroll=8)
-    def _(n):
-        dps[pl.ds((n // 4) * PLANE + (n % 4) * 12, 12)] = jnp.zeros((12, 2, 8, LANES), F32)
-        sums[pl.ds((n // 16) * 96 + (n % 16) * 2, 2)] = jnp.zeros((2, 2, 8, LANES), F32)
-        x, q = n // 8, n % 8
-        g = gm[q, x].astype(F32).reshape(2, 8, LANES)
-        vrel = half + (2 * q - 8)
-        xg = base[0] + x
-        total = [jnp.zeros((2, 8, LANES), F32) for _ in range(3)]
-        for k in range(shears):
-            xs = xg - shear[k] * vrel
-            act, slope = gate(pre_ref[k * 64 + n])
-            gk = jnp.where(xs.astype(jnp.uint32) < LANES, g, 0.0)
-            dp = (beta[k] * gk * slope).astype(BF).astype(F32)
-            parts = (jnp.where(xs >= 1, dp, 0.0), dp, jnp.where(xs <= LANES - 2, dp, 0.0))
-            for j in range(3):
-                dps[(j * shears + k) * PLANE + 48 + n] = parts[j]
-                total[j] = total[j] + parts[j]
-            blend[k] += jnp.sum(gk * act, axis=0)
-        for j in range(3):
-            sums[j * 96 + 32 + n] = total[j]
+    @pl.loop(0, 8)
+    def _(x):
+        for q in range(8):
+            n = x * 8 + q
+            dps[pl.ds((x * 2 + q // 4) * PLANE + (q % 4) * 12, 12)] = jnp.zeros((12, 2, 8, LANES), F32)
+            sums[pl.ds((x // 2) * 96 + (x % 2) * 16 + q * 2, 2)] = jnp.zeros((2, 2, 8, LANES), F32)
+            g = gm[q, x].astype(F32).reshape(2, 8, LANES)
+            vrel = half + (2 * q - 8)
+            xg = base[0] + x
+            total = [jnp.zeros((2, 8, LANES), F32) for _ in range(3)]
+            for k in range(shears):
+                xs = xg - shear[k] * vrel
+                act, slope = gate(pre_ref[k * 64 + n])
+                gk = jnp.where(xs.astype(jnp.uint32) < LANES, g, 0.0)
+                dp = (beta[k] * gk * slope).astype(BF).astype(F32)
+                parts = (jnp.where(xs >= 1, dp, 0.0), dp, jnp.where(xs <= LANES - 2, dp, 0.0))
+                for j in range(3):
+                    dps[(j * shears + k) * PLANE + 48 + n] = parts[j]
+                    total[j] = total[j] + parts[j]
+                blend[k] += jnp.sum(gk * act, axis=0)
+            for j in range(3):
+                sums[j * 96 + 32 + n] = total[j]
 
     @pl.loop(0, WIDE * 8, unroll=8)
     def _(n):

time: 107 us -> 107 us (level)
  no operation moved by 1% of the time
where the time goes in v10:
time: 107 us; the launch traced here: 106 us
  blocking collectives  36 us (34%)
  Pallas kernels  31.1 us (29%)
  starting transfers between devices  25.2 us (24%)
  waiting for transfers between devices  10.9 us (10%)
  local copies, waits for them, and re-layouts  1.94 us (2%)
    pallas_call x5, Pallas kernels, call(): pl.pallas_call(kernel, out_shape=out_shapes, in_specs=specs, out_specs=[p...  30.2 us
    all_to_all x1, blocking collectives, whole_step(): moved = lax.all_to_all(hfeat, 'vrow', 0, 0, tiled=True)  15.2 us
    all_to_all x1, blocking collectives, whole_step(): grad = lax.all_to_all(dvert, 'vrow', 0, 0, tiled=True)  11.2 us
    all_to_all x1, blocking collectives, reduce_all(): part = lax.all_to_all(part, 'vrow', 0, 0, tiled=True)  9.58 us
    all_to_all x1, starting transfers between devices, reduce_all(): part = lax.all_to_all(pay.reshape(16, 40, LANES), 'img', 0, 0, tiled=True)  8.26 us
    all_to_all x1, starting transfers between devices, reduce_all(): return lax.all_to_all(part, 'img', 0, 0, tiled=True).reshape(640, LANES)  5.02 us
    ppermute x1, starting transfers between devices, whole_step(): halo_from_left = lax.ppermute(halo_right, 'img', to_right)  3.53 us
    all_to_all x1, waiting for transfers between devices, reduce_all(): part = lax.all_to_all(pay.reshape(16, 40, LANES), 'img', 0, 0, tiled=True)  3.38 us
  transfers between devices with their start and end apart: 6, of which 5 were waited for; matrix products, arithmetic and copies ran while one was open for 0% of the time, Pallas kernels for 6%

profile of v10, /device:TPU:1, one launch (start us, length us, event | category | flops | bytes accessed | tf_op | source)
XLA Modules:
  0.0 106.0 jit_solution(9530019805250702823)
XLA Ops:
  0.6 1.2 %fusion.3 = (bf16[16,4,1024]{2,1,0:T(4,128)(2,1)S(1)}, bf16[16,4,1024]{2,1,0:T(4,128)(2,1)S(1)}) fusion(bf16[16,8,1024]{2,1,0:T(8,128)(2,1)} %bitcast.27), kind=kLoop, calls=%fused_computation.25 | loop fusion | bytes 524288 | tf_op jit(solution)/shard_map/slice | solution.py:466
  1.8 3.3 %collective-permute-start.1 = (bf16[16,4,1024]{2,1,0:T(4,128)(2,1)S(1)}, bf16[16,4,1024]{2,1,0:T(4,128)(2,1)S(1)}, u32[]{:S(2)}, u32[]{:S(2)}) collective-permute-start(bf16[16,4,1024]{2,1,0:T(4,128)(2,1)S(1)} %get-tuple-element.50), channel_id=1, source_target_pairs={{1,0},{2,1},{3,2},{4,3},{5,4},{6,5},{7,6},{8,7},{9,8},{10,9},{11,1... | collective-permute-start | bytes 393224 | tf_op jit(solution)/shard_map/ppermute | solution.py:466
  5.1 3.2 %collective-permute-start = (bf16[16,4,1024]{2,1,0:T(4,128)(2,1)S(1)}, bf16[16,4,1024]{2,1,0:T(4,128)(2,1)S(1)}, u32[]{:S(2)}, u32[]{:S(2)}) collective-permute-start(bf16[16,4,1024]{2,1,0:T(4,128)(2,1)S(1)} %get-tuple-element.51), channel_id=1, source_target_pairs={{0,1},{1,2},{2,3},{3,4},{4,5},{5,6},{6,7},{7,8},{8,9},{9,10},{10,1... | collective-permute-start | bytes 393224 | tf_op jit(solution)/shard_map/ppermute | solution.py:465
  8.3 0.7 collective-permute-done.1.refs_6_
  9.0 1.6 %collective-permute-done.refs_5_ = bf16[16,4,1024]{2,1,0:T(4,128)(2,1)S(1)} collective-permute-done((bf16[16,4,1024]{2,1,0:T(4,128)(2,1)S(1)}, bf16[16,4,1024]{2,1,0:T(4,128)(2,1)S(1)}, u32[]{:S(2)}, u32[]{:S(2)}) %collective-permute-start) | collective-permute-done | bytes 131104 | tf_op jit(solution)/shard_map/ppermute | solution.py:465
  10.6 5.8 %shard_map.118 = (bf16[8,8,16,128]{3,2,1,0:T(8,128)(2,1)S(1)}, f32[320,2,8,128]{3,2,1,0:T(8,128)S(1)}, bf16[1792,128]{1,0:T(8,128)(2,1)S(1)}, bf16[1792,128]{1,0:T(8,128)(2,1)S(1)}, bf16[1792,128]{1,0:T(8,128)(2,1)S(1)}) custom-call(s32[5]{0:T(128)} %refs_0_.5, f32[5,64]{1,0:T(8,128)} %refs_1_.5, bf16[9,64,64]{2,1,0:T(8,128)(2,1)} %bitcast.24, ...), custom_call_target="tpu_custom_call" | custom-call | flops 528482304 | bytes 4000000 | tf_op jit(solution)/shard_map/pallas_call | solution.py:419
  16.4 15.2 %all_to_all.25.refs_4_ = bf16[8,8,16,128]{3,2,1,0:T(8,128)(2,1)S(1)} all-to-all(bf16[8,8,16,128]{3,2,1,0:T(8,128)(2,1)S(1)} %get-tuple-element.28), channel_id=1, replica_groups=mesh['vrow'=8,'img'=16] {'vrow'}, dimensions={0} | all-to-all | bytes 524288 | tf_op jit(solution)/shard_map/all_to_all | solution.py:485
  31.6 10.3 %shard_map.119 = (bf16[2,8,8192]{2,1,0:T(8,128)(2,1)}, bf16[8,8,16,128]{3,2,1,0:T(8,128)(2,1)S(1)}, bf16[320,128]{1,0:T(8,128)(2,1)S(1)}) custom-call(s32[5]{0:T(128)} %refs_0_.5, f32[5,64]{1,0:T(8,128)} %refs_1_.4, bf16[9,64,64]{2,1,0:T(8,128)(2,1)} %bitcast.32, bf16[2,8,8192]{2,1,0:T(8,128)(2,1)} %refs_3_.1, bf16[8,8,16,128]{3,2,1,0:T(8,128)(2,1)S(1)} %all_to_all.25.refs_4_), custom_call_target="tpu_custom_call" | custom-call | flops 905969664 | bytes 4000000 | tf_op jit(solution)/shard_map/pallas_call | solution.py:419
  42.0 11.2 %all_to_all.26.refs_7_.refs_4_ = bf16[8,8,16,128]{3,2,1,0:T(8,128)(2,1)S(1)} all-to-all(bf16[8,8,16,128]{3,2,1,0:T(8,128)(2,1)S(1)} %get-tuple-element.34), channel_id=1, replica_groups=mesh['vrow'=8,'img'=16] {'vrow'}, dimensions={0} | all-to-all | bytes 524288 | tf_op jit(solution)/shard_map/all_to_all | solution.py:507
  53.1 0.0 copy-start
  53.1 7.6 %shard_map.120 = (bf16[640,128]{1,0:T(8,128)(2,1)}, bf16[768,384]{1,0:T(8,128)(2,1)}, bf16[768,384]{1,0:T(8,128)(2,1)}, bf16[768,384]{1,0:T(8,128)(2,1)}, bf16[1...) custom-call(s32[5]{0:T(128)} %refs_0_.5, f32[5,64]{1,0:T(8,128)} %refs_1_.5, ...), custom_call_target="tpu_custom_call" | custom-call | flops 528482304 | bytes 4000000 | tf_op jit(solution)/shard_map/pallas_call | solution.py:419
  60.7 8.3 %all-to-all-start.2 = ((bf16[16,40,128]{2,1,0:T(8,128)(2,1)}), bf16[16,40,128]{2,1,0:T(8,128)(2,1)S(1)}, u32[]{:S(2)}, u32[]{:S(2)}) async-start(bf16[16,40,128]{2,1,0:T(8,128)(2,1)} %bitcast.8), calls=%async_computation.2 | async-start | bytes 327680 | tf_op jit(solution)/shard_map/all_to_all | solution.py:451
  69.0 3.0 %shard_map.121 = (f32[3,8,16,128]{3,2,1,0:T(8,128)}, f32[3,8,16,128]{3,2,1,0:T(8,128)}, f32[40,128]{1,0:T(8,128)S(1)}) custom-call(bf16[9,64,64]{2,1,0:T(8,128)(2,1)} %bitcast.25, bf16[768,384]{1,0:T(8,128)(2,1)} %get-tuple-element.39.refs_1_, bf16[768,384]{1,0:T(8,128)(2,1)} %get-tuple-element.40.refs_2_, bf16[768,384]{1,0:T(8,128)(2,1)} %get-tuple-element.41.refs_3_), custom_call_target="tpu_custom_call" | custom-call | flops 226492416 | bytes 4000000 | tf_op jit(solution)/shard_map/pallas_call | solution.py:419
  72.0 0.0 copy-done
  72.0 3.4 %all-to-all-done.2 = bf16[16,40,128]{2,1,0:T(8,128)(2,1)S(1)} async-done(((bf16[16,40,128]{2,1,0:T(8,128)(2,1)}), bf16[16,40,128]{2,1,0:T(8,128)(2,1)S(1)}, u32[]{:S(2)}, u32[]{:S(2)}) %all-to-all-start.2) | async-done | bytes 163872 | tf_op jit(solution)/shard_map/all_to_all | solution.py:451
  75.5 9.6 %all_to_all.27 = f32[8,40,128]{2,1,0:T(8,128)S(1)} all-to-all(f32[8,40,128]{2,1,0:T(8,128)S(1)} %broadcast_in_dim.6), channel_id=1, replica_groups=mesh['vrow'=8,'img'=16] {'vrow'}, dimensions={0} | all-to-all | bytes 327680 | tf_op jit(solution)/shard_map/all_to_all | solution.py:453
  85.1 0.7 broadcast_in_dim.16
  85.8 5.0 %all-to-all-start.4 = ((f32[16,40,128]{2,1,0:T(8,128)}), f32[16,40,128]{2,1,0:T(8,128)S(1)}, u32[]{:S(2)}, u32[]{:S(2)}) async-start(f32[16,40,128]{2,1,0:T(8,128)} %broadcast_in_dim.16), calls=%async_computation.4 | async-start | bytes 655360 | tf_op jit(solution)/shard_map/all_to_all | solution.py:455
  90.9 3.5 %collective-permute-start.2 = (f32[3,8,16,128]{3,2,1,0:T(8,128)}, f32[3,8,16,128]{3,2,1,0:T(8,128)S(1)}, u32[]{:S(2)}, u32[]{:S(2)}) collective-permute-start(f32[3,8,16,128]{3,2,1,0:T(8,128)} %get-tuple-element.42), channel_id=1, source_target_pairs={{0,1},{1,2},{2,3},{3,4},{4,5},{5,6},{6,7},{7,8},{8,9},{9,10},{10,1... | collective-permute-start | bytes 589832 | tf_op jit(solution)/shard_map/ppermute | solution.py:535
  94.4 1.9 %collective-permute-start.3 = (f32[3,8,16,128]{3,2,1,0:T(8,128)}, f32[3,8,16,128]{3,2,1,0:T(8,128)S(1)}, u32[]{:S(2)}, u32[]{:S(2)}) collective-permute-start(f32[3,8,16,128]{3,2,1,0:T(8,128)} %get-tuple-element.43), channel_id=1, source_target_pairs={{1,0},{2,1},{3,2},{4,3},{5,4},{6,5},{7,6},{8,7},{9,8},{10,9},{11,1... | collective-permute-start | bytes 589832 | tf_op jit(solution)/shard_map/ppermute | solution.py:534
  96.3 2.8 %collective-permute-done.2.refs_5_ = f32[3,8,16,128]{3,2,1,0:T(8,128)S(1)} collective-permute-done((f32[3,8,16,128]{3,2,1,0:T(8,128)}, f32[3,8,16,128]{3,2,1,0:T(8,128)S(1)}, u32[]{:S(2)}, u32[]{:S(2)}) %collective-permute-start.2) | collective-permute-done | bytes 196640 | tf_op jit(solution)/shard_map/ppermute | solution.py:535
  99.2 2.5 %collective-permute-done.3.refs_6_ = f32[3,8,16,128]{3,2,1,0:T(8,128)S(1)} collective-permute-done((f32[3,8,16,128]{3,2,1,0:T(8,128)}, f32[3,8,16,128]{3,2,1,0:T(8,128)S(1)}, u32[]{:S(2)}, u32[]{:S(2)}) %collective-permute-start.3) | collective-permute-done | bytes 196640 | tf_op jit(solution)/shard_map/ppermute | solution.py:534
  101.6 3.5 %shard_map.122 = bf16[16,8,1024]{2,1,0:T(8,128)(2,1)} custom-call(bf16[9,64,64]{2,1,0:T(8,128)(2,1)} %bitcast.26, bf16[1024,384]{1,0:T(8,128)(2,1)} %get-tuple-element.36.refs_1_, bf16[1024,384]{1,0:T(8,128)(2,1)} %get-tuple-element.37.refs_2_, bf16[1024,384]{1,0:T(8,128)(2,1)} %get-tuple-element.38.refs_3_, bf16[8,8,16,128]{3,2,1,0:T(8,128)(2,1)} %copy-done, ...), custom_call_target="tpu_custom_call" | custom-call | flops 301989888 | bytes 4000000 | tf_op jit(solution)/shard_map/pallas_call | solution.py:419
  105.1 0.0 all-to-all-done.4
  105.1 0.9 shard_map.123
  (4 shorter events, 0.1 us)
Async XLA Ops:
  1.8 7.2 %collective-permute-start.1 = (bf16[16,4,1024]{2,1,0:T(4,128)(2,1)S(1)}, bf16[16,4,1024]{2,1,0:T(4,128)(2,1)S(1)}, u32[]{:S(2)}, u32[]{:S(2)}) collective-permute-start(bf16[16,4,1024]{2,1,0:T(4,128)(2,1)S(1)} %get-tuple-element.50), channel_id=1, source_target_pairs={{1,0},{2,1},{3,2},{4,3},{5,4},{6,5},{7,6},{8,7},{9,8},{10,9},{11,1... | collective-permute-start | bytes 393224 | tf_op jit(solution)/shard_map/ppermute | solution.py:466
  5.1 5.5 %collective-permute-start = (bf16[16,4,1024]{2,1,0:T(4,128)(2,1)S(1)}, bf16[16,4,1024]{2,1,0:T(4,128)(2,1)S(1)}, u32[]{:S(2)}, u32[]{:S(2)}) collective-permute-start(bf16[16,4,1024]{2,1,0:T(4,128)(2,1)S(1)} %get-tuple-element.51), channel_id=1, source_target_pairs={{0,1},{1,2},{2,3},{3,4},{4,5},{5,6},{6,7},{7,8},{8,9},{9,10},{10,1... | collective-permute-start | bytes 393224 | tf_op jit(solution)/shard_map/ppermute | solution.py:465
  53.1 18.9 %copy-start = (bf16[8,8,16,128]{3,2,1,0:T(8,128)(2,1)}, bf16[8,8,16,128]{3,2,1,0:T(8,128)(2,1)S(1)}, u32[]{:S(2)}) copy-start(bf16[8,8,16,128]{3,2,1,0:T(8,128)(2,1)S(1)} %all_to_all.26.refs_7_.refs_4_) | copy-start | bytes 786436
  60.7 14.7 %all-to-all-start.2 = ((bf16[16,40,128]{2,1,0:T(8,128)(2,1)}), bf16[16,40,128]{2,1,0:T(8,128)(2,1)S(1)}, u32[]{:S(2)}, u32[]{:S(2)}) async-start(bf16[16,40,128]{2,1,0:T(8,128)(2,1)} %bitcast.8), calls=%async_computation.2 | async-start | bytes 327680 | tf_op jit(solution)/shard_map/all_to_all | solution.py:451
  85.8 19.3 %all-to-all-start.4 = ((f32[16,40,128]{2,1,0:T(8,128)}), f32[16,40,128]{2,1,0:T(8,128)S(1)}, u32[]{:S(2)}, u32[]{:S(2)}) async-start(f32[16,40,128]{2,1,0:T(8,128)} %broadcast_in_dim.16), calls=%async_computation.4 | async-start | bytes 655360 | tf_op jit(solution)/shard_map/all_to_all | solution.py:455
  90.9 8.3 %collective-permute-start.2 = (f32[3,8,16,128]{3,2,1,0:T(8,128)}, f32[3,8,16,128]{3,2,1,0:T(8,128)S(1)}, u32[]{:S(2)}, u32[]{:S(2)}) collective-permute-start(f32[3,8,16,128]{3,2,1,0:T(8,128)} %get-tuple-element.42), channel_id=1, source_target_pairs={{0,1},{1,2},{2,3},{3,4},{4,5},{5,6},{6,7},{7,8},{8,9},{9,10},{10,1... | collective-permute-start | bytes 589832 | tf_op jit(solution)/shard_map/ppermute | solution.py:535
  94.4 7.2 %collective-permute-start.3 = (f32[3,8,16,128]{3,2,1,0:T(8,128)}, f32[3,8,16,128]{3,2,1,0:T(8,128)S(1)}, u32[]{:S(2)}, u32[]{:S(2)}) collective-permute-start(f32[3,8,16,128]{3,2,1,0:T(8,128)} %get-tuple-element.43), channel_id=1, source_target_pairs={{1,0},{2,1},{3,2},{4,3},{5,4},{6,5},{7,6},{8,7},{9,8},{10,9},{11,1... | collective-permute-start | bytes 589832 | tf_op jit(solution)/shard_map/ppermute | solution.py:534
